TPU v7x, 32 devices: a whole 2x2x4 slice. The times are simulated.
32 devices in a mesh: grp: 4 (over y, x), row: 8 (over z, core).
Axes of the slice: x: 2, y: 2, z: 4, core: 2. Of those that a mesh axis runs over, the one named last changes fastest.
Arguments:
- matrix_tiles: float32 [128, 32, 128, 128], P(('grp', 'row')), may hold values from -2 to 2, as said below
- column_index: int32 [128, 32], P(('grp', 'row')), may hold values from 0 to 127, as said below
- precond: float32 [128, 128, 128], P(('grp', 'row')), may hold values from -12 to 16, as said below
- right_side: float32 [128, 16, 128], P(('grp', 'row')), may hold values from -60 to 60
- lost_group: int32 [1], replicated, may hold values from 0 to 16383
Outputs:
- recovered: float32 [128, 16, 128], P(('grp', 'row'))
- true_residual: float32 [128, 16, 128], P(('grp', 'row'))
Inputs may be any that keep to these rules, and one draw needn't show every extreme that they name: `column_index`: entry 0 of block row i is i; entry 1 is i + 12, or i - 12 where i + 12 passes the end; every entry lies within 12 of its block row. `precond`: every block is symmetric positive definite. `matrix_tiles`: the diagonal tile of each block row is near the identity.
All inputs are finite; a program needn't handle non-finite values.
Results may differ from a plain program's by a relative error of at most 0.0003.
Values sent between devices are 32-bit elements; how exact they have to be, the bound alone decides.
No kernel may reach another device: no remote copies, remote signals or barrier semaphores. Data moves between devices by JAX's collectives and lax.ppermute only.
A program may use at most 64 MiB of HBM per device.

v0:
```python
import jax
import jax.numpy as jnp
from jax import lax
from jax.sharding import PartitionSpec as P

REACH = 3
OUTER = 2
INNER = 2
BAND = 12


def from_behind(value, axis, steps):
    count = lax.axis_size(axis)
    first, last = (max(0, -steps), min(count, count - steps))
    return lax.ppermute(value, axis, [(source, source + steps) for source in range(first, last)])


def inner_products(former, latter):
    return jnp.einsum("ica,ida->cd", former, latter, precision=lax.Precision.HIGHEST)


def scaled_by(vector, coeffs):
    return jnp.einsum("ica,cd->ida", vector, coeffs, precision=lax.Precision.HIGHEST)


def small_product(former, latter):
    return jnp.dot(former, latter, precision=lax.Precision.HIGHEST)


def solve_sym(matrix, target):
    factor = jnp.linalg.cholesky(0.5 * (matrix + matrix.T))
    middle = lax.linalg.triangular_solve(factor, target, left_side=True, lower=True)
    return lax.linalg.triangular_solve(factor, middle, left_side=True, lower=True, transpose_a=True)


def neighbour(vector, offset):
    return from_behind(vector, ("grp", "row"), offset)


def group_neighbour(vector, offset):
    return from_behind(vector, "row", offset)


def window_of(vector, shifter):
    pieces = [shifter(vector, offset) for offset in range(REACH, 0, -1)]
    pieces.append(vector)
    for offset in range(1, REACH + 1):
        pieces.append(shifter(vector, -offset))
    return jnp.concatenate(pieces, 0)


def tile_product(matrix_tiles, window, local_cols, kept_mask):
    picked = jnp.take(window, local_cols, axis=0)
    if kept_mask is not None:
        picked = picked * kept_mask[:, :, None, None]
    return jnp.einsum("ikab,ikcb->ica", matrix_tiles, picked, precision=lax.Precision.HIGHEST)


def per_device(matrix_tiles, column_index, precond, right_side, lost_group):
    blocks = right_side.shape[0]
    row_count = lax.axis_size("row")
    group_count = lax.axis_size("grp")
    group_blocks = blocks * row_count
    my_group = lax.axis_index("grp")
    my_start = lax.axis_index(("grp", "row")) * blocks
    local_cols = column_index - (my_start - BAND)
    other_mask = (column_index // group_blocks != my_group).astype(jnp.float32)
    own_mask = 1.0 - other_mask
    lost = lost_group[0] % group_count

    def full_product(vector):
        return tile_product(matrix_tiles, window_of(vector, neighbour), local_cols, None)

    solution = jnp.zeros_like(right_side)
    residual = right_side
    direction = right_side
    squares = lax.psum(inner_products(residual, residual), ("grp", "row"))
    for outer_step in range(OUTER):
        applied = full_product(direction)
        curvature, crossed, square = lax.psum(
            (
                inner_products(direction, applied),
                inner_products(applied, residual),
                inner_products(applied, applied),
            ),
            ("grp", "row"),
        )
        advance = solve_sym(curvature, squares)
        solution = solution + scaled_by(direction, advance)
        residual = residual - scaled_by(applied, advance)
        squares_next = (
            squares
            - small_product(crossed.T, advance)
            - small_product(advance.T, crossed)
            + small_product(advance.T, small_product(square, advance))
        )
        mixing = solve_sym(squares, squares_next)
        direction = residual + scaled_by(direction, mixing)
        squares = squares_next
    coupled = tile_product(matrix_tiles, window_of(solution, neighbour), local_cols, other_mask)
    inner_target = right_side - coupled

    def condition(vector):
        return jnp.einsum("iab,icb->ica", precond, vector, precision=lax.Precision.HIGHEST)

    estimate = jnp.zeros_like(inner_target)
    remainder = inner_target
    smoothed = condition(remainder)
    heading = smoothed
    weight = lax.psum(inner_products(remainder, smoothed), "row")
    for inner_step in range(INNER):
        applied = tile_product(
            matrix_tiles, window_of(heading, group_neighbour), local_cols, own_mask
        )
        bending = lax.psum(inner_products(heading, applied), "row")
        advance = solve_sym(bending, weight)
        estimate = estimate + scaled_by(heading, advance)
        remainder = remainder - scaled_by(applied, advance)
        if inner_step + 1 < INNER:
            smoothed = condition(remainder)
            weight_next = lax.psum(inner_products(remainder, smoothed), "row")
            heading = smoothed + scaled_by(heading, solve_sym(weight, weight_next))
            weight = weight_next
    recovered = jnp.where(my_group == lost, estimate, solution)
    true_residual = right_side - full_product(recovered)
    return (recovered, true_residual)


def solution(mesh):
    in_specs = (
        P(("grp", "row"), None, None, None),
        P(("grp", "row"), None),
        P(("grp", "row"), None, None),
        P(("grp", "row"), None, None),
        P(),
    )
    out_specs = (P(("grp", "row"), None, None), P(("grp", "row"), None, None))
    return jax.shard_map(
        per_device, mesh=mesh, in_specs=in_specs, out_specs=out_specs, check_vma=False
    )
```

profile of v0, /device:TPU:5, one launch (start us, length us, event | category | flops | bytes accessed | tf_op | source)
XLA Modules:
  0.0 370.1 jit_solution(12967061510973747642)
XLA Ops:
  0.6 6.8 %collective-permute-start.5 = (f32[4,16,128]{2,1,0:T(8,128)}, f32[4,16,128]{2,1,0:T(8,128)S(1)}, u32[]{:S(2)}, u32[]{:S(2)}) collective-permute-start(f32[4,16,128]{2,1,0:T(8,128)} %param.15), channel_id=1, source_target_pairs={{3,0},{4,1},{5,2},{6,3},{7,4},{8,5},{9,6},{10,7},{11,8},{12,9},{13... | collective-permute-start | bytes 98312 | tf_op jit(solution)/shard_map/ppermute | solution.py:15
  7.4 2.1 collective-permute-start.4
  9.5 2.1 collective-permute-start.3
  11.7 3.4 collective-permute-start.2
  15.1 2.9 collective-permute-start
  19.8 4.3 %collective-permute-done = f32[4,16,128]{2,1,0:T(8,128)S(1)} collective-permute-done((f32[4,16,128]{2,1,0:T(8,128)}, f32[4,16,128]{2,1,0:T(8,128)S(1)}, u32[]{:S(2)}, u32[]{:S(2)}) %collective-permute-start) | collective-permute-done | bytes 32800 | tf_op jit(solution)/shard_map/ppermute | solution.py:15
  24.2 1.9 collective-permute-start.1
  26.1 6.5 %collective-permute-done.1 = f32[4,16,128]{2,1,0:T(8,128)S(1)} collective-permute-done((f32[4,16,128]{2,1,0:T(8,128)}, f32[4,16,128]{2,1,0:T(8,128)S(1)}, u32[]{:S(2)}, u32[]{:S(2)}) %collective-permute-start.1) | collective-permute-done | bytes 32800 | tf_op jit(solution)/shard_map/ppermute | solution.py:15
  34.2 9.4 %convolution_bitcast_fusion.9 = f32[4,16,128]{2,1,0:T(8,128)S(1)} fusion(f32[4,32,128,128]{3,2,1,0:T(8,128)} %param.12, f32[4,32,16,128]{3,2,1,0:T(8,128)S(1)} %bitcast.254, pred[4,32]{1,0:T(4,128)(4,1)S(1)} %get-tuple-element.14), kind=kOutput, calls=%fused_computation.26 | convolution fusion | flops 402915328 | bytes 9470080 | tf_op jit(solution)/shard_map/ikab,ikcb->ica/dot_general | solution.py:56
  44.0 36.1 %all-reduce = (f32[16,16]{1,0:T(8,128)S(1)}, f32[16,16]{1,0:T(8,128)S(1)}, f32[16,16]{1,0:T(8,128)S(1)}, f32[16,16]{1,0:T(8,128)S(1)}) all-reduce(f32[16,16]{1,0:T(8,128)S(1)} %convolution_bitcast_fusion.21, f32[16,16]{1,0:T(8,128)S(1)} %bitcast.256, ...), channel_id=1, replica_groups=mesh['grp'=4,'row'=8] {'grp','row'}, use_global_device_ids=true, to_apply=%region_3.6 | all-reduce | flops 1024 | bytes 8192 | tf_op jit(solution)/shard_map/psum | solution.py:77
  80.3 1.5 cholesky.115
  83.1 1.2 custom-call.21
  84.4 1.5 cholesky.104
  87.2 1.2 custom-call.19
  90.4 6.3 %collective-permute-start.6 = (f32[4,16,128]{2,1,0:T(8,128)S(1)}, f32[4,16,128]{2,1,0:T(8,128)S(1)}, u32[]{:S(2)}, u32[]{:S(2)}) collective-permute-start(f32[4,16,128]{2,1,0:T(8,128)S(1)} %fusion.7), channel_id=1, source_target_pairs={{0,3},{1,4},{2,5},{3,6},{4,7},{5,8},{6,9},{7,10},{8,11},{9,12},{10... | collective-permute-start | bytes 98312 | tf_op jit(solution)/shard_map/ppermute | solution.py:15
  96.9 2.8 collective-permute-start.11
  99.8 4.8 %collective-permute-start.10 = (f32[4,16,128]{2,1,0:T(8,128)S(1)}, f32[4,16,128]{2,1,0:T(8,128)S(1)}, u32[]{:S(2)}, u32[]{:S(2)}) collective-permute-start(f32[4,16,128]{2,1,0:T(8,128)S(1)} %fusion.7), channel_id=1, source_target_pairs={{2,0},{3,1},{4,2},{5,3},{6,4},{7,5},{8,6},{9,7},{10,8},{11,9},{12,... | collective-permute-start | bytes 98312 | tf_op jit(solution)/shard_map/ppermute | solution.py:15
  104.6 1.9 collective-permute-start.9
  106.5 3.6 collective-permute-start.8
  110.2 2.5 collective-permute-start.7
  112.7 5.8 %collective-permute-done.7 = f32[4,16,128]{2,1,0:T(8,128)S(1)} collective-permute-done((f32[4,16,128]{2,1,0:T(8,128)S(1)}, f32[4,16,128]{2,1,0:T(8,128)S(1)}, u32[]{:S(2)}, u32[]{:S(2)}) %collective-permute-start.7) | collective-permute-done | bytes 32800 | tf_op jit(solution)/shard_map/ppermute | solution.py:15
  119.3 9.4 %convolution_bitcast_fusion.6 = f32[4,16,128]{2,1,0:T(8,128)S(1)} fusion(f32[4,32,128,128]{3,2,1,0:T(8,128)} %param.12, f32[4,32,16,128]{3,2,1,0:T(8,128)S(1)} %bitcast.255, pred[4,32]{1,0:T(4,128)(4,1)S(1)} %get-tuple-element.14), kind=kOutput, calls=%fused_computation.21 | convolution fusion | flops 402915328 | bytes 9470080 | tf_op jit(solution)/shard_map/ikab,ikcb->ica/dot_general | solution.py:56
  128.8 36.1 %psum.67 = f32[16,16]{1,0:T(8,128)S(1)} all-reduce(f32[16,16]{1,0:T(8,128)S(1)} %convolution_bitcast_fusion.18), channel_id=1, replica_groups=mesh['grp'=4,'row'=8] {'grp','row'}, use_global_device_ids=true, to_apply=%region_6.11 | all-reduce | flops 256 | bytes 2048 | tf_op jit(solution)/shard_map/psum | solution.py:80
  165.1 1.5 cholesky.126
  167.9 1.2 custom-call.23
  169.7 6.0 %collective-permute-start.12 = (f32[4,16,128]{2,1,0:T(8,128)S(1)}, f32[4,16,128]{2,1,0:T(8,128)S(1)}, u32[]{:S(2)}, u32[]{:S(2)}) collective-permute-start(f32[4,16,128]{2,1,0:T(8,128)S(1)} %fusion.6), channel_id=1, source_target_pairs={{0,3},{1,4},{2,5},{3,6},{4,7},{5,8},{6,9},{7,10},{8,11},{9,12},{10... | collective-permute-start | bytes 98312 | tf_op jit(solution)/shard_map/ppermute | solution.py:15
  176.4 3.2 collective-permute-start.17
  179.6 4.4 %collective-permute-start.16 = (f32[4,16,128]{2,1,0:T(8,128)S(1)}, f32[4,16,128]{2,1,0:T(8,128)S(1)}, u32[]{:S(2)}, u32[]{:S(2)}) collective-permute-start(f32[4,16,128]{2,1,0:T(8,128)S(1)} %fusion.6), channel_id=1, source_target_pairs={{2,0},{3,1},{4,2},{5,3},{6,4},{7,5},{8,6},{9,7},{10,8},{11,9},{12,... | collective-permute-start | bytes 98312 | tf_op jit(solution)/shard_map/ppermute | solution.py:15
  184.0 1.9 collective-permute-start.15
  186.0 3.6 collective-permute-start.14
  189.6 2.7 collective-permute-start.13
  192.3 5.6 %collective-permute-done.13 = f32[4,16,128]{2,1,0:T(8,128)S(1)} collective-permute-done((f32[4,16,128]{2,1,0:T(8,128)S(1)}, f32[4,16,128]{2,1,0:T(8,128)S(1)}, u32[]{:S(2)}, u32[]{:S(2)}) %collective-permute-start.13) | collective-permute-done | bytes 32800 | tf_op jit(solution)/shard_map/ppermute | solution.py:15
  198.8 9.4 %fusion.5 = f32[4,16,128]{2,1,0:T(8,128)S(1)} fusion(f32[4,16,128]{2,1,0:T(8,128)S(1)} %copy-done.1, f32[4,32,128,128]{3,2,1,0:T(8,128)} %param.12, f32[4,32,16,128]{3,2,1,0:T(8,128)S(1)} %bitcast.250, f32[4,32]{1,0:T(4,128)S(1)} %get-tuple-element.13, pred[4,32]{1,0:T(4,128)(4,1)S(1)} %get-tuple-element.14), kind=kOutput, calls=%fused_computation.18 | convolution fusion | flops 403185664 | bytes 9503360 | tf_op jit(solution)/shard_map/ikab,ikcb->ica/dot_general | solution.py:56
  208.7 1.3 collective-permute-start.18
  210.2 1.3 collective-permute-start.23
  211.5 1.3 collective-permute-start.22
  212.8 1.9 collective-permute-start.21
  214.7 4.1 %collective-permute-start.20 = (f32[4,16,128]{2,1,0:T(8,128)S(1)}, f32[4,16,128]{2,1,0:T(8,128)S(1)}, u32[]{:S(2)}, u32[]{:S(2)}) collective-permute-start(f32[4,16,128]{2,1,0:T(8,128)S(1)} %fusion.85), channel_id=1, source_target_pairs={{0,1},{1,2},{2,3},{3,4},{4,5},{5,6},{6,7},{8,9},{9,10},{10,11},{11... | collective-permute-start | bytes 98312 | tf_op jit(solution)/shard_map/ppermute | solution.py:15
  218.8 4.0 %collective-permute-start.19 = (f32[4,16,128]{2,1,0:T(8,128)S(1)}, f32[4,16,128]{2,1,0:T(8,128)S(1)}, u32[]{:S(2)}, u32[]{:S(2)}) collective-permute-start(f32[4,16,128]{2,1,0:T(8,128)S(1)} %fusion.85), channel_id=1, source_target_pairs={{0,2},{1,3},{2,4},{3,5},{4,6},{5,7},{8,10},{9,11},{10,12},{11,13},... | collective-permute-start | bytes 98312 | tf_op jit(solution)/shard_map/ppermute | solution.py:15
  224.7 9.4 %convolution_bitcast_fusion.4 = f32[4,16,128]{2,1,0:T(8,128)S(1)} fusion(f32[4,32,128,128]{3,2,1,0:T(8,128)} %param.12, f32[4,32,16,128]{3,2,1,0:T(8,128)S(1)} %bitcast.251, f32[4,32]{1,0:T(4,128)S(1)} %get-tuple-element.12, pred[4,32]{1,0:T(4,128)(4,1)S(1)} %get-tuple-element.14), kind=kOutput, calls=%fused_computation.16 | convolution fusion | flops 403177472 | bytes 9470592 | tf_op jit(solution)/shard_map/ikab,ikcb->ica/dot_general | solution.py:56
  234.2 24.9 %all-reduce.1 = (f32[16,16]{1,0:T(8,128)S(1)}, f32[16,16]{1,0:T(8,128)S(1)}) all-reduce(f32[16,16]{1,0:T(8,128)S(1)} %convolution_bitcast_fusion.15, f32[16,16]{1,0:T(8,128)S(1)} %convolution_bitcast_fusion.16), channel_id=1, replica_groups=mesh['grp'=4,'row'=8] {'row'}, use_global_device_ids=true, to_apply=%region_8.13 | all-reduce | flops 512 | bytes 4096 | tf_op jit(solution)/shard_map/psum | solution.py:110
  259.3 1.5 cholesky.137
  262.1 1.2 custom-call.25
  264.1 1.5 cholesky.148
  266.9 1.2 custom-call.27
  268.8 17.3 %psum.70 = f32[16,16]{1,0:T(8,128)S(1)} all-reduce(f32[16,16]{1,0:T(8,128)S(1)} %convolution_bitcast_fusion.13), channel_id=1, replica_groups=mesh['grp'=4,'row'=8] {'row'}, use_global_device_ids=true, to_apply=%region_9.14 | all-reduce | flops 256 | bytes 2048 | tf_op jit(solution)/shard_map/psum | solution.py:121
  286.6 1.3 collective-permute-start.24
  288.1 1.3 collective-permute-start.29
  289.4 1.3 collective-permute-start.28
  290.7 2.7 collective-permute-start.27
  293.4 4.2 %collective-permute-start.26 = (f32[4,16,128]{2,1,0:T(8,128)S(1)}, f32[4,16,128]{2,1,0:T(8,128)S(1)}, u32[]{:S(2)}, u32[]{:S(2)}) collective-permute-start(f32[4,16,128]{2,1,0:T(8,128)S(1)} %fusion.3), channel_id=1, source_target_pairs={{0,1},{1,2},{2,3},{3,4},{4,5},{5,6},{6,7},{8,9},{9,10},{10,11},{11... | collective-permute-start | bytes 98312 | tf_op jit(solution)/shard_map/ppermute | solution.py:15
  297.5 4.2 %collective-permute-start.25 = (f32[4,16,128]{2,1,0:T(8,128)S(1)}, f32[4,16,128]{2,1,0:T(8,128)S(1)}, u32[]{:S(2)}, u32[]{:S(2)}) collective-permute-start(f32[4,16,128]{2,1,0:T(8,128)S(1)} %fusion.3), channel_id=1, source_target_pairs={{0,2},{1,3},{2,4},{3,5},{4,6},{5,7},{8,10},{9,11},{10,12},{11,13},... | collective-permute-start | bytes 98312 | tf_op jit(solution)/shard_map/ppermute | solution.py:15
  303.4 9.4 %convolution_bitcast_fusion.1 = f32[4,16,128]{2,1,0:T(8,128)S(1)} fusion(f32[4,32,128,128]{3,2,1,0:T(8,128)} %param.12, f32[4,32,16,128]{3,2,1,0:T(8,128)S(1)} %bitcast.252, f32[4,32]{1,0:T(4,128)S(1)} %get-tuple-element.12, pred[4,32]{1,0:T(4,128)(4,1)S(1)} %get-tuple-element.14), kind=kOutput, calls=%fused_computation.11 | convolution fusion | flops 403177472 | bytes 9470592 | tf_op jit(solution)/shard_map/ikab,ikcb->ica/dot_general | solution.py:56
  313.0 13.9 %psum.71 = f32[16,16]{1,0:T(8,128)S(1)} all-reduce(f32[16,16]{1,0:T(8,128)S(1)} %convolution_bitcast_fusion.11), channel_id=1, replica_groups=mesh['grp'=4,'row'=8] {'row'}, use_global_device_ids=true, to_apply=%region_10.15 | all-reduce | flops 256 | bytes 2048 | tf_op jit(solution)/shard_map/psum | solution.py:115
  327.1 1.5 cholesky.159
  329.9 1.2 custom-call.29
  331.7 1.9 collective-permute-start.30
  333.6 7.2 %collective-permute-start.35 = (f32[4,16,128]{2,1,0:T(8,128)S(1)}, f32[4,16,128]{2,1,0:T(8,128)S(1)}, u32[]{:S(2)}, u32[]{:S(2)}) collective-permute-start(f32[4,16,128]{2,1,0:T(8,128)S(1)} %fusion.2), channel_id=1, source_target_pairs={{3,0},{4,1},{5,2},{6,3},{7,4},{8,5},{9,6},{10,7},{11,8},{12,9},{13... | collective-permute-start | bytes 98312 | tf_op jit(solution)/shard_map/ppermute | solution.py:15
  340.9 1.9 collective-permute-start.34
  342.8 4.0 %collective-permute-start.33 = (f32[4,16,128]{2,1,0:T(8,128)S(1)}, f32[4,16,128]{2,1,0:T(8,128)S(1)}, u32[]{:S(2)}, u32[]{:S(2)}) collective-permute-start(f32[4,16,128]{2,1,0:T(8,128)S(1)} %fusion.2), channel_id=1, source_target_pairs={{1,0},{2,1},{3,2},{4,3},{5,4},{6,5},{7,6},{8,7},{9,8},{10,9},{11,1... | collective-permute-start | bytes 98312 | tf_op jit(solution)/shard_map/ppermute | solution.py:15
  346.8 3.5 collective-permute-start.32
  350.3 2.0 collective-permute-start.31
  352.4 6.8 %collective-permute-done.31 = f32[4,16,128]{2,1,0:T(8,128)S(1)} collective-permute-done((f32[4,16,128]{2,1,0:T(8,128)S(1)}, f32[4,16,128]{2,1,0:T(8,128)S(1)}, u32[]{:S(2)}, u32[]{:S(2)}) %collective-permute-start.31) | collective-permute-done | bytes 32800 | tf_op jit(solution)/shard_map/ppermute | solution.py:15
  360.1 10.0 %fusion = f32[4,16,128]{2,1,0:T(8,128)} fusion(f32[4,16,128]{2,1,0:T(8,128)S(1)} %copy-done.1, f32[4,32,128,128]{3,2,1,0:T(8,128)} %param.12, f32[4,32,16,128]{3,2,1,0:T(8,128)S(1)} %bitcast.253, pred[4,32]{1,0:T(4,128)(4,1)S(1)} %get-tuple-element.14), kind=kOutput, calls=%fused_computation.7 | convolution fusion | flops 402923520 | bytes 9502848 | tf_op jit(solution)/shard_map/ikab,ikcb->ica/dot_general | solution.py:56
  (167 shorter events, 24.8 us)
Async XLA Ops:
  0.6 207.6 %copy-start = (f32[4,128,128]{2,1,0:T(8,128)S(1)}, f32[4,128,128]{2,1,0:T(8,128)}, u32[]{:S(2)}) copy-start(f32[4,128,128]{2,1,0:T(8,128)} %param.14) | copy-start | bytes 786436
  0.6 32.8 %collective-permute-start.5 = (f32[4,16,128]{2,1,0:T(8,128)}, f32[4,16,128]{2,1,0:T(8,128)S(1)}, u32[]{:S(2)}, u32[]{:S(2)}) collective-permute-start(f32[4,16,128]{2,1,0:T(8,128)} %param.15), channel_id=1, source_target_pairs={{3,0},{4,1},{5,2},{6,3},{7,4},{8,5},{9,6},{10,7},{11,8},{12,9},{13... | collective-permute-start | bytes 98312 | tf_op jit(solution)/shard_map/ppermute | solution.py:15
  7.4 26.0 %collective-permute-start.4 = (f32[4,16,128]{2,1,0:T(8,128)}, f32[4,16,128]{2,1,0:T(8,128)S(1)}, u32[]{:S(2)}, u32[]{:S(2)}) collective-permute-start(f32[4,16,128]{2,1,0:T(8,128)} %param.15), channel_id=1, source_target_pairs={{2,0},{3,1},{4,2},{5,3},{6,4},{7,5},{8,6},{9,7},{10,8},{11,9},{12,... | collective-permute-start | bytes 98312 | tf_op jit(solution)/shard_map/ppermute | solution.py:15
  9.5 23.9 %collective-permute-start.3 = (f32[4,16,128]{2,1,0:T(8,128)}, f32[4,16,128]{2,1,0:T(8,128)S(1)}, u32[]{:S(2)}, u32[]{:S(2)}) collective-permute-start(f32[4,16,128]{2,1,0:T(8,128)} %param.15), channel_id=1, source_target_pairs={{1,0},{2,1},{3,2},{4,3},{5,4},{6,5},{7,6},{8,7},{9,8},{10,9},{11,1... | collective-permute-start | bytes 98312 | tf_op jit(solution)/shard_map/ppermute | solution.py:15
  11.7 20.9 %collective-permute-start.2 = (f32[4,16,128]{2,1,0:T(8,128)}, f32[4,16,128]{2,1,0:T(8,128)S(1)}, u32[]{:S(2)}, u32[]{:S(2)}) collective-permute-start(f32[4,16,128]{2,1,0:T(8,128)} %param.15), channel_id=1, source_target_pairs={{0,1},{1,2},{2,3},{3,4},{4,5},{5,6},{6,7},{7,8},{8,9},{9,10},{10,1... | collective-permute-start | bytes 98312 | tf_op jit(solution)/shard_map/ppermute | solution.py:15
  15.1 9.0 %collective-permute-start = (f32[4,16,128]{2,1,0:T(8,128)}, f32[4,16,128]{2,1,0:T(8,128)S(1)}, u32[]{:S(2)}, u32[]{:S(2)}) collective-permute-start(f32[4,16,128]{2,1,0:T(8,128)} %param.15), channel_id=1, source_target_pairs={{0,3},{1,4},{2,5},{3,6},{4,7},{5,8},{6,9},{7,10},{8,11},{9,12},{10... | collective-permute-start | bytes 98312 | tf_op jit(solution)/shard_map/ppermute | solution.py:15
  19.0 24.6 %copy-start.1 = (f32[4,16,128]{2,1,0:T(8,128)S(1)}, f32[4,16,128]{2,1,0:T(8,128)}, u32[]{:S(2)}) copy-start(f32[4,16,128]{2,1,0:T(8,128)} %param.15) | copy-start | bytes 98308
  24.2 8.5 %collective-permute-start.1 = (f32[4,16,128]{2,1,0:T(8,128)}, f32[4,16,128]{2,1,0:T(8,128)S(1)}, u32[]{:S(2)}, u32[]{:S(2)}) collective-permute-start(f32[4,16,128]{2,1,0:T(8,128)} %param.15), channel_id=1, source_target_pairs={{0,2},{1,3},{2,4},{3,5},{4,6},{5,7},{6,8},{7,9},{8,10},{9,11},{10,... | collective-permute-start | bytes 98312 | tf_op jit(solution)/shard_map/ppermute | solution.py:15
  90.4 19.8 %collective-permute-start.6 = (f32[4,16,128]{2,1,0:T(8,128)S(1)}, f32[4,16,128]{2,1,0:T(8,128)S(1)}, u32[]{:S(2)}, u32[]{:S(2)}) collective-permute-start(f32[4,16,128]{2,1,0:T(8,128)S(1)} %fusion.7), channel_id=1, source_target_pairs={{0,3},{1,4},{2,5},{3,6},{4,7},{5,8},{6,9},{7,10},{8,11},{9,12},{10... | collective-permute-start | bytes 98312 | tf_op jit(solution)/shard_map/ppermute | solution.py:15
  96.9 21.6 %collective-permute-start.11 = (f32[4,16,128]{2,1,0:T(8,128)S(1)}, f32[4,16,128]{2,1,0:T(8,128)S(1)}, u32[]{:S(2)}, u32[]{:S(2)}) collective-permute-start(f32[4,16,128]{2,1,0:T(8,128)S(1)} %fusion.7), channel_id=1, source_target_pairs={{3,0},{4,1},{5,2},{6,3},{7,4},{8,5},{9,6},{10,7},{11,8},{12,9},{13... | collective-permute-start | bytes 98312 | tf_op jit(solution)/shard_map/ppermute | solution.py:15
  99.8 18.7 %collective-permute-start.10 = (f32[4,16,128]{2,1,0:T(8,128)S(1)}, f32[4,16,128]{2,1,0:T(8,128)S(1)}, u32[]{:S(2)}, u32[]{:S(2)}) collective-permute-start(f32[4,16,128]{2,1,0:T(8,128)S(1)} %fusion.7), channel_id=1, source_target_pairs={{2,0},{3,1},{4,2},{5,3},{6,4},{7,5},{8,6},{9,7},{10,8},{11,9},{12,... | collective-permute-start | bytes 98312 | tf_op jit(solution)/shard_map/ppermute | solution.py:15
  104.6 13.9 %collective-permute-start.9 = (f32[4,16,128]{2,1,0:T(8,128)S(1)}, f32[4,16,128]{2,1,0:T(8,128)S(1)}, u32[]{:S(2)}, u32[]{:S(2)}) collective-permute-start(f32[4,16,128]{2,1,0:T(8,128)S(1)} %fusion.7), channel_id=1, source_target_pairs={{1,0},{2,1},{3,2},{4,3},{5,4},{6,5},{7,6},{8,7},{9,8},{10,9},{11,1... | collective-permute-start | bytes 98312 | tf_op jit(solution)/shard_map/ppermute | solution.py:15
  106.5 11.9 %collective-permute-start.8 = (f32[4,16,128]{2,1,0:T(8,128)S(1)}, f32[4,16,128]{2,1,0:T(8,128)S(1)}, u32[]{:S(2)}, u32[]{:S(2)}) collective-permute-start(f32[4,16,128]{2,1,0:T(8,128)S(1)} %fusion.7), channel_id=1, source_target_pairs={{0,1},{1,2},{2,3},{3,4},{4,5},{5,6},{6,7},{7,8},{8,9},{9,10},{10,1... | collective-permute-start | bytes 98312 | tf_op jit(solution)/shard_map/ppermute | solution.py:15
  110.2 8.3 %collective-permute-start.7 = (f32[4,16,128]{2,1,0:T(8,128)S(1)}, f32[4,16,128]{2,1,0:T(8,128)S(1)}, u32[]{:S(2)}, u32[]{:S(2)}) collective-permute-start(f32[4,16,128]{2,1,0:T(8,128)S(1)} %fusion.7), channel_id=1, source_target_pairs={{0,2},{1,3},{2,4},{3,5},{4,6},{5,7},{6,8},{7,9},{8,10},{9,11},{10,... | collective-permute-start | bytes 98312 | tf_op jit(solution)/shard_map/ppermute | solution.py:15
  118.5 57.2 %copy-start.3 = (s32[4,32]{1,0:T(4,128)S(1)}, s32[4,32]{1,0:T(4,128)}, u32[]{:S(2)}) copy-start(s32[4,32]{1,0:T(4,128)} %param.13) | copy-start | bytes 1540
  169.7 19.9 %collective-permute-start.12 = (f32[4,16,128]{2,1,0:T(8,128)S(1)}, f32[4,16,128]{2,1,0:T(8,128)S(1)}, u32[]{:S(2)}, u32[]{:S(2)}) collective-permute-start(f32[4,16,128]{2,1,0:T(8,128)S(1)} %fusion.6), channel_id=1, source_target_pairs={{0,3},{1,4},{2,5},{3,6},{4,7},{5,8},{6,9},{7,10},{8,11},{9,12},{10... | collective-permute-start | bytes 98312 | tf_op jit(solution)/shard_map/ppermute | solution.py:15
  176.4 21.6 %collective-permute-start.17 = (f32[4,16,128]{2,1,0:T(8,128)S(1)}, f32[4,16,128]{2,1,0:T(8,128)S(1)}, u32[]{:S(2)}, u32[]{:S(2)}) collective-permute-start(f32[4,16,128]{2,1,0:T(8,128)S(1)} %fusion.6), channel_id=1, source_target_pairs={{3,0},{4,1},{5,2},{6,3},{7,4},{8,5},{9,6},{10,7},{11,8},{12,9},{13... | collective-permute-start | bytes 98312 | tf_op jit(solution)/shard_map/ppermute | solution.py:15
  179.6 18.4 %collective-permute-start.16 = (f32[4,16,128]{2,1,0:T(8,128)S(1)}, f32[4,16,128]{2,1,0:T(8,128)S(1)}, u32[]{:S(2)}, u32[]{:S(2)}) collective-permute-start(f32[4,16,128]{2,1,0:T(8,128)S(1)} %fusion.6), channel_id=1, source_target_pairs={{2,0},{3,1},{4,2},{5,3},{6,4},{7,5},{8,6},{9,7},{10,8},{11,9},{12,... | collective-permute-start | bytes 98312 | tf_op jit(solution)/shard_map/ppermute | solution.py:15
  184.0 13.9 %collective-permute-start.15 = (f32[4,16,128]{2,1,0:T(8,128)S(1)}, f32[4,16,128]{2,1,0:T(8,128)S(1)}, u32[]{:S(2)}, u32[]{:S(2)}) collective-permute-start(f32[4,16,128]{2,1,0:T(8,128)S(1)} %fusion.6), channel_id=1, source_target_pairs={{1,0},{2,1},{3,2},{4,3},{5,4},{6,5},{7,6},{8,7},{9,8},{10,9},{11,1... | collective-permute-start | bytes 98312 | tf_op jit(solution)/shard_map/ppermute | solution.py:15
  186.0 11.9 %collective-permute-start.14 = (f32[4,16,128]{2,1,0:T(8,128)S(1)}, f32[4,16,128]{2,1,0:T(8,128)S(1)}, u32[]{:S(2)}, u32[]{:S(2)}) collective-permute-start(f32[4,16,128]{2,1,0:T(8,128)S(1)} %fusion.6), channel_id=1, source_target_pairs={{0,1},{1,2},{2,3},{3,4},{4,5},{5,6},{6,7},{7,8},{8,9},{9,10},{10,1... | collective-permute-start | bytes 98312 | tf_op jit(solution)/shard_map/ppermute | solution.py:15
  189.6 8.3 %collective-permute-start.13 = (f32[4,16,128]{2,1,0:T(8,128)S(1)}, f32[4,16,128]{2,1,0:T(8,128)S(1)}, u32[]{:S(2)}, u32[]{:S(2)}) collective-permute-start(f32[4,16,128]{2,1,0:T(8,128)S(1)} %fusion.6), channel_id=1, source_target_pairs={{0,2},{1,3},{2,4},{3,5},{4,6},{5,7},{6,8},{7,9},{8,10},{9,11},{10,... | collective-permute-start | bytes 98312 | tf_op jit(solution)/shard_map/ppermute | solution.py:15
  208.7 10.1 %collective-permute-start.18 = (f32[4,16,128]{2,1,0:T(8,128)S(1)}, f32[4,16,128]{2,1,0:T(8,128)S(1)}, u32[]{:S(2)}, u32[]{:S(2)}) collective-permute-start(f32[4,16,128]{2,1,0:T(8,128)S(1)} %fusion.85), channel_id=1, source_target_pairs={{0,3},{1,4},{2,5},{3,6},{4,7},{8,11},{9,12},{10,13},{11,14},{12,15... | collective-permute-start | bytes 98312 | tf_op jit(solution)/shard_map/ppermute | solution.py:15
  210.2 13.7 %collective-permute-start.23 = (f32[4,16,128]{2,1,0:T(8,128)S(1)}, f32[4,16,128]{2,1,0:T(8,128)S(1)}, u32[]{:S(2)}, u32[]{:S(2)}) collective-permute-start(f32[4,16,128]{2,1,0:T(8,128)S(1)} %fusion.85), channel_id=1, source_target_pairs={{3,0},{4,1},{5,2},{6,3},{7,4},{11,8},{12,9},{13,10},{14,11},{15,12... | collective-permute-start | bytes 98312 | tf_op jit(solution)/shard_map/ppermute | solution.py:15
  211.5 12.4 %collective-permute-start.22 = (f32[4,16,128]{2,1,0:T(8,128)S(1)}, f32[4,16,128]{2,1,0:T(8,128)S(1)}, u32[]{:S(2)}, u32[]{:S(2)}) collective-permute-start(f32[4,16,128]{2,1,0:T(8,128)S(1)} %fusion.85), channel_id=1, source_target_pairs={{2,0},{3,1},{4,2},{5,3},{6,4},{7,5},{10,8},{11,9},{12,10},{13,11},... | collective-permute-start | bytes 98312 | tf_op jit(solution)/shard_map/ppermute | solution.py:15
  212.8 11.1 %collective-permute-start.21 = (f32[4,16,128]{2,1,0:T(8,128)S(1)}, f32[4,16,128]{2,1,0:T(8,128)S(1)}, u32[]{:S(2)}, u32[]{:S(2)}) collective-permute-start(f32[4,16,128]{2,1,0:T(8,128)S(1)} %fusion.85), channel_id=1, source_target_pairs={{1,0},{2,1},{3,2},{4,3},{5,4},{6,5},{7,6},{9,8},{10,9},{11,10},{12... | collective-permute-start | bytes 98312 | tf_op jit(solution)/shard_map/ppermute | solution.py:15
  214.7 9.1 %collective-permute-start.20 = (f32[4,16,128]{2,1,0:T(8,128)S(1)}, f32[4,16,128]{2,1,0:T(8,128)S(1)}, u32[]{:S(2)}, u32[]{:S(2)}) collective-permute-start(f32[4,16,128]{2,1,0:T(8,128)S(1)} %fusion.85), channel_id=1, source_target_pairs={{0,1},{1,2},{2,3},{3,4},{4,5},{5,6},{6,7},{8,9},{9,10},{10,11},{11... | collective-permute-start | bytes 98312 | tf_op jit(solution)/shard_map/ppermute | solution.py:15
  218.8 5.0 %collective-permute-start.19 = (f32[4,16,128]{2,1,0:T(8,128)S(1)}, f32[4,16,128]{2,1,0:T(8,128)S(1)}, u32[]{:S(2)}, u32[]{:S(2)}) collective-permute-start(f32[4,16,128]{2,1,0:T(8,128)S(1)} %fusion.85), channel_id=1, source_target_pairs={{0,2},{1,3},{2,4},{3,5},{4,6},{5,7},{8,10},{9,11},{10,12},{11,13},... | collective-permute-start | bytes 98312 | tf_op jit(solution)/shard_map/ppermute | solution.py:15
  286.6 10.9 %collective-permute-start.24 = (f32[4,16,128]{2,1,0:T(8,128)S(1)}, f32[4,16,128]{2,1,0:T(8,128)S(1)}, u32[]{:S(2)}, u32[]{:S(2)}) collective-permute-start(f32[4,16,128]{2,1,0:T(8,128)S(1)} %fusion.3), channel_id=1, source_target_pairs={{0,3},{1,4},{2,5},{3,6},{4,7},{8,11},{9,12},{10,13},{11,14},{12,15... | collective-permute-start | bytes 98312 | tf_op jit(solution)/shard_map/ppermute | solution.py:15
  288.1 14.6 %collective-permute-start.29 = (f32[4,16,128]{2,1,0:T(8,128)S(1)}, f32[4,16,128]{2,1,0:T(8,128)S(1)}, u32[]{:S(2)}, u32[]{:S(2)}) collective-permute-start(f32[4,16,128]{2,1,0:T(8,128)S(1)} %fusion.3), channel_id=1, source_target_pairs={{3,0},{4,1},{5,2},{6,3},{7,4},{11,8},{12,9},{13,10},{14,11},{15,12... | collective-permute-start | bytes 98312 | tf_op jit(solution)/shard_map/ppermute | solution.py:15
  289.4 13.2 %collective-permute-start.28 = (f32[4,16,128]{2,1,0:T(8,128)S(1)}, f32[4,16,128]{2,1,0:T(8,128)S(1)}, u32[]{:S(2)}, u32[]{:S(2)}) collective-permute-start(f32[4,16,128]{2,1,0:T(8,128)S(1)} %fusion.3), channel_id=1, source_target_pairs={{2,0},{3,1},{4,2},{5,3},{6,4},{7,5},{10,8},{11,9},{12,10},{13,11},... | collective-permute-start | bytes 98312 | tf_op jit(solution)/shard_map/ppermute | solution.py:15
  290.7 11.9 %collective-permute-start.27 = (f32[4,16,128]{2,1,0:T(8,128)S(1)}, f32[4,16,128]{2,1,0:T(8,128)S(1)}, u32[]{:S(2)}, u32[]{:S(2)}) collective-permute-start(f32[4,16,128]{2,1,0:T(8,128)S(1)} %fusion.3), channel_id=1, source_target_pairs={{1,0},{2,1},{3,2},{4,3},{5,4},{6,5},{7,6},{9,8},{10,9},{11,10},{12... | collective-permute-start | bytes 98312 | tf_op jit(solution)/shard_map/ppermute | solution.py:15
  293.4 9.2 %collective-permute-start.26 = (f32[4,16,128]{2,1,0:T(8,128)S(1)}, f32[4,16,128]{2,1,0:T(8,128)S(1)}, u32[]{:S(2)}, u32[]{:S(2)}) collective-permute-start(f32[4,16,128]{2,1,0:T(8,128)S(1)} %fusion.3), channel_id=1, source_target_pairs={{0,1},{1,2},{2,3},{3,4},{4,5},{5,6},{6,7},{8,9},{9,10},{10,11},{11... | collective-permute-start | bytes 98312 | tf_op jit(solution)/shard_map/ppermute | solution.py:15
  297.5 5.0 %collective-permute-start.25 = (f32[4,16,128]{2,1,0:T(8,128)S(1)}, f32[4,16,128]{2,1,0:T(8,128)S(1)}, u32[]{:S(2)}, u32[]{:S(2)}) collective-permute-start(f32[4,16,128]{2,1,0:T(8,128)S(1)} %fusion.3), channel_id=1, source_target_pairs={{0,2},{1,3},{2,4},{3,5},{4,6},{5,7},{8,10},{9,11},{10,12},{11,13},... | collective-permute-start | bytes 98312 | tf_op jit(solution)/shard_map/ppermute | solution.py:15
  331.7 38.4 %copy-start.2 = (f32[4,16,128]{2,1,0:T(8,128)}, f32[4,16,128]{2,1,0:T(8,128)S(1)}, u32[]{:S(2)}) copy-start(f32[4,16,128]{2,1,0:T(8,128)S(1)} %fusion.2) | copy-start | bytes 98308
  331.7 18.6 %collective-permute-start.30 = (f32[4,16,128]{2,1,0:T(8,128)S(1)}, f32[4,16,128]{2,1,0:T(8,128)S(1)}, u32[]{:S(2)}, u32[]{:S(2)}) collective-permute-start(f32[4,16,128]{2,1,0:T(8,128)S(1)} %fusion.2), channel_id=1, source_target_pairs={{0,3},{1,4},{2,5},{3,6},{4,7},{5,8},{6,9},{7,10},{8,11},{9,12},{10... | collective-permute-start | bytes 98312 | tf_op jit(solution)/shard_map/ppermute | solution.py:15
  333.6 25.7 %collective-permute-start.35 = (f32[4,16,128]{2,1,0:T(8,128)S(1)}, f32[4,16,128]{2,1,0:T(8,128)S(1)}, u32[]{:S(2)}, u32[]{:S(2)}) collective-permute-start(f32[4,16,128]{2,1,0:T(8,128)S(1)} %fusion.2), channel_id=1, source_target_pairs={{3,0},{4,1},{5,2},{6,3},{7,4},{8,5},{9,6},{10,7},{11,8},{12,9},{13... | collective-permute-start | bytes 98312 | tf_op jit(solution)/shard_map/ppermute | solution.py:15
  340.9 18.4 %collective-permute-start.34 = (f32[4,16,128]{2,1,0:T(8,128)S(1)}, f32[4,16,128]{2,1,0:T(8,128)S(1)}, u32[]{:S(2)}, u32[]{:S(2)}) collective-permute-start(f32[4,16,128]{2,1,0:T(8,128)S(1)} %fusion.2), channel_id=1, source_target_pairs={{2,0},{3,1},{4,2},{5,3},{6,4},{7,5},{8,6},{9,7},{10,8},{11,9},{12,... | collective-permute-start | bytes 98312 | tf_op jit(solution)/shard_map/ppermute | solution.py:15
  342.8 16.4 %collective-permute-start.33 = (f32[4,16,128]{2,1,0:T(8,128)S(1)}, f32[4,16,128]{2,1,0:T(8,128)S(1)}, u32[]{:S(2)}, u32[]{:S(2)}) collective-permute-start(f32[4,16,128]{2,1,0:T(8,128)S(1)} %fusion.2), channel_id=1, source_target_pairs={{1,0},{2,1},{3,2},{4,3},{5,4},{6,5},{7,6},{8,7},{9,8},{10,9},{11,1... | collective-permute-start | bytes 98312 | tf_op jit(solution)/shard_map/ppermute | solution.py:15
  346.8 12.4 %collective-permute-start.32 = (f32[4,16,128]{2,1,0:T(8,128)S(1)}, f32[4,16,128]{2,1,0:T(8,128)S(1)}, u32[]{:S(2)}, u32[]{:S(2)}) collective-permute-start(f32[4,16,128]{2,1,0:T(8,128)S(1)} %fusion.2), channel_id=1, source_target_pairs={{0,1},{1,2},{2,3},{3,4},{4,5},{5,6},{6,7},{7,8},{8,9},{9,10},{10,1... | collective-permute-start | bytes 98312 | tf_op jit(solution)/shard_map/ppermute | solution.py:15
  350.3 8.9 %collective-permute-start.31 = (f32[4,16,128]{2,1,0:T(8,128)S(1)}, f32[4,16,128]{2,1,0:T(8,128)S(1)}, u32[]{:S(2)}, u32[]{:S(2)}) collective-permute-start(f32[4,16,128]{2,1,0:T(8,128)S(1)} %fusion.2), channel_id=1, source_target_pairs={{0,2},{1,3},{2,4},{3,5},{4,6},{5,7},{6,8},{7,9},{8,10},{9,11},{10,... | collective-permute-start | bytes 98312 | tf_op jit(solution)/shard_map/ppermute | solution.py:15
where the time goes:
time: 372 us; the launch traced here: 370 us
  blocking collectives  128 us (34%)
  starting transfers between devices  113 us (30%)
  matrix products  64.6 us (17%)
  waiting for transfers between devices  30.9 us (8%)
  other arithmetic  24.9 us (7%)
  local copies, waits for them, and re-layouts  6.56 us (2%)
    ppermute x36, starting transfers between devices, from_behind(): lax.ppermute(value, axis, [(source, source + steps) for source in range(f...  113 us
    dot_general x6, matrix products, tile_product(): jnp.einsum('ikab,ikcb->ica', matrix_tiles, picked, precision=lax.Precisio...  57 us
    psum x1, blocking collectives, per_device(): lax.psum((inner_products(direction, applied), inner_products(applied, res...  36.1 us
    psum x1, blocking collectives, per_device(): squares = lax.psum(inner_products(residual, residual), ('grp', 'row'))  36.1 us
    ppermute x36, waiting for transfers between devices, from_behind(): lax.ppermute(value, axis, [(source, source + steps) for source in range(f...  30.9 us
    psum x1, blocking collectives, per_device(): weight = lax.psum(inner_products(remainder, smoothed), 'row')  24.9 us
    psum x1, blocking collectives, per_device(): weight_next = lax.psum(inner_products(remainder, smoothed), 'row')  17.3 us
    psum x1, blocking collectives, per_device(): bending = lax.psum(inner_products(heading, applied), 'row')  13.9 us
  transfers between devices with their start and end apart: 36, of which 7 were waited for; matrix products, arithmetic and copies ran while one was open for 1% of the time, Pallas kernels for 0%

commit v1 on v0

v1 whole, which is shorter than its diff:
```python
import jax
import jax.numpy as jnp
from jax import lax
from jax.experimental import pallas as pl
from jax.experimental.pallas import tpu as pltpu
from jax.sharding import PartitionSpec as P

BAND = 12
SLOTS = 7
HIGHEST = lax.Precision.HIGHEST
AXES = ("grp", "row")
VMEM = pltpu.VMEM
SMEM = pltpu.SMEM


def spec(space):
    return pl.BlockSpec(memory_space=space)


def params(mib):
    return pltpu.CompilerParams(vmem_limit_bytes=mib << 20)


def dot_nt(former, latter):
    return lax.dot_general(
        former, latter, (((1,), (1,)), ((), ())), precision=HIGHEST,
        preferred_element_type=jnp.float32,
    )


def dot_tn(former, latter):
    return lax.dot_general(
        former, latter, (((0,), (0,)), ((), ())), precision=HIGHEST,
        preferred_element_type=jnp.float32,
    )


def dot_nn(former, latter):
    return jnp.dot(former, latter, precision=HIGHEST, preferred_element_type=jnp.float32)


def split3(value):
    high = value.astype(jnp.bfloat16)
    rest = value - high.astype(jnp.float32)
    middle = rest.astype(jnp.bfloat16)
    low = (rest - middle.astype(jnp.float32)).astype(jnp.bfloat16)
    return high, middle, low


def build_table(pieces, flags_ref, table_ref, classes, blocks, cols):
    slot = 0
    for piece in pieces:
        for first in range(0, piece.shape[0], blocks):
            for block in range(blocks):
                value = piece[first + block]
                for k in range(classes):
                    terms = split3(value * flags_ref[k, slot])
                    for s, term in enumerate(terms):
                        table_ref[slot * blocks + block, pl.ds((3 * k + s) * cols, cols), :] = term
            slot += 1


def row_product(index_ref, table_ref, tile_ref, row, classes, cols):
    count, tb = tile_ref.shape[1], tile_ref.shape[2]
    total = None
    for k in range(0, count, 2):
        left = jnp.concatenate(
            [table_ref[index_ref[row, k]], table_ref[index_ref[row, k + 1]]], axis=1
        )
        highs, rests = [], []
        for j in (k, k + 1):
            tile = tile_ref[row, j]
            high = tile.astype(jnp.bfloat16)
            highs.append(high)
            rests.append((tile - high.astype(jnp.float32)).astype(jnp.bfloat16))
        right = jnp.concatenate(
            [jnp.concatenate(highs, axis=1), jnp.concatenate(rests, axis=1)], axis=0
        )
        part = lax.dot_general(
            left, right, (((1,), (1,)), ((), ())), preferred_element_type=jnp.float32
        )
        total = part if total is None else total + part
    total = total[:, :tb] + total[:, tb:]
    out = []
    for k in range(classes):
        base = 3 * k * cols
        out.append(
            total[base : base + cols]
            + total[base + cols : base + 2 * cols]
            + total[base + 2 * cols : base + 3 * cols]
        )
    return out


def stream(tiles_hbm, tiles, sems):
    copies = [
        pltpu.make_async_copy(tiles_hbm.at[row], tiles.at[row], sems.at[row])
        for row in range(tiles.shape[0])
    ]
    for copy in copies:
        copy.start()
    return copies


def lanes(ref):
    return jnp.concatenate([ref[i] for i in range(ref.shape[0])], axis=1)


def pack_gram(gram_ref, former, latter, scale, cols):
    gram = dot_nt(former, latter)
    if scale is not None:
        gram = gram * scale
    width = gram.shape[1]
    packed = jnp.concatenate(
        [gram[:cols], gram[cols:], jnp.zeros((cols, gram_ref.shape[2] - 2 * width), jnp.float32)],
        axis=1,
    )
    gram_ref[...] = jnp.broadcast_to(packed[None], gram_ref.shape)


def first_kernel(index_ref, flags_ref, tiles_hbm, v, sw, p1, p2, p3, parts, image, tiles, table, sems):
    blocks, cols, _ = v.shape
    copies = stream(tiles_hbm, tiles, sems)
    build_table((v, sw, p1, p2, p3), flags_ref, table, 3, blocks, cols)
    for row in range(blocks):
        copies[row].wait()
        out = row_product(index_ref, table, tiles, row, 3, cols)
        for k in range(3):
            parts[k, row] = out[k]
        image[row] = out[0] + out[1] + out[2]


def second_kernel(
    index_ref, flags_ref, tiles_hbm, right, v, sw, p1, p2, p3, parts, gram, tiles, table, sems, image
):
    blocks, cols, _ = v.shape
    copies = stream(tiles_hbm, tiles, sems)
    build_table((v, sw, p1, p2, p3), flags_ref, table, 3, blocks, cols)
    for row in range(blocks):
        copies[row].wait()
        out = row_product(index_ref, table, tiles, row, 3, cols)
        for k in range(3):
            parts[k, row] = out[k]
        image[row] = out[0] + out[1] + out[2]
    former = jnp.concatenate([lanes(right), lanes(v)], axis=0)
    latter = jnp.concatenate([former, lanes(image)], axis=0)
    pack_gram(gram, former, latter, None, cols)


def third_kernel(
    index_ref, flags_ref, tiles_hbm, precond, v, sw, p1, p2, p3, applied, smooth, lost, tiles, table, sems
):
    blocks, cols, _ = v.shape
    copies = stream(tiles_hbm, tiles, sems)
    build_table((v, sw, p1, p2, p3), flags_ref, table, 2, blocks, cols)
    mine = flags_ref[3, 0]
    for row in range(blocks):
        copies[row].wait()
        out = row_product(index_ref, table, tiles, row, 2, cols)
        applied[row] = out[0]
        lost[row] = out[0] * mine + out[1]
        smooth[row] = dot_nt(out[0], precond[row])


def fourth_kernel(
    index_ref, flags_ref, tiles_hbm, target, head, applied, v, sw, p1, p2, p3, lost, gram,
    tiles, table, sems, second,
):
    blocks, cols, _ = v.shape
    copies = stream(tiles_hbm, tiles, sems)
    build_table((v, sw, p1, p2, p3), flags_ref, table, 2, blocks, cols)
    mine = flags_ref[3, 0]
    for row in range(blocks):
        copies[row].wait()
        out = row_product(index_ref, table, tiles, row, 2, cols)
        second[row] = out[0]
        lost[row] = out[0] * mine + out[1]
    former = jnp.concatenate([lanes(head), lanes(v)], axis=0)
    latter = jnp.concatenate([lanes(target), lanes(applied), lanes(second)], axis=0)
    pack_gram(gram, former, latter, mine, cols)


def tile_call(kernel, classes, outs, extra, tiles, operands_vmem, index, flags):
    blocks, count, tb, _ = tiles.shape
    cols = operands_vmem[-1].shape[1]
    scratch = [
        VMEM((blocks, count, tb, tb), jnp.float32),
        VMEM((SLOTS * blocks, 3 * classes * cols, tb), jnp.bfloat16),
        pltpu.SemaphoreType.DMA((blocks,)),
    ] + extra
    return pl.pallas_call(
        kernel,
        out_shape=outs,
        in_specs=[spec(SMEM), spec(SMEM), spec(pl.ANY)] + [spec(VMEM)] * len(operands_vmem),
        out_specs=[spec(VMEM)] * len(outs),
        scratch_shapes=scratch,
        compiler_params=params(32),
    )(index, flags, tiles, *operands_vmem)


def eliminate(matrix, target):
    size = matrix.shape[0]
    work = jnp.concatenate([matrix, target], axis=1)
    rows = lax.broadcasted_iota(jnp.int32, (size, 1), 0)
    for j in range(size):
        pivot = work[j : j + 1, :] / work[j : j + 1, j : j + 1]
        column = work[:, j : j + 1]
        work = jnp.where(rows == j, pivot, work - column * pivot)
    return work[:, size:]


def coefficients(gathered, cols):
    packed = jnp.sum(gathered[...], axis=0)
    width = 3 * cols
    top, bottom = packed[:, :width], packed[:, width : 2 * width]
    g00, g01 = top[:, :cols], top[:, cols : 2 * cols]
    g11 = bottom[:, cols : 2 * cols]
    big = jnp.concatenate([top[:, cols:], bottom[:, cols:]], axis=0)
    unit = (
        lax.broadcasted_iota(jnp.int32, (cols, cols), 0)
        == lax.broadcasted_iota(jnp.int32, (cols, cols), 1)
    ).astype(jnp.float32)
    g00 = 0.5 * (g00 + g00.T)
    advance = eliminate(0.5 * (g01 + g01.T), g00)
    inverse = eliminate(g00, unit)
    crossed = dot_nn(g01, advance)
    squares = g00 - crossed - crossed.T + dot_tn(advance, dot_nn(g11, advance))
    mixing = dot_nn(inverse, squares)
    heading = jnp.concatenate([unit + mixing, -advance], axis=0)
    curvature = dot_tn(heading, dot_nn(big, heading))
    second = eliminate(0.5 * (curvature + curvature.T), squares)
    combo = dot_nn(heading, second)
    return jnp.concatenate([combo[:cols] + advance, combo[cols:]], axis=0)


def outer_kernel(
    flags_ref, gathered, right, image, parts_b, parts_y, precond, solution, target, head, kept
):
    blocks, cols, tb = right.shape
    mine = flags_ref[3, 0]
    weights = coefficients(gathered, cols)

    def basis(pick):
        return jnp.concatenate(
            [
                jnp.concatenate([pick(0, i) for i in range(blocks)], axis=1),
                jnp.concatenate([pick(1, i) for i in range(blocks)], axis=1),
            ],
            axis=0,
        )

    parts = (parts_b, parts_y)
    own = (right, image)
    stacked = jnp.concatenate(
        [
            basis(lambda n, i: own[n][i]),
            basis(lambda n, i: parts[n][1, i] + parts[n][2, i]),
            basis(lambda n, i: parts[n][0, i] * (1.0 - mine) + parts[n][2, i]),
        ],
        axis=1,
    )
    made = dot_tn(weights, stacked)
    span = blocks * tb
    for i in range(blocks):
        solution[i] = made[:, i * tb : (i + 1) * tb]
        aim = right[i] - made[:, span + i * tb : span + (i + 1) * tb]
        target[i] = aim
        head[i] = dot_nt(aim, precond[i])
        kept[i] = made[:, 2 * span + i * tb : 2 * span + (i + 1) * tb]


def inner_kernel(
    flags_ref, gathered, right, solution, kept, head, smooth, lost0, lost1, recovered, residual
):
    blocks, cols, tb = right.shape
    mine = flags_ref[3, 0]
    weights = coefficients(gathered, cols)
    stacked = jnp.concatenate(
        [
            jnp.concatenate([lanes(head), lanes(lost0)], axis=1),
            jnp.concatenate([lanes(smooth), lanes(lost1)], axis=1),
        ],
        axis=0,
    )
    made = dot_tn(weights, stacked)
    span = blocks * tb
    for i in range(blocks):
        estimate = made[:, i * tb : (i + 1) * tb]
        recovered[i] = jnp.where(mine > 0.5, estimate, solution[i])
        residual[i] = right[i] - kept[i] - made[:, span + i * tb : span + (i + 1) * tb]


def small_call(kernel, outs, flags, gathered, *arrays):
    return pl.pallas_call(
        kernel,
        out_shape=outs,
        in_specs=[spec(SMEM)] + [spec(VMEM)] * (1 + len(arrays)),
        out_specs=[spec(VMEM)] * len(outs),
        compiler_params=params(16),
    )(flags, gathered, *arrays)


def move(value, total, where):
    pairs = [(i, where(i)) for i in range(total) if 0 <= where(i) < total]
    return lax.ppermute(value, AXES, pairs)


def window(value, total):
    swapped = move(value, total, lambda i: i ^ 1)
    far = move(value, total, lambda i: i - 3 if i % 2 == 0 else i + 3)
    pair = jnp.concatenate([value, swapped], axis=0)
    near = move(pair, total, lambda i: i - 1 if i % 2 == 0 else i + 1)
    other = move(near, total, lambda i: i ^ 1)
    return value, swapped, near, other, far


def slot_offsets(odd):
    even_slots = jnp.array([0, 1, -1, -2, 2, 3, -3], jnp.int32)
    return jnp.where(odd, -even_slots, even_slots)


def exchange(gram):
    return lax.all_to_all(gram, AXES, 0, 0)


def per_device(matrix_tiles, column_index, precond, right_side, lost_group):
    blocks, cols, tb = right_side.shape
    assert -(-BAND // blocks) * 2 + 1 == SLOTS
    row_count = lax.axis_size("row")
    group_count = lax.axis_size("grp")
    total = row_count * group_count
    me = lax.axis_index(AXES)
    my_group = lax.axis_index("grp")
    lost = lost_group[0] % group_count
    mine = my_group == lost

    offsets = slot_offsets(me % 2 == 1)
    device = column_index // blocks - me
    signed = jnp.where(me % 2 == 1, -device, device)
    slot = jnp.zeros_like(signed)
    for place, offset in enumerate((0, 1, -1, -2, 2, 3, -3)):
        slot = jnp.where(signed == offset, place, slot)
    index = slot * blocks + column_index % blocks
    owner = (me + offsets) // row_count
    in_own = owner == my_group
    in_lost = owner == lost
    flags = jnp.stack(
        [
            in_own,
            jnp.logical_and(in_lost, jnp.logical_not(in_own)),
            jnp.logical_not(jnp.logical_or(in_own, in_lost)),
            jnp.broadcast_to(mine, (SLOTS,)),
        ]
    ).astype(jnp.float32)

    vec = jax.ShapeDtypeStruct(right_side.shape, jnp.float32)
    vec3 = jax.ShapeDtypeStruct((3,) + right_side.shape, jnp.float32)
    gram = jax.ShapeDtypeStruct((total, cols, tb), jnp.float32)
    held = VMEM(right_side.shape, jnp.float32)

    parts_b, image = tile_call(
        first_kernel, 3, [vec3, vec], [], matrix_tiles, window(right_side, total), index, flags
    )
    parts_y, gram_outer = tile_call(
        second_kernel, 3, [vec3, gram], [held], matrix_tiles,
        (right_side,) + window(image, total), index, flags,
    )
    solution, target, head, kept = small_call(
        outer_kernel, [vec] * 4, flags, exchange(gram_outer), right_side, image, parts_b, parts_y, precond
    )
    applied, smooth, lost0 = tile_call(
        third_kernel, 2, [vec] * 3, [], matrix_tiles, (precond,) + window(head, total), index, flags
    )
    lost1, gram_inner = tile_call(
        fourth_kernel, 2, [vec, gram], [held], matrix_tiles,
        (target, head, applied) + window(smooth, total), index, flags,
    )
    recovered, residual = small_call(
        inner_kernel, [vec] * 2, flags, exchange(gram_inner), right_side, solution, kept, head, smooth,
        lost0, lost1,
    )
    return (recovered, residual)


def solution(mesh):
    in_specs = (
        P(("grp", "row"), None, None, None),
        P(("grp", "row"), None),
        P(("grp", "row"), None, None),
        P(("grp", "row"), None, None),
        P(),
    )
    out_specs = (P(("grp", "row"), None, None), P(("grp", "row"), None, None))
    return jax.shard_map(
        per_device, mesh=mesh, in_specs=in_specs, out_specs=out_specs, check_vma=False
    )
```

time: 372 us -> 144 us (0.39)
  blocking collectives: 128 us -> 27.8 us
  starting transfers between devices: 113 us -> 37.7 us
  matrix products: 64.6 us -> 0 us
  Pallas kernels: 0 us -> 38.4 us
  other arithmetic: 24.9 us -> 2.24 us
    psum x5 -> x0, blocking collectives: 128 us -> none  [the longest x1 36.1 us: per_device(): lax.psum((inner_products(direction, applied), inner_products(applied, res...]
    ppermute x36 -> x16, starting transfers between devices: 113 us -> 37.7 us  [move(): return lax.ppermute(value, AXES, pairs)]
    dot_general x28 -> x0, matrix products: 62.2 us -> none  [the longest x6 57 us: tile_product(): jnp.einsum('ikab,ikcb->ica', matrix_tiles, picked, precision=lax.Precisio...]
    pallas_call x0 -> x6, Pallas kernels: none -> 38.4 us  [the longest x4 27.3 us: tile_call(): pl.pallas_call(kernel, out_shape=outs, in_specs=[spec(SMEM), spec(SMEM),...]
    all_to_all x0 -> x2, blocking collectives: none -> 27.8 us  [exchange(): return lax.all_to_all(gram, AXES, 0, 0)]
    another operation x30 -> x2, other arithmetic: 24.1 us -> 0.69 us  [per_device(): jnp.stack([in_own, jnp.logical_and(in_lost, jnp.logical_not(in_own)), jnp...]
    gather x6 -> x0, local copies, waits for them, and re-layouts: 4.55 us -> none  [tile_product(): picked = jnp.take(window, local_cols, axis=0)]
    ppermute x36 -> x16, waiting for transfers between devices: 30.9 us -> 29.8 us  [move(): return lax.ppermute(value, AXES, pairs)]
  transfers between devices with their start and end apart: 36 -> 16, of which waited for: 7 -> 11; matrix products, arithmetic and copies ran while one was open for 1% -> 2% of each run, Pallas kernels for 0% -> 0%
where the time goes in v1:
time: 144 us; the launch traced here: 142 us
  Pallas kernels  38.4 us (27%)
  starting transfers between devices  37.7 us (26%)
  waiting for transfers between devices  29.8 us (21%)
  blocking collectives  27.8 us (19%)
  local copies, waits for them, and re-layouts  4.22 us (3%)
  other arithmetic  2.24 us (2%)
    ppermute x16, starting transfers between devices, move(): return lax.ppermute(value, AXES, pairs)  37.7 us
    ppermute x16, waiting for transfers between devices, move(): return lax.ppermute(value, AXES, pairs)  29.8 us
    all_to_all x2, blocking collectives, exchange(): return lax.all_to_all(gram, AXES, 0, 0)  27.8 us
    pallas_call x4, Pallas kernels, tile_call(): pl.pallas_call(kernel, out_shape=outs, in_specs=[spec(SMEM), spec(SMEM),...  27.3 us
    pallas_call x2, Pallas kernels, small_call(): pl.pallas_call(kernel, out_shape=outs, in_specs=[spec(SMEM)] + [spec(VMEM...  11.1 us
    unnamed x8, local copies, waits for them, and re-layouts  4.15 us
  transfers between devices with their start and end apart: 16, of which 11 were waited for; matrix products, arithmetic and copies ran while one was open for 2% of the time, Pallas kernels for 0%

profile of v1, /device:TPU:5, one launch (start us, length us, event | category | flops | bytes accessed | tf_op | source)
XLA Modules:
  0.0 141.6 jit_solution(1954624070188841025)
XLA Ops:
  0.6 4.8 %collective-permute-start.3 = (f32[4,16,128]{2,1,0:T(8,128)}, f32[4,16,128]{2,1,0:T(8,128)S(1)}, u32[]{:S(2)}, u32[]{:S(2)}) collective-permute-start(f32[4,16,128]{2,1,0:T(8,128)} %right.5), channel_id=1, source_target_pairs={{1,4},{3,6},{4,1},{5,8},{6,3},{7,10},{8,5},{9,12},{10,7},{11,14},{... | collective-permute-start | bytes 98312 | tf_op jit(solution)/shard_map/ppermute | solution.py:305
  5.4 0.8 collective-permute-start
  6.2 0.7 fusion.1.index_ref
  6.9 0.7 fusion.4
  8.2 0.0 collective-permute-done.sw
  8.2 0.8 pad_maximum_fusion
  9.0 3.1 %collective-permute-start.1 = (f32[8,16,128]{2,1,0:T(8,128)S(1)}, f32[8,16,128]{2,1,0:T(8,128)S(1)}, u32[]{:S(2)}, u32[]{:S(2)}) collective-permute-start(f32[8,16,128]{2,1,0:T(8,128)S(1)} %pad_maximum_fusion), channel_id=1, source_target_pairs={{1,2},{2,1},{3,4},{4,3},{5,6},{6,5},{7,8},{8,7},{9,10},{10,9},{11,... | collective-permute-start | bytes 196616 | tf_op jit(solution)/shard_map/ppermute | solution.py:305
  12.2 0.1 pad.11.clone
  12.2 2.4 %collective-permute-done.1.p1 = f32[8,16,128]{2,1,0:T(8,128)S(1)} collective-permute-done((f32[8,16,128]{2,1,0:T(8,128)S(1)}, f32[8,16,128]{2,1,0:T(8,128)S(1)}, u32[]{:S(2)}, u32[]{:S(2)}) %collective-permute-start.1) | collective-permute-done | bytes 65568 | tf_op jit(solution)/shard_map/ppermute | solution.py:305
  14.6 3.6 %collective-permute-start.2 = (f32[8,16,128]{2,1,0:T(8,128)S(1)}, f32[8,16,128]{2,1,0:T(8,128)S(1)}, u32[]{:S(2)}, u32[]{:S(2)}) collective-permute-start(f32[8,16,128]{2,1,0:T(8,128)S(1)} %collective-permute-done.1.p1), channel_id=1, source_target_pairs={{0,1},{1,0},{2,3},{3,2},{4,5},{5,4},{6,7},{7,6},{8,9},{9,8},{10,11... | collective-permute-start | bytes 196616 | tf_op jit(solution)/shard_map/ppermute | solution.py:305
  18.2 0.1 add_convert_fusion.flags_ref
  18.3 0.0 collective-permute-done.3.p3
  18.3 0.8 collective-permute-done.2.p2
  19.1 0.0 copy-start
  19.1 3.4 %copy-done = f32[4,32,128,128]{3,2,1,0:T(8,128)S(1)} copy-done((f32[4,32,128,128]{3,2,1,0:T(8,128)S(1)}, f32[4,32,128,128]{3,2,1,0:T(8,128)}, u32[]{:S(2)}) %copy-start) | copy-done | bytes 8388632
  22.5 0.0 copy-start.2
  22.5 0.8 copy-done.2
  23.3 0.0 copy-start.1
  23.3 6.5 %shard_map.77 = (f32[3,4,16,128]{3,2,1,0:T(8,128)S(1)}, f32[4,16,128]{2,1,0:T(8,128)S(1)}) custom-call(s32[4,32]{1,0:T(4,128)S(1)} %fusion.1.index_ref, f32[4,7]{1,0:T(4,128)S(1)} %add_convert_fusion.flags_ref, f32[4,32,128,128]{3,2,1,0:T(8,128)S(1)} %copy-done, f32[4,16,128]{2,1,0:T(8,128)S(1)} %copy-done.2, f32[4,16,128]{2,1,0:T(8,128)S(1)} %collective-permute-done.sw, ...), custom_call_target="tpu_custom_call" | custom-call | tf_op jit(solution)/shard_map/pallas_call | solution.py:191
  29.8 0.4 collective-permute-start.4
  30.2 0.9 collective-permute-done.4.sw
  31.0 1.9 %collective-permute-start.5 = (f32[8,16,128]{2,1,0:T(8,128)S(1)}, f32[8,16,128]{2,1,0:T(8,128)S(1)}, u32[]{:S(2)}, u32[]{:S(2)}) collective-permute-start(f32[8,16,128]{2,1,0:T(8,128)S(1)} %pad_maximum_fusion.1), channel_id=1, source_target_pairs={{1,2},{2,1},{3,4},{4,3},{5,6},{6,5},{7,8},{8,7},{9,10},{10,9},{11,... | collective-permute-start | bytes 196616 | tf_op jit(solution)/shard_map/ppermute | solution.py:305
  33.0 3.7 %collective-permute-done.5.p1 = f32[8,16,128]{2,1,0:T(8,128)S(1)} collective-permute-done((f32[8,16,128]{2,1,0:T(8,128)S(1)}, f32[8,16,128]{2,1,0:T(8,128)S(1)}, u32[]{:S(2)}, u32[]{:S(2)}) %collective-permute-start.5) | collective-permute-done | bytes 65568 | tf_op jit(solution)/shard_map/ppermute | solution.py:305
  36.6 3.9 %collective-permute-start.6 = (f32[8,16,128]{2,1,0:T(8,128)S(1)}, f32[8,16,128]{2,1,0:T(8,128)S(1)}, u32[]{:S(2)}, u32[]{:S(2)}) collective-permute-start(f32[8,16,128]{2,1,0:T(8,128)S(1)} %collective-permute-done.5.p1), channel_id=1, source_target_pairs={{0,1},{1,0},{2,3},{3,2},{4,5},{5,4},{6,7},{7,6},{8,9},{9,8},{10,11... | collective-permute-start | bytes 196616 | tf_op jit(solution)/shard_map/ppermute | solution.py:305
  40.6 1.9 %collective-permute-start.7 = (f32[4,16,128]{2,1,0:T(8,128)S(1)}, f32[4,16,128]{2,1,0:T(8,128)S(1)}, u32[]{:S(2)}, u32[]{:S(2)}) collective-permute-start(f32[4,16,128]{2,1,0:T(8,128)S(1)} %get-tuple-element.15.v.image), channel_id=1, source_target_pairs={{1,4},{3,6},{4,1},{5,8},{6,3},{7,10},{8,5},{9,12},{10,7},{11,14},{... | collective-permute-start | bytes 98312 | tf_op jit(solution)/shard_map/ppermute | solution.py:305
  42.5 4.2 %collective-permute-done.7.p3 = f32[4,16,128]{2,1,0:T(8,128)S(1)} collective-permute-done((f32[4,16,128]{2,1,0:T(8,128)S(1)}, f32[4,16,128]{2,1,0:T(8,128)S(1)}, u32[]{:S(2)}, u32[]{:S(2)}) %collective-permute-start.7) | collective-permute-done | bytes 32800 | tf_op jit(solution)/shard_map/ppermute | solution.py:305
  46.7 0.0 collective-permute-done.6.p2
  46.7 6.7 %shard_map.78 = (f32[3,4,16,128]{3,2,1,0:T(8,128)S(1)}, f32[32,16,128]{2,1,0:T(8,128)S(1)}) custom-call(s32[4,32]{1,0:T(4,128)S(1)} %fusion.1.index_ref, f32[4,7]{1,0:T(4,128)S(1)} %add_convert_fusion.flags_ref, f32[4,32,128,128]{3,2,1,0:T(8,128)S(1)} %copy-done, f32[4,16,128]{2,1,0:T(8,128)S(1)} %copy-done.2, f32[4,16,128]{2,1,0:T(8,128)S(1)} %get-tuple-element.15.v.image, ...), custom_call_target="tpu_custom_call" | custom-call | tf_op jit(solution)/shard_map/pallas_call | solution.py:191
  53.4 14.1 %all_to_all.10.gathered = f32[32,16,128]{2,1,0:T(8,128)S(1)} all-to-all(f32[32,16,128]{2,1,0:T(8,128)S(1)} %get-tuple-element.16), channel_id=1, replica_groups=mesh['grp'=4,'row'=8] {'grp','row'}, dimensions={0} | all-to-all | bytes 524288 | tf_op jit(solution)/shard_map/all_to_all | solution.py:323
  67.5 0.0 copy-done.1
  67.5 5.5 %shard_map.79 = (f32[4,16,128]{2,1,0:T(8,128)S(1)}, f32[4,16,128]{2,1,0:T(8,128)S(1)}, f32[4,16,128]{2,1,0:T(8,128)S(1)}, f32[4,16,128]{2,1,0:T(8,128)S(1)}) custom-call(f32[4,7]{1,0:T(4,128)S(1)} %add_convert_fusion.flags_ref, f32[32,16,128]{2,1,0:T(8,128)S(1)} %all_to_all.10.gathered, f32[4,16,128]{2,1,0:T(8,128)S(1)} %copy-done.2, ...), custom_call_target="tpu_custom_call" | custom-call | tf_op jit(solution)/shard_map/pallas_call | solution.py:294
  73.0 0.0 collective-permute-start.8
  73.0 1.2 collective-permute-done.8.sw
  74.2 0.0 copy-start.3
  74.2 2.0 %collective-permute-start.9 = (f32[8,16,128]{2,1,0:T(8,128)S(1)}, f32[8,16,128]{2,1,0:T(8,128)S(1)}, u32[]{:S(2)}, u32[]{:S(2)}) collective-permute-start(f32[8,16,128]{2,1,0:T(8,128)S(1)} %pad_maximum_fusion.2), channel_id=1, source_target_pairs={{1,2},{2,1},{3,4},{4,3},{5,6},{6,5},{7,8},{8,7},{9,10},{10,9},{11,... | collective-permute-start | bytes 196616 | tf_op jit(solution)/shard_map/ppermute | solution.py:305
  76.3 3.6 %collective-permute-done.9.p1 = f32[8,16,128]{2,1,0:T(8,128)S(1)} collective-permute-done((f32[8,16,128]{2,1,0:T(8,128)S(1)}, f32[8,16,128]{2,1,0:T(8,128)S(1)}, u32[]{:S(2)}, u32[]{:S(2)}) %collective-permute-start.9) | collective-permute-done | bytes 65568 | tf_op jit(solution)/shard_map/ppermute | solution.py:305
  79.8 3.9 %collective-permute-start.10 = (f32[8,16,128]{2,1,0:T(8,128)S(1)}, f32[8,16,128]{2,1,0:T(8,128)S(1)}, u32[]{:S(2)}, u32[]{:S(2)}) collective-permute-start(f32[8,16,128]{2,1,0:T(8,128)S(1)} %collective-permute-done.9.p1), channel_id=1, source_target_pairs={{0,1},{1,0},{2,3},{3,2},{4,5},{5,4},{6,7},{7,6},{8,9},{9,8},{10,11... | collective-permute-start | bytes 196616 | tf_op jit(solution)/shard_map/ppermute | solution.py:305
  83.7 1.9 %collective-permute-start.11 = (f32[4,16,128]{2,1,0:T(8,128)S(1)}, f32[4,16,128]{2,1,0:T(8,128)S(1)}, u32[]{:S(2)}, u32[]{:S(2)}) collective-permute-start(f32[4,16,128]{2,1,0:T(8,128)S(1)} %get-tuple-element.20.v.head), channel_id=1, source_target_pairs={{1,4},{3,6},{4,1},{5,8},{6,3},{7,10},{8,5},{9,12},{10,7},{11,14},{... | collective-permute-start | bytes 98312 | tf_op jit(solution)/shard_map/ppermute | solution.py:305
  85.6 4.2 %collective-permute-done.11.p3 = f32[4,16,128]{2,1,0:T(8,128)S(1)} collective-permute-done((f32[4,16,128]{2,1,0:T(8,128)S(1)}, f32[4,16,128]{2,1,0:T(8,128)S(1)}, u32[]{:S(2)}, u32[]{:S(2)}) %collective-permute-start.11) | collective-permute-done | bytes 32800 | tf_op jit(solution)/shard_map/ppermute | solution.py:305
  89.8 0.0 collective-permute-done.10.p2
  89.8 7.5 %shard_map.80 = (f32[4,16,128]{2,1,0:T(8,128)S(1)}, f32[4,16,128]{2,1,0:T(8,128)S(1)}, f32[4,16,128]{2,1,0:T(8,128)S(1)}) custom-call(s32[4,32]{1,0:T(4,128)S(1)} %fusion.1.index_ref, f32[4,7]{1,0:T(4,128)S(1)} %add_convert_fusion.flags_ref, f32[4,32,128,128]{3,2,1,0:T(8,128)S(1)} %copy-done, f32[4,128,128]{2,1,0:T(8,128)S(1)} %copy-done.1, ...), custom_call_target="tpu_custom_call" | custom-call | tf_op jit(solution)/shard_map/pallas_call | solution.py:191
  97.4 1.9 %collective-permute-start.12 = (f32[4,16,128]{2,1,0:T(8,128)S(1)}, f32[4,16,128]{2,1,0:T(8,128)S(1)}, u32[]{:S(2)}, u32[]{:S(2)}) collective-permute-start(f32[4,16,128]{2,1,0:T(8,128)S(1)} %get-tuple-element.22.v.smooth), channel_id=1, source_target_pairs={{0,1},{1,0},{2,3},{3,2},{4,5},{5,4},{6,7},{7,6},{8,9},{9,8},{10,11... | collective-permute-start | bytes 98312 | tf_op jit(solution)/shard_map/ppermute | solution.py:305
  99.3 0.9 collective-permute-done.12.sw
  100.1 1.9 %collective-permute-start.13 = (f32[8,16,128]{2,1,0:T(8,128)S(1)}, f32[8,16,128]{2,1,0:T(8,128)S(1)}, u32[]{:S(2)}, u32[]{:S(2)}) collective-permute-start(f32[8,16,128]{2,1,0:T(8,128)S(1)} %pad_maximum_fusion.3), channel_id=1, source_target_pairs={{1,2},{2,1},{3,4},{4,3},{5,6},{6,5},{7,8},{8,7},{9,10},{10,9},{11,... | collective-permute-start | bytes 196616 | tf_op jit(solution)/shard_map/ppermute | solution.py:305
  102.0 4.0 %collective-permute-done.13.p1 = f32[8,16,128]{2,1,0:T(8,128)S(1)} collective-permute-done((f32[8,16,128]{2,1,0:T(8,128)S(1)}, f32[8,16,128]{2,1,0:T(8,128)S(1)}, u32[]{:S(2)}, u32[]{:S(2)}) %collective-permute-start.13) | collective-permute-done | bytes 65568 | tf_op jit(solution)/shard_map/ppermute | solution.py:305
  106.0 3.6 %collective-permute-start.14 = (f32[8,16,128]{2,1,0:T(8,128)S(1)}, f32[8,16,128]{2,1,0:T(8,128)S(1)}, u32[]{:S(2)}, u32[]{:S(2)}) collective-permute-start(f32[8,16,128]{2,1,0:T(8,128)S(1)} %collective-permute-done.13.p1), channel_id=1, source_target_pairs={{0,1},{1,0},{2,3},{3,2},{4,5},{5,4},{6,7},{7,6},{8,9},{9,8},{10,11... | collective-permute-start | bytes 196616 | tf_op jit(solution)/shard_map/ppermute | solution.py:305
  109.6 2.1 %collective-permute-start.15 = (f32[4,16,128]{2,1,0:T(8,128)S(1)}, f32[4,16,128]{2,1,0:T(8,128)S(1)}, u32[]{:S(2)}, u32[]{:S(2)}) collective-permute-start(f32[4,16,128]{2,1,0:T(8,128)S(1)} %get-tuple-element.22.v.smooth), channel_id=1, source_target_pairs={{1,4},{3,6},{4,1},{5,8},{6,3},{7,10},{8,5},{9,12},{10,7},{11,14},{... | collective-permute-start | bytes 98312 | tf_op jit(solution)/shard_map/ppermute | solution.py:305
  111.7 4.0 %collective-permute-done.15.p3 = f32[4,16,128]{2,1,0:T(8,128)S(1)} collective-permute-done((f32[4,16,128]{2,1,0:T(8,128)S(1)}, f32[4,16,128]{2,1,0:T(8,128)S(1)}, u32[]{:S(2)}, u32[]{:S(2)}) %collective-permute-start.15) | collective-permute-done | bytes 32800 | tf_op jit(solution)/shard_map/ppermute | solution.py:305
  115.8 0.0 collective-permute-done.14.p2
  115.8 6.6 %shard_map.81 = (f32[4,16,128]{2,1,0:T(8,128)S(1)}, f32[32,16,128]{2,1,0:T(8,128)S(1)}) custom-call(s32[4,32]{1,0:T(4,128)S(1)} %fusion.1.index_ref, f32[4,7]{1,0:T(4,128)S(1)} %add_convert_fusion.flags_ref, f32[4,32,128,128]{3,2,1,0:T(8,128)S(1)} %copy-done, f32[4,16,128]{2,1,0:T(8,128)S(1)} %get-tuple-element.19.target, ...), custom_call_target="tpu_custom_call" | custom-call | tf_op jit(solution)/shard_map/pallas_call | solution.py:191
  122.3 13.6 %all_to_all.11.gathered = f32[32,16,128]{2,1,0:T(8,128)S(1)} all-to-all(f32[32,16,128]{2,1,0:T(8,128)S(1)} %get-tuple-element.23), channel_id=1, replica_groups=mesh['grp'=4,'row'=8] {'grp','row'}, dimensions={0} | all-to-all | bytes 524288 | tf_op jit(solution)/shard_map/all_to_all | solution.py:323
  136.0 0.0 copy-done.3
  136.0 5.6 %shard_map.82 = (f32[4,16,128]{2,1,0:T(8,128)}, f32[4,16,128]{2,1,0:T(8,128)}) custom-call(f32[4,7]{1,0:T(4,128)S(1)} %add_convert_fusion.flags_ref, f32[32,16,128]{2,1,0:T(8,128)S(1)} %all_to_all.11.gathered, f32[4,16,128]{2,1,0:T(8,128)S(1)} %copy-done.3, f32[4,16,128]{2,1,0:T(8,128)S(1)} %get-tuple-element.24.solution, ...), custom_call_target="tpu_custom_call" | custom-call | tf_op jit(solution)/shard_map/pallas_call | solution.py:294
  (4 shorter events, 0.0 us)
Async XLA Ops:
  0.6 17.7 %collective-permute-start.3 = (f32[4,16,128]{2,1,0:T(8,128)}, f32[4,16,128]{2,1,0:T(8,128)S(1)}, u32[]{:S(2)}, u32[]{:S(2)}) collective-permute-start(f32[4,16,128]{2,1,0:T(8,128)} %right.5), channel_id=1, source_target_pairs={{1,4},{3,6},{4,1},{5,8},{6,3},{7,10},{8,5},{9,12},{10,7},{11,14},{... | collective-permute-start | bytes 98312 | tf_op jit(solution)/shard_map/ppermute | solution.py:305
  5.4 2.8 %collective-permute-start = (f32[4,16,128]{2,1,0:T(8,128)}, f32[4,16,128]{2,1,0:T(8,128)S(1)}, u32[]{:S(2)}, u32[]{:S(2)}) collective-permute-start(f32[4,16,128]{2,1,0:T(8,128)} %right.5), channel_id=1, source_target_pairs={{0,1},{1,0},{2,3},{3,2},{4,5},{5,4},{6,7},{7,6},{8,9},{9,8},{10,11... | collective-permute-start | bytes 98312 | tf_op jit(solution)/shard_map/ppermute | solution.py:305
  9.0 5.6 %collective-permute-start.1 = (f32[8,16,128]{2,1,0:T(8,128)S(1)}, f32[8,16,128]{2,1,0:T(8,128)S(1)}, u32[]{:S(2)}, u32[]{:S(2)}) collective-permute-start(f32[8,16,128]{2,1,0:T(8,128)S(1)} %pad_maximum_fusion), channel_id=1, source_target_pairs={{1,2},{2,1},{3,4},{4,3},{5,6},{6,5},{7,8},{8,7},{9,10},{10,9},{11,... | collective-permute-start | bytes 196616 | tf_op jit(solution)/shard_map/ppermute | solution.py:305
  14.6 4.5 %collective-permute-start.2 = (f32[8,16,128]{2,1,0:T(8,128)S(1)}, f32[8,16,128]{2,1,0:T(8,128)S(1)}, u32[]{:S(2)}, u32[]{:S(2)}) collective-permute-start(f32[8,16,128]{2,1,0:T(8,128)S(1)} %collective-permute-done.1.p1), channel_id=1, source_target_pairs={{0,1},{1,0},{2,3},{3,2},{4,5},{5,4},{6,7},{7,6},{8,9},{9,8},{10,11... | collective-permute-start | bytes 196616 | tf_op jit(solution)/shard_map/ppermute | solution.py:305
  19.1 3.4 %copy-start = (f32[4,32,128,128]{3,2,1,0:T(8,128)S(1)}, f32[4,32,128,128]{3,2,1,0:T(8,128)}, u32[]{:S(2)}) copy-start(f32[4,32,128,128]{3,2,1,0:T(8,128)} %tiles_hbm.7) | copy-start | bytes 25165828
  22.5 0.8 copy-start.2
  23.3 44.3 %copy-start.1 = (f32[4,128,128]{2,1,0:T(8,128)S(1)}, f32[4,128,128]{2,1,0:T(8,128)}, u32[]{:S(2)}) copy-start(f32[4,128,128]{2,1,0:T(8,128)} %precond.3) | copy-start | bytes 786436
  29.8 1.3 collective-permute-start.4
  31.0 5.6 %collective-permute-start.5 = (f32[8,16,128]{2,1,0:T(8,128)S(1)}, f32[8,16,128]{2,1,0:T(8,128)S(1)}, u32[]{:S(2)}, u32[]{:S(2)}) collective-permute-start(f32[8,16,128]{2,1,0:T(8,128)S(1)} %pad_maximum_fusion.1), channel_id=1, source_target_pairs={{1,2},{2,1},{3,4},{4,3},{5,6},{6,5},{7,8},{8,7},{9,10},{10,9},{11,... | collective-permute-start | bytes 196616 | tf_op jit(solution)/shard_map/ppermute | solution.py:305
  36.6 10.1 %collective-permute-start.6 = (f32[8,16,128]{2,1,0:T(8,128)S(1)}, f32[8,16,128]{2,1,0:T(8,128)S(1)}, u32[]{:S(2)}, u32[]{:S(2)}) collective-permute-start(f32[8,16,128]{2,1,0:T(8,128)S(1)} %collective-permute-done.5.p1), channel_id=1, source_target_pairs={{0,1},{1,0},{2,3},{3,2},{4,5},{5,4},{6,7},{7,6},{8,9},{9,8},{10,11... | collective-permute-start | bytes 196616 | tf_op jit(solution)/shard_map/ppermute | solution.py:305
  40.6 6.1 %collective-permute-start.7 = (f32[4,16,128]{2,1,0:T(8,128)S(1)}, f32[4,16,128]{2,1,0:T(8,128)S(1)}, u32[]{:S(2)}, u32[]{:S(2)}) collective-permute-start(f32[4,16,128]{2,1,0:T(8,128)S(1)} %get-tuple-element.15.v.image), channel_id=1, source_target_pairs={{1,4},{3,6},{4,1},{5,8},{6,3},{7,10},{8,5},{9,12},{10,7},{11,14},{... | collective-permute-start | bytes 98312 | tf_op jit(solution)/shard_map/ppermute | solution.py:305
  73.0 1.2 collective-permute-start.8
  74.2 61.7 %copy-start.3 = (f32[4,16,128]{2,1,0:T(8,128)S(1)}, f32[4,16,128]{2,1,0:T(8,128)}, u32[]{:S(2)}) copy-start(f32[4,16,128]{2,1,0:T(8,128)} %right.5) | copy-start | bytes 98308
  74.2 5.6 %collective-permute-start.9 = (f32[8,16,128]{2,1,0:T(8,128)S(1)}, f32[8,16,128]{2,1,0:T(8,128)S(1)}, u32[]{:S(2)}, u32[]{:S(2)}) collective-permute-start(f32[8,16,128]{2,1,0:T(8,128)S(1)} %pad_maximum_fusion.2), channel_id=1, source_target_pairs={{1,2},{2,1},{3,4},{4,3},{5,6},{6,5},{7,8},{8,7},{9,10},{10,9},{11,... | collective-permute-start | bytes 196616 | tf_op jit(solution)/shard_map/ppermute | solution.py:305
  79.8 10.0 %collective-permute-start.10 = (f32[8,16,128]{2,1,0:T(8,128)S(1)}, f32[8,16,128]{2,1,0:T(8,128)S(1)}, u32[]{:S(2)}, u32[]{:S(2)}) collective-permute-start(f32[8,16,128]{2,1,0:T(8,128)S(1)} %collective-permute-done.9.p1), channel_id=1, source_target_pairs={{0,1},{1,0},{2,3},{3,2},{4,5},{5,4},{6,7},{7,6},{8,9},{9,8},{10,11... | collective-permute-start | bytes 196616 | tf_op jit(solution)/shard_map/ppermute | solution.py:305
  83.7 6.1 %collective-permute-start.11 = (f32[4,16,128]{2,1,0:T(8,128)S(1)}, f32[4,16,128]{2,1,0:T(8,128)S(1)}, u32[]{:S(2)}, u32[]{:S(2)}) collective-permute-start(f32[4,16,128]{2,1,0:T(8,128)S(1)} %get-tuple-element.20.v.head), channel_id=1, source_target_pairs={{1,4},{3,6},{4,1},{5,8},{6,3},{7,10},{8,5},{9,12},{10,7},{11,14},{... | collective-permute-start | bytes 98312 | tf_op jit(solution)/shard_map/ppermute | solution.py:305
  97.4 2.7 %collective-permute-start.12 = (f32[4,16,128]{2,1,0:T(8,128)S(1)}, f32[4,16,128]{2,1,0:T(8,128)S(1)}, u32[]{:S(2)}, u32[]{:S(2)}) collective-permute-start(f32[4,16,128]{2,1,0:T(8,128)S(1)} %get-tuple-element.22.v.smooth), channel_id=1, source_target_pairs={{0,1},{1,0},{2,3},{3,2},{4,5},{5,4},{6,7},{7,6},{8,9},{9,8},{10,11... | collective-permute-start | bytes 98312 | tf_op jit(solution)/shard_map/ppermute | solution.py:305
  100.1 5.9 %collective-permute-start.13 = (f32[8,16,128]{2,1,0:T(8,128)S(1)}, f32[8,16,128]{2,1,0:T(8,128)S(1)}, u32[]{:S(2)}, u32[]{:S(2)}) collective-permute-start(f32[8,16,128]{2,1,0:T(8,128)S(1)} %pad_maximum_fusion.3), channel_id=1, source_target_pairs={{1,2},{2,1},{3,4},{4,3},{5,6},{6,5},{7,8},{8,7},{9,10},{10,9},{11,... | collective-permute-start | bytes 196616 | tf_op jit(solution)/shard_map/ppermute | solution.py:305
  106.0 9.7 %collective-permute-start.14 = (f32[8,16,128]{2,1,0:T(8,128)S(1)}, f32[8,16,128]{2,1,0:T(8,128)S(1)}, u32[]{:S(2)}, u32[]{:S(2)}) collective-permute-start(f32[8,16,128]{2,1,0:T(8,128)S(1)} %collective-permute-done.13.p1), channel_id=1, source_target_pairs={{0,1},{1,0},{2,3},{3,2},{4,5},{5,4},{6,7},{7,6},{8,9},{9,8},{10,11... | collective-permute-start | bytes 196616 | tf_op jit(solution)/shard_map/ppermute | solution.py:305
  109.6 6.1 %collective-permute-start.15 = (f32[4,16,128]{2,1,0:T(8,128)S(1)}, f32[4,16,128]{2,1,0:T(8,128)S(1)}, u32[]{:S(2)}, u32[]{:S(2)}) collective-permute-start(f32[4,16,128]{2,1,0:T(8,128)S(1)} %get-tuple-element.22.v.smooth), channel_id=1, source_target_pairs={{1,4},{3,6},{4,1},{5,8},{6,3},{7,10},{8,5},{9,12},{10,7},{11,14},{... | collective-permute-start | bytes 98312 | tf_op jit(solution)/shard_map/ppermute | solution.py:305

commit v2 on v1

--- a/solution.py
+++ b/solution.py
@@ -4,6 +4,7 @@
 from jax.experimental import pallas as pl
 from jax.experimental.pallas import tpu as pltpu
 from jax.sharding import PartitionSpec as P
+
 
 BAND = 12
 SLOTS = 7
@@ -60,24 +61,16 @@
             slot += 1
 
 
-def row_product(index_ref, table_ref, tile_ref, row, classes, cols):
-    count, tb = tile_ref.shape[1], tile_ref.shape[2]
+def row_product(index_ref, table_ref, split_ref, row, classes, cols):
+    pairs, tb = split_ref.shape[1], split_ref.shape[2] // 2
     total = None
-    for k in range(0, count, 2):
+    for pair in range(pairs):
         left = jnp.concatenate(
-            [table_ref[index_ref[row, k]], table_ref[index_ref[row, k + 1]]], axis=1
-        )
-        highs, rests = [], []
-        for j in (k, k + 1):
-            tile = tile_ref[row, j]
-            high = tile.astype(jnp.bfloat16)
-            highs.append(high)
-            rests.append((tile - high.astype(jnp.float32)).astype(jnp.bfloat16))
-        right = jnp.concatenate(
-            [jnp.concatenate(highs, axis=1), jnp.concatenate(rests, axis=1)], axis=0
+            [table_ref[index_ref[row, 2 * pair]], table_ref[index_ref[row, 2 * pair + 1]]], axis=1
         )
         part = lax.dot_general(
-            left, right, (((1,), (1,)), ((), ())), preferred_element_type=jnp.float32
+            left, split_ref[row, pair], (((1,), (1,)), ((), ())),
+            preferred_element_type=jnp.float32,
         )
         total = part if total is None else total + part
     total = total[:, :tb] + total[:, tb:]
@@ -92,53 +85,99 @@
     return out
 
 
-def stream(tiles_hbm, tiles, sems):
+def split_kernel(tiles_hbm, split, tiles, sems):
+    blocks, count, tb, _ = tiles.shape
     copies = [
         pltpu.make_async_copy(tiles_hbm.at[row], tiles.at[row], sems.at[row])
-        for row in range(tiles.shape[0])
+        for row in range(blocks)
     ]
     for copy in copies:
         copy.start()
-    return copies
+    for row in range(blocks):
+        copies[row].wait()
+        for k in range(count):
+            tile = tiles[row, k]
+            high = tile.astype(jnp.bfloat16)
+            rest = (tile - high.astype(jnp.float32)).astype(jnp.bfloat16)
+            side = (k % 2) * tb
+            split[row, k // 2, 0:tb, side : side + tb] = high
+            split[row, k // 2, tb : 2 * tb, side : side + tb] = rest
+
+
+def split_call(tiles):
+    blocks, count, tb, _ = tiles.shape
+    return pl.pallas_call(
+        split_kernel,
+        out_shape=jax.ShapeDtypeStruct((blocks, count // 2, 2 * tb, 2 * tb), jnp.bfloat16),
+        in_specs=[spec(pltpu.HBM)],
+        out_specs=spec(VMEM),
+        scratch_shapes=[VMEM(tiles.shape, jnp.float32), pltpu.SemaphoreType.DMA((blocks,))],
+        compiler_params=params(24),
+        cost_estimate=pl.CostEstimate(flops=0, bytes_accessed=12 * tiles.size // 2, transcendentals=0),
+    )(pltpu.with_memory_space_constraint(tiles, pltpu.HBM))
 
 
 def lanes(ref):
     return jnp.concatenate([ref[i] for i in range(ref.shape[0])], axis=1)
+
+
+def grid16(cols):
+    rows = lax.broadcasted_iota(jnp.int32, (cols, cols), 0)
+    columns = lax.broadcasted_iota(jnp.int32, (cols, cols), 1)
+    return rows, columns
 
 
 def pack_gram(gram_ref, former, latter, scale, cols):
     gram = dot_nt(former, latter)
     if scale is not None:
         gram = gram * scale
-    width = gram.shape[1]
-    packed = jnp.concatenate(
-        [gram[:cols], gram[cols:], jnp.zeros((cols, gram_ref.shape[2] - 2 * width), jnp.float32)],
-        axis=1,
-    )
+    g00, g01, g02 = (gram[:cols, k * cols : (k + 1) * cols] for k in range(3))
+    g11, g12 = (gram[cols:, k * cols : (k + 1) * cols] for k in (1, 2))
+    rows, columns = grid16(cols)
+    upper = rows <= columns
+    first = jnp.where(upper, g00, g11)
+    middle = jnp.sum(jnp.where(rows == columns, g11, 0.0), axis=1, keepdims=True)
+    last = jnp.where(rows == columns + 1, middle, 0.0)
+    last = jnp.where((rows == cols - 1) & (columns == 0), g11[0:1, 0:1], last)
+    last = jnp.where(upper, 0.5 * (g12 + g12.T), last)
+    flat = jnp.concatenate([first, g01, g02, last], axis=1)
+    half = cols // 2
+    packed = jnp.concatenate([flat[:half], flat[half:]], axis=1)
     gram_ref[...] = jnp.broadcast_to(packed[None], gram_ref.shape)
 
 
-def first_kernel(index_ref, flags_ref, tiles_hbm, v, sw, p1, p2, p3, parts, image, tiles, table, sems):
+def unpack_gram(packed, cols):
+    width = packed.shape[1] // 2
+    flat = jnp.concatenate([packed[:, :width], packed[:, width:]], axis=0)
+    first, g01, g02, last = (flat[:, k * cols : (k + 1) * cols] for k in range(4))
+    rows, columns = grid16(cols)
+    above, below, diagonal = rows < columns, rows > columns, rows == columns
+    g00 = jnp.where(rows <= columns, first, 0.0) + jnp.where(above, first, 0.0).T
+    middle = jnp.sum(jnp.where(rows == columns + 1, last, 0.0), axis=1, keepdims=True)
+    middle = jnp.where(rows == 0, last[cols - 1 : cols, 0:1], middle)
+    lower = jnp.where(below, first, 0.0)
+    g11 = lower + lower.T + jnp.where(diagonal, middle, 0.0)
+    g12 = jnp.where(rows <= columns, last, 0.0) + jnp.where(above, last, 0.0).T
+    return g00, g01, g02, g11, g12
+
+
+def first_kernel(index_ref, flags_ref, split, v, sw, p1, p2, p3, parts, image, table):
     blocks, cols, _ = v.shape
-    copies = stream(tiles_hbm, tiles, sems)
     build_table((v, sw, p1, p2, p3), flags_ref, table, 3, blocks, cols)
     for row in range(blocks):
-        copies[row].wait()
-        out = row_product(index_ref, table, tiles, row, 3, cols)
+        out = row_product(index_ref, table, split, row, 3, cols)
         for k in range(3):
             parts[k, row] = out[k]
         image[row] = out[0] + out[1] + out[2]
 
 
 def second_kernel(
-    index_ref, flags_ref, tiles_hbm, right, v, sw, p1, p2, p3, parts, gram, tiles, table, sems, image
+    index_ref, flags_ref, split, right, v, sw, p1, p2, p3, parts, gram, table, image
 ):
     blocks, cols, _ = v.shape
-    copies = stream(tiles_hbm, tiles, sems)
     build_table((v, sw, p1, p2, p3), flags_ref, table, 3, blocks, cols)
     for row in range(blocks):
-        copies[row].wait()
-        out = row_product(index_ref, table, tiles, row, 3, cols)
+        out = row_product(index_ref, table, split, row, 3, cols)
         for k in range(3):
             parts[k, row] = out[k]
         image[row] = out[0] + out[1] + out[2]
@@ -148,31 +187,27 @@
 
 
 def third_kernel(
-    index_ref, flags_ref, tiles_hbm, precond, v, sw, p1, p2, p3, applied, smooth, lost, tiles, table, sems
+    index_ref, flags_ref, split, precond, v, sw, p1, p2, p3, applied, smooth, lost, table
 ):
     blocks, cols, _ = v.shape
-    copies = stream(tiles_hbm, tiles, sems)
     build_table((v, sw, p1, p2, p3), flags_ref, table, 2, blocks, cols)
     mine = flags_ref[3, 0]
     for row in range(blocks):
-        copies[row].wait()
-        out = row_product(index_ref, table, tiles, row, 2, cols)
+        out = row_product(index_ref, table, split, row, 2, cols)
         applied[row] = out[0]
         lost[row] = out[0] * mine + out[1]
         smooth[row] = dot_nt(out[0], precond[row])
 
 
 def fourth_kernel(
-    index_ref, flags_ref, tiles_hbm, target, head, applied, v, sw, p1, p2, p3, lost, gram,
-    tiles, table, sems, second,
+    index_ref, flags_ref, split, target, head, applied, v, sw, p1, p2, p3, lost, gram,
+    table, second,
 ):
     blocks, cols, _ = v.shape
-    copies = stream(tiles_hbm, tiles, sems)
     build_table((v, sw, p1, p2, p3), flags_ref, table, 2, blocks, cols)
     mine = flags_ref[3, 0]
     for row in range(blocks):
-        copies[row].wait()
-        out = row_product(index_ref, table, tiles, row, 2, cols)
+        out = row_product(index_ref, table, split, row, 2, cols)
         second[row] = out[0]
         lost[row] = out[0] * mine + out[1]
     former = jnp.concatenate([lanes(head), lanes(v)], axis=0)
@@ -180,22 +215,17 @@
     pack_gram(gram, former, latter, mine, cols)
 
 
-def tile_call(kernel, classes, outs, extra, tiles, operands_vmem, index, flags):
-    blocks, count, tb, _ = tiles.shape
-    cols = operands_vmem[-1].shape[1]
-    scratch = [
-        VMEM((blocks, count, tb, tb), jnp.float32),
-        VMEM((SLOTS * blocks, 3 * classes * cols, tb), jnp.bfloat16),
-        pltpu.SemaphoreType.DMA((blocks,)),
-    ] + extra
+def tile_call(kernel, classes, outs, extra, split, operands_vmem, index, flags):
+    blocks, cols, tb = operands_vmem[-1].shape
+    scratch = [VMEM((SLOTS * blocks, 3 * classes * cols, tb), jnp.bfloat16)] + extra
     return pl.pallas_call(
         kernel,
         out_shape=outs,
-        in_specs=[spec(SMEM), spec(SMEM), spec(pl.ANY)] + [spec(VMEM)] * len(operands_vmem),
+        in_specs=[spec(SMEM), spec(SMEM)] + [spec(VMEM)] * (1 + len(operands_vmem)),
         out_specs=[spec(VMEM)] * len(outs),
         scratch_shapes=scratch,
-        compiler_params=params(32),
-    )(index, flags, tiles, *operands_vmem)
+        compiler_params=params(16),
+    )(index, flags, split, *operands_vmem)
 
 
 def eliminate(matrix, target):
@@ -210,17 +240,12 @@
 
 
 def coefficients(gathered, cols):
-    packed = jnp.sum(gathered[...], axis=0)
-    width = 3 * cols
-    top, bottom = packed[:, :width], packed[:, width : 2 * width]
-    g00, g01 = top[:, :cols], top[:, cols : 2 * cols]
-    g11 = bottom[:, cols : 2 * cols]
-    big = jnp.concatenate([top[:, cols:], bottom[:, cols:]], axis=0)
-    unit = (
-        lax.broadcasted_iota(jnp.int32, (cols, cols), 0)
-        == lax.broadcasted_iota(jnp.int32, (cols, cols), 1)
-    ).astype(jnp.float32)
-    g00 = 0.5 * (g00 + g00.T)
+    g00, g01, g02, g11, g12 = unpack_gram(jnp.sum(gathered[...], axis=0), cols)
+    big = jnp.concatenate(
+        [jnp.concatenate([g01, g02], axis=1), jnp.concatenate([g11, g12], axis=1)], axis=0
+    )
+    rows, columns = grid16(cols)
+    unit = (rows == columns).astype(jnp.float32)
     advance = eliminate(0.5 * (g01 + g01.T), g00)
     inverse = eliminate(g00, unit)
     crossed = dot_nn(g01, advance)
@@ -307,9 +332,9 @@
 
 def window(value, total):
     swapped = move(value, total, lambda i: i ^ 1)
-    far = move(value, total, lambda i: i - 3 if i % 2 == 0 else i + 3)
     pair = jnp.concatenate([value, swapped], axis=0)
     near = move(pair, total, lambda i: i - 1 if i % 2 == 0 else i + 1)
+    far = move(value, total, lambda i: i - 3 if i % 2 == 0 else i + 3)
     other = move(near, total, lambda i: i ^ 1)
     return value, swapped, near, other, far
 
@@ -355,24 +380,26 @@
 
     vec = jax.ShapeDtypeStruct(right_side.shape, jnp.float32)
     vec3 = jax.ShapeDtypeStruct((3,) + right_side.shape, jnp.float32)
-    gram = jax.ShapeDtypeStruct((total, cols, tb), jnp.float32)
+    gram = jax.ShapeDtypeStruct((total, cols // 2, 8 * cols), jnp.float32)
+    assert tb == 8 * cols
     held = VMEM(right_side.shape, jnp.float32)
 
+    split = split_call(matrix_tiles)
     parts_b, image = tile_call(
-        first_kernel, 3, [vec3, vec], [], matrix_tiles, window(right_side, total), index, flags
+        first_kernel, 3, [vec3, vec], [], split, window(right_side, total), index, flags
     )
     parts_y, gram_outer = tile_call(
-        second_kernel, 3, [vec3, gram], [held], matrix_tiles,
+        second_kernel, 3, [vec3, gram], [held], split,
         (right_side,) + window(image, total), index, flags,
     )
     solution, target, head, kept = small_call(
         outer_kernel, [vec] * 4, flags, exchange(gram_outer), right_side, image, parts_b, parts_y, precond
     )
     applied, smooth, lost0 = tile_call(
-        third_kernel, 2, [vec] * 3, [], matrix_tiles, (precond,) + window(head, total), index, flags
+        third_kernel, 2, [vec] * 3, [], split, (precond,) + window(head, total), index, flags
     )
     lost1, gram_inner = tile_call(
-        fourth_kernel, 2, [vec, gram], [held], matrix_tiles,
+        fourth_kernel, 2, [vec, gram], [held], split,
         (target, head, applied) + window(smooth, total), index, flags,
     )
     recovered, residual = small_call(
@@ -391,6 +418,7 @@
         P(),
     )
     out_specs = (P(("grp", "row"), None, None), P(("grp", "row"), None, None))
+
     return jax.shard_map(
         per_device, mesh=mesh, in_specs=in_specs, out_specs=out_specs, check_vma=False
     )

time: 144 us -> 128 us (0.89)
  blocking collectives: 27.8 us -> 22.2 us
  Pallas kernels: 38.4 us -> 33.2 us
  local copies, waits for them, and re-layouts: 4.22 us -> 0.09 us
    all_to_all x2, blocking collectives: 27.8 us -> 22.2 us  [exchange(): return lax.all_to_all(gram, AXES, 0, 0)]
    pallas_call x4 -> x5, Pallas kernels: 27.3 us -> 21.9 us  [the longest x4 18.1 us: tile_call(): pl.pallas_call(kernel, out_shape=outs, in_specs=[spec(SMEM), spec(SMEM)]...]
    unnamed x8 -> x4, local copies, waits for them, and re-layouts: 4.15 us -> 0.01 us
  transfers between devices with their start and end apart: 16 -> 16, of which waited for: 11 -> 10; matrix products, arithmetic and copies ran while one was open for 2% -> 2% of each run, Pallas kernels for 0% -> 3%
where the time goes in v2:
time: 128 us; the launch traced here: 126 us
  starting transfers between devices  37.5 us (29%)
  Pallas kernels  33.2 us (26%)
  waiting for transfers between devices  29.2 us (23%)
  blocking collectives  22.2 us (17%)
  other arithmetic  2.24 us (2%)
  between operations  1.46 us (1%)
    ppermute x16, starting transfers between devices, move(): return lax.ppermute(value, AXES, pairs)  37.5 us
    ppermute x16, waiting for transfers between devices, move(): return lax.ppermute(value, AXES, pairs)  29.2 us
    all_to_all x2, blocking collectives, exchange(): return lax.all_to_all(gram, AXES, 0, 0)  22.2 us
    pallas_call x4, Pallas kernels, tile_call(): pl.pallas_call(kernel, out_shape=outs, in_specs=[spec(SMEM), spec(SMEM)]...  18.1 us
    pallas_call x2, Pallas kernels, small_call(): pl.pallas_call(kernel, out_shape=outs, in_specs=[spec(SMEM)] + [spec(VMEM...  11.3 us
    pallas_call x1, Pallas kernels, split_call(): pl.pallas_call(split_kernel, out_shape=jax.ShapeDtypeStruct((blocks, coun...  3.85 us
  transfers between devices with their start and end apart: 16, of which 10 were waited for; matrix products, arithmetic and copies ran while one was open for 2% of the time, Pallas kernels for 3%

profile of v2, /device:TPU:5, one launch (start us, length us, event | category | flops | bytes accessed | tf_op | source)
XLA Modules:
  0.0 125.9 jit_solution(5008528571291465313)
XLA Ops:
  0.6 4.8 %collective-permute-start.3 = (f32[4,16,128]{2,1,0:T(8,128)}, f32[4,16,128]{2,1,0:T(8,128)S(1)}, u32[]{:S(2)}, u32[]{:S(2)}) collective-permute-start(f32[4,16,128]{2,1,0:T(8,128)} %right.5), channel_id=1, source_target_pairs={{1,4},{3,6},{4,1},{5,8},{6,3},{7,10},{8,5},{9,12},{10,7},{11,14},{... | collective-permute-start | bytes 98312 | tf_op jit(solution)/shard_map/ppermute | solution.py:330
  5.4 0.8 collective-permute-start
  6.2 0.7 fusion.1.index_ref
  6.9 0.7 fusion.4
  8.2 0.0 collective-permute-done.sw
  8.2 0.8 pad_maximum_fusion
  9.0 3.1 %collective-permute-start.1 = (f32[8,16,128]{2,1,0:T(8,128)S(1)}, f32[8,16,128]{2,1,0:T(8,128)S(1)}, u32[]{:S(2)}, u32[]{:S(2)}) collective-permute-start(f32[8,16,128]{2,1,0:T(8,128)S(1)} %pad_maximum_fusion), channel_id=1, source_target_pairs={{1,2},{2,1},{3,4},{4,3},{5,6},{6,5},{7,8},{8,7},{9,10},{10,9},{11,... | collective-permute-start | bytes 196616 | tf_op jit(solution)/shard_map/ppermute | solution.py:330
  12.2 0.1 pad.11.clone
  12.2 2.4 %collective-permute-done.1.p1 = f32[8,16,128]{2,1,0:T(8,128)S(1)} collective-permute-done((f32[8,16,128]{2,1,0:T(8,128)S(1)}, f32[8,16,128]{2,1,0:T(8,128)S(1)}, u32[]{:S(2)}, u32[]{:S(2)}) %collective-permute-start.1) | collective-permute-done | bytes 65568 | tf_op jit(solution)/shard_map/ppermute | solution.py:330
  14.6 3.6 %collective-permute-start.2 = (f32[8,16,128]{2,1,0:T(8,128)S(1)}, f32[8,16,128]{2,1,0:T(8,128)S(1)}, u32[]{:S(2)}, u32[]{:S(2)}) collective-permute-start(f32[8,16,128]{2,1,0:T(8,128)S(1)} %collective-permute-done.1.p1), channel_id=1, source_target_pairs={{0,1},{1,0},{2,3},{3,2},{4,5},{5,4},{6,7},{7,6},{8,9},{9,8},{10,11... | collective-permute-start | bytes 196616 | tf_op jit(solution)/shard_map/ppermute | solution.py:330
  18.2 0.1 add_convert_fusion.flags_ref
  18.3 0.0 copy-start.1
  18.3 3.8 %shard_map.77.split = bf16[4,16,256,256]{3,2,1,0:T(8,128)(2,1)S(1)} custom-call(f32[4,32,128,128]{3,2,1,0:T(8,128)} %tiles_hbm.1), custom_call_target="tpu_custom_call" | custom-call | bytes 12582912 | tf_op jit(solution)/shard_map/pallas_call | solution.py:109
  22.1 0.0 copy-start
  22.2 0.0 collective-permute-done.3.p3
  22.2 0.0 collective-permute-done.2.p2
  22.2 0.0 copy-done.1
  22.2 3.6 %shard_map.78 = (f32[3,4,16,128]{3,2,1,0:T(8,128)S(1)}, f32[4,16,128]{2,1,0:T(8,128)S(1)}) custom-call(s32[4,32]{1,0:T(4,128)S(1)} %fusion.1.index_ref, f32[4,7]{1,0:T(4,128)S(1)} %add_convert_fusion.flags_ref, bf16[4,16,256,256]{3,2,1,0:T(8,128)(2,1)S(1)} %shard_map.77.split, f32[4,16,128]{2,1,0:T(8,128)S(1)} %copy-done.1, ...), custom_call_target="tpu_custom_call" | custom-call | tf_op jit(solution)/shard_map/pallas_call | solution.py:221
  25.7 0.1 collective-permute-start.4
  25.8 1.2 collective-permute-done.4.sw
  27.0 1.9 %collective-permute-start.5 = (f32[8,16,128]{2,1,0:T(8,128)S(1)}, f32[8,16,128]{2,1,0:T(8,128)S(1)}, u32[]{:S(2)}, u32[]{:S(2)}) collective-permute-start(f32[8,16,128]{2,1,0:T(8,128)S(1)} %pad_maximum_fusion.1), channel_id=1, source_target_pairs={{1,2},{2,1},{3,4},{4,3},{5,6},{6,5},{7,8},{8,7},{9,10},{10,9},{11,... | collective-permute-start | bytes 196616 | tf_op jit(solution)/shard_map/ppermute | solution.py:330
  28.9 3.7 %collective-permute-done.5.p1 = f32[8,16,128]{2,1,0:T(8,128)S(1)} collective-permute-done((f32[8,16,128]{2,1,0:T(8,128)S(1)}, f32[8,16,128]{2,1,0:T(8,128)S(1)}, u32[]{:S(2)}, u32[]{:S(2)}) %collective-permute-start.5) | collective-permute-done | bytes 65568 | tf_op jit(solution)/shard_map/ppermute | solution.py:330
  32.6 3.8 %collective-permute-start.6 = (f32[8,16,128]{2,1,0:T(8,128)S(1)}, f32[8,16,128]{2,1,0:T(8,128)S(1)}, u32[]{:S(2)}, u32[]{:S(2)}) collective-permute-start(f32[8,16,128]{2,1,0:T(8,128)S(1)} %collective-permute-done.5.p1), channel_id=1, source_target_pairs={{0,1},{1,0},{2,3},{3,2},{4,5},{5,4},{6,7},{7,6},{8,9},{9,8},{10,11... | collective-permute-start | bytes 196616 | tf_op jit(solution)/shard_map/ppermute | solution.py:330
  36.4 1.9 %collective-permute-start.7 = (f32[4,16,128]{2,1,0:T(8,128)S(1)}, f32[4,16,128]{2,1,0:T(8,128)S(1)}, u32[]{:S(2)}, u32[]{:S(2)}) collective-permute-start(f32[4,16,128]{2,1,0:T(8,128)S(1)} %get-tuple-element.15.v.image), channel_id=1, source_target_pairs={{1,4},{3,6},{4,1},{5,8},{6,3},{7,10},{8,5},{9,12},{10,7},{11,14},{... | collective-permute-start | bytes 98312 | tf_op jit(solution)/shard_map/ppermute | solution.py:330
  38.3 4.2 %collective-permute-done.7.p3 = f32[4,16,128]{2,1,0:T(8,128)S(1)} collective-permute-done((f32[4,16,128]{2,1,0:T(8,128)S(1)}, f32[4,16,128]{2,1,0:T(8,128)S(1)}, u32[]{:S(2)}, u32[]{:S(2)}) %collective-permute-start.7) | collective-permute-done | bytes 32800 | tf_op jit(solution)/shard_map/ppermute | solution.py:330
  42.5 0.0 collective-permute-done.6.p2
  42.5 4.2 %shard_map.79 = (f32[3,4,16,128]{3,2,1,0:T(8,128)S(1)}, f32[32,8,128]{2,1,0:T(8,128)S(1)}) custom-call(s32[4,32]{1,0:T(4,128)S(1)} %fusion.1.index_ref, f32[4,7]{1,0:T(4,128)S(1)} %add_convert_fusion.flags_ref, bf16[4,16,256,256]{3,2,1,0:T(8,128)(2,1)S(1)} %shard_map.77.split, f32[4,16,128]{2,1,0:T(8,128)S(1)} %copy-done.1, ...), custom_call_target="tpu_custom_call" | custom-call | tf_op jit(solution)/shard_map/pallas_call | solution.py:221
  46.7 11.5 %all_to_all.10.gathered = f32[32,8,128]{2,1,0:T(8,128)S(1)} all-to-all(f32[32,8,128]{2,1,0:T(8,128)S(1)} %get-tuple-element.16), channel_id=1, replica_groups=mesh['grp'=4,'row'=8] {'grp','row'}, dimensions={0} | all-to-all | bytes 262144 | tf_op jit(solution)/shard_map/all_to_all | solution.py:348
  58.2 0.0 copy-done
  58.2 5.6 %shard_map.80 = (f32[4,16,128]{2,1,0:T(8,128)S(1)}, f32[4,16,128]{2,1,0:T(8,128)S(1)}, f32[4,16,128]{2,1,0:T(8,128)S(1)}, f32[4,16,128]{2,1,0:T(8,128)S(1)}) custom-call(f32[4,7]{1,0:T(4,128)S(1)} %add_convert_fusion.flags_ref, f32[32,8,128]{2,1,0:T(8,128)S(1)} %all_to_all.10.gathered, f32[4,16,128]{2,1,0:T(8,128)S(1)} %copy-done.1, ...), custom_call_target="tpu_custom_call" | custom-call | tf_op jit(solution)/shard_map/pallas_call | solution.py:319
  63.8 0.5 collective-permute-start.8
  64.3 0.9 collective-permute-done.8.sw
  65.2 2.1 %collective-permute-start.9 = (f32[8,16,128]{2,1,0:T(8,128)S(1)}, f32[8,16,128]{2,1,0:T(8,128)S(1)}, u32[]{:S(2)}, u32[]{:S(2)}) collective-permute-start(f32[8,16,128]{2,1,0:T(8,128)S(1)} %pad_maximum_fusion.2), channel_id=1, source_target_pairs={{1,2},{2,1},{3,4},{4,3},{5,6},{6,5},{7,8},{8,7},{9,10},{10,9},{11,... | collective-permute-start | bytes 196616 | tf_op jit(solution)/shard_map/ppermute | solution.py:330
  67.3 3.5 %collective-permute-done.9.p1 = f32[8,16,128]{2,1,0:T(8,128)S(1)} collective-permute-done((f32[8,16,128]{2,1,0:T(8,128)S(1)}, f32[8,16,128]{2,1,0:T(8,128)S(1)}, u32[]{:S(2)}, u32[]{:S(2)}) %collective-permute-start.9) | collective-permute-done | bytes 65568 | tf_op jit(solution)/shard_map/ppermute | solution.py:330
  70.8 3.9 %collective-permute-start.10 = (f32[8,16,128]{2,1,0:T(8,128)S(1)}, f32[8,16,128]{2,1,0:T(8,128)S(1)}, u32[]{:S(2)}, u32[]{:S(2)}) collective-permute-start(f32[8,16,128]{2,1,0:T(8,128)S(1)} %collective-permute-done.9.p1), channel_id=1, source_target_pairs={{0,1},{1,0},{2,3},{3,2},{4,5},{5,4},{6,7},{7,6},{8,9},{9,8},{10,11... | collective-permute-start | bytes 196616 | tf_op jit(solution)/shard_map/ppermute | solution.py:330
  74.7 1.9 %collective-permute-start.11 = (f32[4,16,128]{2,1,0:T(8,128)S(1)}, f32[4,16,128]{2,1,0:T(8,128)S(1)}, u32[]{:S(2)}, u32[]{:S(2)}) collective-permute-start(f32[4,16,128]{2,1,0:T(8,128)S(1)} %get-tuple-element.20.v.head), channel_id=1, source_target_pairs={{1,4},{3,6},{4,1},{5,8},{6,3},{7,10},{8,5},{9,12},{10,7},{11,14},{... | collective-permute-start | bytes 98312 | tf_op jit(solution)/shard_map/ppermute | solution.py:330
  76.6 4.2 %collective-permute-done.11.p3 = f32[4,16,128]{2,1,0:T(8,128)S(1)} collective-permute-done((f32[4,16,128]{2,1,0:T(8,128)S(1)}, f32[4,16,128]{2,1,0:T(8,128)S(1)}, u32[]{:S(2)}, u32[]{:S(2)}) %collective-permute-start.11) | collective-permute-done | bytes 32800 | tf_op jit(solution)/shard_map/ppermute | solution.py:330
  80.9 0.0 collective-permute-done.10.p2
  80.9 6.4 %shard_map.81 = (f32[4,16,128]{2,1,0:T(8,128)S(1)}, f32[4,16,128]{2,1,0:T(8,128)S(1)}, f32[4,16,128]{2,1,0:T(8,128)S(1)}) custom-call(s32[4,32]{1,0:T(4,128)S(1)} %fusion.1.index_ref, f32[4,7]{1,0:T(4,128)S(1)} %add_convert_fusion.flags_ref, bf16[4,16,256,256]{3,2,1,0:T(8,128)(2,1)S(1)} %shard_map.77.split, f32[4,128,128]{2,1,0:T(8,128)S(1)} %copy-done, ...), custom_call_target="tpu_custom_call" | custom-call | tf_op jit(solution)/shard_map/pallas_call | solution.py:221
  87.2 1.8 %collective-permute-start.12 = (f32[4,16,128]{2,1,0:T(8,128)S(1)}, f32[4,16,128]{2,1,0:T(8,128)S(1)}, u32[]{:S(2)}, u32[]{:S(2)}) collective-permute-start(f32[4,16,128]{2,1,0:T(8,128)S(1)} %get-tuple-element.22.v.smooth), channel_id=1, source_target_pairs={{0,1},{1,0},{2,3},{3,2},{4,5},{5,4},{6,7},{7,6},{8,9},{9,8},{10,11... | collective-permute-start | bytes 98312 | tf_op jit(solution)/shard_map/ppermute | solution.py:330
  89.1 0.9 collective-permute-done.12.sw
  89.9 1.9 %collective-permute-start.13 = (f32[8,16,128]{2,1,0:T(8,128)S(1)}, f32[8,16,128]{2,1,0:T(8,128)S(1)}, u32[]{:S(2)}, u32[]{:S(2)}) collective-permute-start(f32[8,16,128]{2,1,0:T(8,128)S(1)} %pad_maximum_fusion.3), channel_id=1, source_target_pairs={{1,2},{2,1},{3,4},{4,3},{5,6},{6,5},{7,8},{8,7},{9,10},{10,9},{11,... | collective-permute-start | bytes 196616 | tf_op jit(solution)/shard_map/ppermute | solution.py:330
  91.8 4.2 %collective-permute-done.13.p1 = f32[8,16,128]{2,1,0:T(8,128)S(1)} collective-permute-done((f32[8,16,128]{2,1,0:T(8,128)S(1)}, f32[8,16,128]{2,1,0:T(8,128)S(1)}, u32[]{:S(2)}, u32[]{:S(2)}) %collective-permute-start.13) | collective-permute-done | bytes 65568 | tf_op jit(solution)/shard_map/ppermute | solution.py:330
  96.0 3.4 %collective-permute-start.14 = (f32[8,16,128]{2,1,0:T(8,128)S(1)}, f32[8,16,128]{2,1,0:T(8,128)S(1)}, u32[]{:S(2)}, u32[]{:S(2)}) collective-permute-start(f32[8,16,128]{2,1,0:T(8,128)S(1)} %collective-permute-done.13.p1), channel_id=1, source_target_pairs={{0,1},{1,0},{2,3},{3,2},{4,5},{5,4},{6,7},{7,6},{8,9},{9,8},{10,11... | collective-permute-start | bytes 196616 | tf_op jit(solution)/shard_map/ppermute | solution.py:330
  99.4 1.9 %collective-permute-start.15 = (f32[4,16,128]{2,1,0:T(8,128)S(1)}, f32[4,16,128]{2,1,0:T(8,128)S(1)}, u32[]{:S(2)}, u32[]{:S(2)}) collective-permute-start(f32[4,16,128]{2,1,0:T(8,128)S(1)} %get-tuple-element.22.v.smooth), channel_id=1, source_target_pairs={{1,4},{3,6},{4,1},{5,8},{6,3},{7,10},{8,5},{9,12},{10,7},{11,14},{... | collective-permute-start | bytes 98312 | tf_op jit(solution)/shard_map/ppermute | solution.py:330
  101.4 4.2 %collective-permute-done.15.p3 = f32[4,16,128]{2,1,0:T(8,128)S(1)} collective-permute-done((f32[4,16,128]{2,1,0:T(8,128)S(1)}, f32[4,16,128]{2,1,0:T(8,128)S(1)}, u32[]{:S(2)}, u32[]{:S(2)}) %collective-permute-start.15) | collective-permute-done | bytes 32800 | tf_op jit(solution)/shard_map/ppermute | solution.py:330
  105.6 0.0 collective-permute-done.14.p2
  105.6 3.9 %shard_map.82 = (f32[4,16,128]{2,1,0:T(8,128)S(1)}, f32[32,8,128]{2,1,0:T(8,128)S(1)}) custom-call(s32[4,32]{1,0:T(4,128)S(1)} %fusion.1.index_ref, f32[4,7]{1,0:T(4,128)S(1)} %add_convert_fusion.flags_ref, bf16[4,16,256,256]{3,2,1,0:T(8,128)(2,1)S(1)} %shard_map.77.split, f32[4,16,128]{2,1,0:T(8,128)S(1)} %get-tuple-element.19.target, ...), custom_call_target="tpu_custom_call" | custom-call | tf_op jit(solution)/shard_map/pallas_call | solution.py:221
  109.5 10.7 %all_to_all.11.gathered = f32[32,8,128]{2,1,0:T(8,128)S(1)} all-to-all(f32[32,8,128]{2,1,0:T(8,128)S(1)} %get-tuple-element.23), channel_id=1, replica_groups=mesh['grp'=4,'row'=8] {'grp','row'}, dimensions={0} | all-to-all | bytes 262144 | tf_op jit(solution)/shard_map/all_to_all | solution.py:348
  120.2 5.7 %shard_map.83 = (f32[4,16,128]{2,1,0:T(8,128)}, f32[4,16,128]{2,1,0:T(8,128)}) custom-call(f32[4,7]{1,0:T(4,128)S(1)} %add_convert_fusion.flags_ref, f32[32,8,128]{2,1,0:T(8,128)S(1)} %all_to_all.11.gathered, f32[4,16,128]{2,1,0:T(8,128)S(1)} %copy-done.1, f32[4,16,128]{2,1,0:T(8,128)S(1)} %get-tuple-element.24.solution, ...), custom_call_target="tpu_custom_call" | custom-call | tf_op jit(solution)/shard_map/pallas_call | solution.py:319
  (4 shorter events, 0.0 us)
Async XLA Ops:
  0.6 21.5 %collective-permute-start.3 = (f32[4,16,128]{2,1,0:T(8,128)}, f32[4,16,128]{2,1,0:T(8,128)S(1)}, u32[]{:S(2)}, u32[]{:S(2)}) collective-permute-start(f32[4,16,128]{2,1,0:T(8,128)} %right.5), channel_id=1, source_target_pairs={{1,4},{3,6},{4,1},{5,8},{6,3},{7,10},{8,5},{9,12},{10,7},{11,14},{... | collective-permute-start | bytes 98312 | tf_op jit(solution)/shard_map/ppermute | solution.py:330
  5.4 2.8 %collective-permute-start = (f32[4,16,128]{2,1,0:T(8,128)}, f32[4,16,128]{2,1,0:T(8,128)S(1)}, u32[]{:S(2)}, u32[]{:S(2)}) collective-permute-start(f32[4,16,128]{2,1,0:T(8,128)} %right.5), channel_id=1, source_target_pairs={{0,1},{1,0},{2,3},{3,2},{4,5},{5,4},{6,7},{7,6},{8,9},{9,8},{10,11... | collective-permute-start | bytes 98312 | tf_op jit(solution)/shard_map/ppermute | solution.py:330
  9.0 5.6 %collective-permute-start.1 = (f32[8,16,128]{2,1,0:T(8,128)S(1)}, f32[8,16,128]{2,1,0:T(8,128)S(1)}, u32[]{:S(2)}, u32[]{:S(2)}) collective-permute-start(f32[8,16,128]{2,1,0:T(8,128)S(1)} %pad_maximum_fusion), channel_id=1, source_target_pairs={{1,2},{2,1},{3,4},{4,3},{5,6},{6,5},{7,8},{8,7},{9,10},{10,9},{11,... | collective-permute-start | bytes 196616 | tf_op jit(solution)/shard_map/ppermute | solution.py:330
  14.6 7.6 %collective-permute-start.2 = (f32[8,16,128]{2,1,0:T(8,128)S(1)}, f32[8,16,128]{2,1,0:T(8,128)S(1)}, u32[]{:S(2)}, u32[]{:S(2)}) collective-permute-start(f32[8,16,128]{2,1,0:T(8,128)S(1)} %collective-permute-done.1.p1), channel_id=1, source_target_pairs={{0,1},{1,0},{2,3},{3,2},{4,5},{5,4},{6,7},{7,6},{8,9},{9,8},{10,11... | collective-permute-start | bytes 196616 | tf_op jit(solution)/shard_map/ppermute | solution.py:330
  18.3 3.9 %copy-start.1 = (f32[4,16,128]{2,1,0:T(8,128)S(1)}, f32[4,16,128]{2,1,0:T(8,128)}, u32[]{:S(2)}) copy-start(f32[4,16,128]{2,1,0:T(8,128)} %right.5) | copy-start | bytes 98308
  22.1 36.1 %copy-start = (f32[4,128,128]{2,1,0:T(8,128)S(1)}, f32[4,128,128]{2,1,0:T(8,128)}, u32[]{:S(2)}) copy-start(f32[4,128,128]{2,1,0:T(8,128)} %precond.3) | copy-start | bytes 786436
  25.7 1.3 %collective-permute-start.4 = (f32[4,16,128]{2,1,0:T(8,128)S(1)}, f32[4,16,128]{2,1,0:T(8,128)S(1)}, u32[]{:S(2)}, u32[]{:S(2)}) collective-permute-start(f32[4,16,128]{2,1,0:T(8,128)S(1)} %get-tuple-element.15.v.image), channel_id=1, source_target_pairs={{0,1},{1,0},{2,3},{3,2},{4,5},{5,4},{6,7},{7,6},{8,9},{9,8},{10,11... | collective-permute-start | bytes 98312 | tf_op jit(solution)/shard_map/ppermute | solution.py:330
  27.0 5.6 %collective-permute-start.5 = (f32[8,16,128]{2,1,0:T(8,128)S(1)}, f32[8,16,128]{2,1,0:T(8,128)S(1)}, u32[]{:S(2)}, u32[]{:S(2)}) collective-permute-start(f32[8,16,128]{2,1,0:T(8,128)S(1)} %pad_maximum_fusion.1), channel_id=1, source_target_pairs={{1,2},{2,1},{3,4},{4,3},{5,6},{6,5},{7,8},{8,7},{9,10},{10,9},{11,... | collective-permute-start | bytes 196616 | tf_op jit(solution)/shard_map/ppermute | solution.py:330
  32.6 9.9 %collective-permute-start.6 = (f32[8,16,128]{2,1,0:T(8,128)S(1)}, f32[8,16,128]{2,1,0:T(8,128)S(1)}, u32[]{:S(2)}, u32[]{:S(2)}) collective-permute-start(f32[8,16,128]{2,1,0:T(8,128)S(1)} %collective-permute-done.5.p1), channel_id=1, source_target_pairs={{0,1},{1,0},{2,3},{3,2},{4,5},{5,4},{6,7},{7,6},{8,9},{9,8},{10,11... | collective-permute-start | bytes 196616 | tf_op jit(solution)/shard_map/ppermute | solution.py:330
  36.4 6.1 %collective-permute-start.7 = (f32[4,16,128]{2,1,0:T(8,128)S(1)}, f32[4,16,128]{2,1,0:T(8,128)S(1)}, u32[]{:S(2)}, u32[]{:S(2)}) collective-permute-start(f32[4,16,128]{2,1,0:T(8,128)S(1)} %get-tuple-element.15.v.image), channel_id=1, source_target_pairs={{1,4},{3,6},{4,1},{5,8},{6,3},{7,10},{8,5},{9,12},{10,7},{11,14},{... | collective-permute-start | bytes 98312 | tf_op jit(solution)/shard_map/ppermute | solution.py:330
  63.8 1.4 %collective-permute-start.8 = (f32[4,16,128]{2,1,0:T(8,128)S(1)}, f32[4,16,128]{2,1,0:T(8,128)S(1)}, u32[]{:S(2)}, u32[]{:S(2)}) collective-permute-start(f32[4,16,128]{2,1,0:T(8,128)S(1)} %get-tuple-element.20.v.head), channel_id=1, source_target_pairs={{0,1},{1,0},{2,3},{3,2},{4,5},{5,4},{6,7},{7,6},{8,9},{9,8},{10,11... | collective-permute-start | bytes 98312 | tf_op jit(solution)/shard_map/ppermute | solution.py:330
  65.2 5.6 %collective-permute-start.9 = (f32[8,16,128]{2,1,0:T(8,128)S(1)}, f32[8,16,128]{2,1,0:T(8,128)S(1)}, u32[]{:S(2)}, u32[]{:S(2)}) collective-permute-start(f32[8,16,128]{2,1,0:T(8,128)S(1)} %pad_maximum_fusion.2), channel_id=1, source_target_pairs={{1,2},{2,1},{3,4},{4,3},{5,6},{6,5},{7,8},{8,7},{9,10},{10,9},{11,... | collective-permute-start | bytes 196616 | tf_op jit(solution)/shard_map/ppermute | solution.py:330
  70.8 10.1 %collective-permute-start.10 = (f32[8,16,128]{2,1,0:T(8,128)S(1)}, f32[8,16,128]{2,1,0:T(8,128)S(1)}, u32[]{:S(2)}, u32[]{:S(2)}) collective-permute-start(f32[8,16,128]{2,1,0:T(8,128)S(1)} %collective-permute-done.9.p1), channel_id=1, source_target_pairs={{0,1},{1,0},{2,3},{3,2},{4,5},{5,4},{6,7},{7,6},{8,9},{9,8},{10,11... | collective-permute-start | bytes 196616 | tf_op jit(solution)/shard_map/ppermute | solution.py:330
  74.7 6.1 %collective-permute-start.11 = (f32[4,16,128]{2,1,0:T(8,128)S(1)}, f32[4,16,128]{2,1,0:T(8,128)S(1)}, u32[]{:S(2)}, u32[]{:S(2)}) collective-permute-start(f32[4,16,128]{2,1,0:T(8,128)S(1)} %get-tuple-element.20.v.head), channel_id=1, source_target_pairs={{1,4},{3,6},{4,1},{5,8},{6,3},{7,10},{8,5},{9,12},{10,7},{11,14},{... | collective-permute-start | bytes 98312 | tf_op jit(solution)/shard_map/ppermute | solution.py:330
  87.2 2.7 %collective-permute-start.12 = (f32[4,16,128]{2,1,0:T(8,128)S(1)}, f32[4,16,128]{2,1,0:T(8,128)S(1)}, u32[]{:S(2)}, u32[]{:S(2)}) collective-permute-start(f32[4,16,128]{2,1,0:T(8,128)S(1)} %get-tuple-element.22.v.smooth), channel_id=1, source_target_pairs={{0,1},{1,0},{2,3},{3,2},{4,5},{5,4},{6,7},{7,6},{8,9},{9,8},{10,11... | collective-permute-start | bytes 98312 | tf_op jit(solution)/shard_map/ppermute | solution.py:330
  89.9 6.1 %collective-permute-start.13 = (f32[8,16,128]{2,1,0:T(8,128)S(1)}, f32[8,16,128]{2,1,0:T(8,128)S(1)}, u32[]{:S(2)}, u32[]{:S(2)}) collective-permute-start(f32[8,16,128]{2,1,0:T(8,128)S(1)} %pad_maximum_fusion.3), channel_id=1, source_target_pairs={{1,2},{2,1},{3,4},{4,3},{5,6},{6,5},{7,8},{8,7},{9,10},{10,9},{11,... | collective-permute-start | bytes 196616 | tf_op jit(solution)/shard_map/ppermute | solution.py:330
  96.0 9.6 %collective-permute-start.14 = (f32[8,16,128]{2,1,0:T(8,128)S(1)}, f32[8,16,128]{2,1,0:T(8,128)S(1)}, u32[]{:S(2)}, u32[]{:S(2)}) collective-permute-start(f32[8,16,128]{2,1,0:T(8,128)S(1)} %collective-permute-done.13.p1), channel_id=1, source_target_pairs={{0,1},{1,0},{2,3},{3,2},{4,5},{5,4},{6,7},{7,6},{8,9},{9,8},{10,11... | collective-permute-start | bytes 196616 | tf_op jit(solution)/shard_map/ppermute | solution.py:330
  99.4 6.1 %collective-permute-start.15 = (f32[4,16,128]{2,1,0:T(8,128)S(1)}, f32[4,16,128]{2,1,0:T(8,128)S(1)}, u32[]{:S(2)}, u32[]{:S(2)}) collective-permute-start(f32[4,16,128]{2,1,0:T(8,128)S(1)} %get-tuple-element.22.v.smooth), channel_id=1, source_target_pairs={{1,4},{3,6},{4,1},{5,8},{6,3},{7,10},{8,5},{9,12},{10,7},{11,14},{... | collective-permute-start | bytes 98312 | tf_op jit(solution)/shard_map/ppermute | solution.py:330

commit v3 on v2

v3 whole, which is shorter than its diff:
```python
import jax
import jax.numpy as jnp
from jax import lax
from jax.experimental import pallas as pl
from jax.experimental.pallas import tpu as pltpu
from jax.sharding import PartitionSpec as P


BAND = 12
OFFSETS = (0, 1, -1, -2, 2, 3, -3)
REACH = 3
SLOTS = len(OFFSETS)
HIGHEST = lax.Precision.HIGHEST
AXES = ("grp", "row")
VMEM = pltpu.VMEM
SMEM = pltpu.SMEM


def spec(space):
    return pl.BlockSpec(memory_space=space)


def params(mib):
    return pltpu.CompilerParams(vmem_limit_bytes=mib << 20)


def dot_nt(former, latter):
    return lax.dot_general(
        former, latter, (((1,), (1,)), ((), ())), precision=HIGHEST,
        preferred_element_type=jnp.float32,
    )


def dot_tn(former, latter):
    return lax.dot_general(
        former, latter, (((0,), (0,)), ((), ())), precision=HIGHEST,
        preferred_element_type=jnp.float32,
    )


def dot_nn(former, latter):
    return jnp.dot(former, latter, precision=HIGHEST, preferred_element_type=jnp.float32)


def split3(value):
    high = value.astype(jnp.bfloat16)
    rest = value - high.astype(jnp.float32)
    middle = rest.astype(jnp.bfloat16)
    low = (rest - middle.astype(jnp.float32)).astype(jnp.bfloat16)
    return high, middle, low


def build_table(pieces, place, table_ref, classes, blocks, cols):
    slot = 0
    for piece in pieces:
        for first in range(0, piece.shape[0], blocks):
            position, flags = place.slot(slot)
            for block in range(blocks):
                value = piece[first + block]
                for k in range(classes):
                    terms = split3(value * flags[k])
                    for s, term in enumerate(terms):
                        rows = pl.ds((3 * k + s) * cols, cols)
                        table_ref[position * blocks + block, rows, :] = term
            slot += 1


class Place:
    def __init__(self, lost_ref):
        self.me = lax.axis_index(AXES)
        self.row = lax.axis_index("row")
        self.group = lax.axis_index("grp")
        self.rows = lax.axis_size("row")
        self.lost = lax.rem(lost_ref[0], lax.axis_size("grp"))
        self.sign = 1 - 2 * lax.rem(self.me, 2)
        self.mine = jnp.where(self.group == self.lost, 1.0, 0.0)

    def slot(self, slot):
        offset = self.sign * OFFSETS[slot]
        row = self.row + offset
        side = jnp.where(row < 0, -1, jnp.where(row >= self.rows, 1, 0))
        own = jnp.where(side == 0, 1.0, 0.0)
        lost = jnp.where((side != 0) & (self.group + side == self.lost), 1.0, 0.0)
        return offset + REACH, (own, lost, 1.0 - own - lost)

    def base(self, blocks):
        return (self.me - REACH) * blocks


def row_product(columns_ref, base, table_ref, split_ref, row, classes, cols):
    pairs, tb = split_ref.shape[1], split_ref.shape[2] // 2
    total = None
    for pair in range(pairs):
        left = jnp.concatenate(
            [table_ref[columns_ref[row, 2 * pair + j] - base] for j in (0, 1)], axis=1
        )
        part = lax.dot_general(
            left, split_ref[row, pair], (((1,), (1,)), ((), ())),
            preferred_element_type=jnp.float32,
        )
        total = part if total is None else total + part
    total = total[:, :tb] + total[:, tb:]
    out = []
    for k in range(classes):
        base = 3 * k * cols
        out.append(
            total[base : base + cols]
            + total[base + cols : base + 2 * cols]
            + total[base + 2 * cols : base + 3 * cols]
        )
    return out


def split_kernel(tiles_hbm, precond, split, halves, tiles, sems):
    blocks, count, tb, _ = tiles.shape
    copies = [
        pltpu.make_async_copy(tiles_hbm.at[row], tiles.at[row], sems.at[row])
        for row in range(blocks)
    ]
    for copy in copies:
        copy.start()
    for row in range(blocks):
        high = precond[row].astype(jnp.bfloat16)
        halves[row, 0:tb] = high
        halves[row, tb : 2 * tb] = (precond[row] - high.astype(jnp.float32)).astype(jnp.bfloat16)
    for row in range(blocks):
        copies[row].wait()
        for k in range(count):
            tile = tiles[row, k]
            high = tile.astype(jnp.bfloat16)
            rest = (tile - high.astype(jnp.float32)).astype(jnp.bfloat16)
            side = (k % 2) * tb
            split[row, k // 2, 0:tb, side : side + tb] = high
            split[row, k // 2, tb : 2 * tb, side : side + tb] = rest


def split_call(tiles, precond):
    blocks, count, tb, _ = tiles.shape
    return pl.pallas_call(
        split_kernel,
        out_shape=[
            jax.ShapeDtypeStruct((blocks, count // 2, 2 * tb, 2 * tb), jnp.bfloat16),
            jax.ShapeDtypeStruct((blocks, 2 * tb, tb), jnp.bfloat16),
        ],
        in_specs=[spec(pltpu.HBM), spec(VMEM)],
        out_specs=[spec(VMEM)] * 2,
        scratch_shapes=[VMEM(tiles.shape, jnp.float32), pltpu.SemaphoreType.DMA((blocks,))],
        compiler_params=params(24),
        cost_estimate=pl.CostEstimate(flops=0, bytes_accessed=12 * tiles.size // 2, transcendentals=0),
    )(pltpu.with_memory_space_constraint(tiles, pltpu.HBM), precond)


def smoothed(value, halves, cols, tb):
    left = jnp.concatenate(split3(value), axis=0)
    both = lax.dot_general(
        left, halves, (((1,), (1,)), ((), ())), preferred_element_type=jnp.float32
    )
    both = both[:, :tb] + both[:, tb:]
    return both[:cols] + both[cols : 2 * cols] + both[2 * cols :]


def lanes(ref):
    return jnp.concatenate([ref[i] for i in range(ref.shape[0])], axis=1)


def grid16(cols):
    rows = lax.broadcasted_iota(jnp.int32, (cols, cols), 0)
    columns = lax.broadcasted_iota(jnp.int32, (cols, cols), 1)
    return rows, columns


def pack_gram(gram_ref, former, latter, scale, cols):
    gram = dot_nt(former, latter)
    if scale is not None:
        gram = gram * scale
    g00, g01, g02 = (gram[:cols, k * cols : (k + 1) * cols] for k in range(3))
    g11, g12 = (gram[cols:, k * cols : (k + 1) * cols] for k in (1, 2))
    rows, columns = grid16(cols)
    upper = rows <= columns
    first = jnp.where(upper, g00, g11)
    middle = jnp.sum(jnp.where(rows == columns, g11, 0.0), axis=1, keepdims=True)
    last = jnp.where(rows == columns + 1, middle, 0.0)
    last = jnp.where((rows == cols - 1) & (columns == 0), g11[0:1, 0:1], last)
    last = jnp.where(upper, 0.5 * (g12 + g12.T), last)
    flat = jnp.concatenate([first, g01, g02, last], axis=1)
    half = cols // 2
    packed = jnp.concatenate([flat[:half], flat[half:]], axis=1)
    gram_ref[...] = jnp.broadcast_to(packed[None], gram_ref.shape)


def unpack_gram(packed, cols):
    width = packed.shape[1] // 2
    flat = jnp.concatenate([packed[:, :width], packed[:, width:]], axis=0)
    turned = flat.T
    first, g01, g02, last = (flat[:, k * cols : (k + 1) * cols] for k in range(4))
    first_t, g01_t, g02_t, last_t = (turned[k * cols : (k + 1) * cols] for k in range(4))
    rows, columns = grid16(cols)
    upper = rows <= columns
    g00 = jnp.where(upper, first, first_t)
    middle = jnp.sum(jnp.where(rows == columns + 1, last, 0.0), axis=1, keepdims=True)
    middle = jnp.where(rows == 0, last[cols - 1 : cols, 0:1], middle)
    g11 = jnp.where(rows > columns, first, jnp.where(rows < columns, first_t, middle))
    g12 = jnp.where(upper, last, last_t)
    return g00, g01, g01_t, g02, g02_t, g11, g12


def first_kernel(columns_ref, lost_ref, split, v, sw, p1, p2, p3, parts, image, table):
    blocks, cols, _ = v.shape
    place = Place(lost_ref)
    base = place.base(blocks)
    build_table((v, sw, p1, p2, p3), place, table, 3, blocks, cols)
    for row in range(blocks):
        out = row_product(columns_ref, base, table, split, row, 3, cols)
        for k in range(3):
            parts[k, row] = out[k]
        image[row] = out[0] + out[1] + out[2]


def second_kernel(
    columns_ref, lost_ref, split, right, v, sw, p1, p2, p3, parts, gram, table, image
):
    blocks, cols, _ = v.shape
    place = Place(lost_ref)
    base = place.base(blocks)
    build_table((v, sw, p1, p2, p3), place, table, 3, blocks, cols)
    for row in range(blocks):
        out = row_product(columns_ref, base, table, split, row, 3, cols)
        for k in range(3):
            parts[k, row] = out[k]
        image[row] = out[0] + out[1] + out[2]
    former = jnp.concatenate([lanes(right), lanes(v)], axis=0)
    latter = jnp.concatenate([former, lanes(image)], axis=0)
    pack_gram(gram, former, latter, None, cols)


def third_kernel(
    columns_ref, lost_ref, split, precond, v, sw, p1, p2, p3, applied, smooth, lost, table
):
    blocks, cols, _ = v.shape
    place = Place(lost_ref)
    base = place.base(blocks)
    build_table((v, sw, p1, p2, p3), place, table, 2, blocks, cols)
    mine = place.mine
    for row in range(blocks):
        out = row_product(columns_ref, base, table, split, row, 2, cols)
        applied[row] = out[0]
        lost[row] = out[0] * mine + out[1]
        smooth[row] = smoothed(out[0], precond[row], cols, v.shape[2])


def fourth_kernel(
    columns_ref, lost_ref, split, target, head, applied, v, sw, p1, p2, p3, lost, gram,
    table, second,
):
    blocks, cols, _ = v.shape
    place = Place(lost_ref)
    base = place.base(blocks)
    build_table((v, sw, p1, p2, p3), place, table, 2, blocks, cols)
    mine = place.mine
    for row in range(blocks):
        out = row_product(columns_ref, base, table, split, row, 2, cols)
        second[row] = out[0]
        lost[row] = out[0] * mine + out[1]
    former = jnp.concatenate([lanes(head), lanes(v)], axis=0)
    latter = jnp.concatenate([lanes(target), lanes(applied), lanes(second)], axis=0)
    pack_gram(gram, former, latter, mine, cols)


def tile_call(kernel, classes, outs, extra, split, operands_vmem, columns, lost):
    blocks, cols, tb = operands_vmem[-1].shape
    scratch = [VMEM((SLOTS * blocks, 3 * classes * cols, tb), jnp.bfloat16)] + extra
    return pl.pallas_call(
        kernel,
        out_shape=outs,
        in_specs=[spec(SMEM), spec(SMEM)] + [spec(VMEM)] * (1 + len(operands_vmem)),
        out_specs=[spec(VMEM)] * len(outs),
        scratch_shapes=scratch,
        compiler_params=params(16),
    )(columns, lost, split, *operands_vmem)


def eliminate(matrix, target):
    size = matrix.shape[0]
    rows = lax.broadcasted_iota(jnp.int32, target.shape, 0)
    columns = [jnp.broadcast_to(matrix[:, k : k + 1], target.shape) for k in range(size)]
    for k in range(size):
        pivot = columns[k]
        inverse = 1.0 / pivot[k : k + 1, :]
        scaled = pivot * inverse
        here = rows == k
        top = target[k : k + 1, :]
        target = jnp.where(here, top * inverse, target - scaled * top)
        for i in range(k + 1, size):
            entry = pivot[i : i + 1, :]
            columns[i] = jnp.where(here, entry * inverse, columns[i] - scaled * entry)
    return target


def coefficients(gathered, cols):
    g00, g01, g01_t, g02, g02_t, g11, g12 = unpack_gram(jnp.sum(gathered[...], axis=0), cols)
    whole, cross = 0.5 * (g01 + g01_t), 0.5 * (g02 + g11)
    cross_t = 0.5 * (g02_t + g11)
    big = jnp.concatenate(
        [jnp.concatenate([whole, cross], axis=1), jnp.concatenate([cross_t, g12], axis=1)], axis=0
    )
    rows, columns = grid16(cols)
    unit = (rows == columns).astype(jnp.float32)
    advance = eliminate(whole, g00)
    inverse = eliminate(g00, unit)
    moved = dot_nn(jnp.concatenate([g01, g11], axis=0), advance)
    squares = g00 - moved[:cols] - dot_tn(advance, g01_t - moved[cols:])
    mixing = dot_nn(inverse, squares)
    heading = jnp.concatenate([unit + mixing, -advance], axis=0)
    curvature = dot_tn(heading, dot_nn(big, heading))
    second = eliminate(curvature, squares)
    combo = dot_nn(heading, second)
    return jnp.concatenate([combo[:cols] + advance, combo[cols:]], axis=0)


def outer_kernel(
    lost_ref, gathered, right, image, parts_b, parts_y, precond, solution, target, head, kept
):
    blocks, cols, tb = right.shape
    mine = Place(lost_ref).mine
    weights = coefficients(gathered, cols)

    def basis(pick):
        return jnp.concatenate(
            [
                jnp.concatenate([pick(0, i) for i in range(blocks)], axis=1),
                jnp.concatenate([pick(1, i) for i in range(blocks)], axis=1),
            ],
            axis=0,
        )

    parts = (parts_b, parts_y)
    own = (right, image)
    stacked = jnp.concatenate(
        [
            basis(lambda n, i: own[n][i]),
            basis(lambda n, i: parts[n][1, i] + parts[n][2, i]),
            basis(lambda n, i: parts[n][0, i] * (1.0 - mine) + parts[n][2, i]),
        ],
        axis=1,
    )
    made = dot_tn(weights, stacked)
    span = blocks * tb
    for i in range(blocks):
        solution[i] = made[:, i * tb : (i + 1) * tb]
        aim = right[i] - made[:, span + i * tb : span + (i + 1) * tb]
        target[i] = aim
        head[i] = smoothed(aim, precond[i], cols, tb)
        kept[i] = made[:, 2 * span + i * tb : 2 * span + (i + 1) * tb]


def inner_kernel(
    lost_ref, gathered, right, solution, kept, head, smooth, lost0, lost1, recovered, residual
):
    blocks, cols, tb = right.shape
    mine = Place(lost_ref).mine
    weights = coefficients(gathered, cols)
    stacked = jnp.concatenate(
        [
            jnp.concatenate([lanes(head), lanes(lost0)], axis=1),
            jnp.concatenate([lanes(smooth), lanes(lost1)], axis=1),
        ],
        axis=0,
    )
    made = dot_tn(weights, stacked)
    span = blocks * tb
    for i in range(blocks):
        estimate = made[:, i * tb : (i + 1) * tb]
        recovered[i] = jnp.where(mine > 0.5, estimate, solution[i])
        residual[i] = right[i] - kept[i] - made[:, span + i * tb : span + (i + 1) * tb]


def small_call(kernel, outs, lost, gathered, *arrays):
    return pl.pallas_call(
        kernel,
        out_shape=outs,
        in_specs=[spec(SMEM)] + [spec(VMEM)] * (1 + len(arrays)),
        out_specs=[spec(VMEM)] * len(outs),
        compiler_params=params(16),
    )(lost, gathered, *arrays)


def move(value, total, where):
    pairs = [(i, where(i)) for i in range(total) if 0 <= where(i) < total]
    return lax.ppermute(value, AXES, pairs)


def window(value, total):
    swapped = move(value, total, lambda i: i ^ 1)
    pair = jnp.concatenate([value, swapped], axis=0)
    near = move(pair, total, lambda i: i - 1 if i % 2 == 0 else i + 1)
    far = move(value, total, lambda i: i - 3 if i % 2 == 0 else i + 3)
    other = move(near, total, lambda i: i ^ 1)
    return value, swapped, near, other, far


def exchange(gram):
    return lax.all_to_all(gram, AXES, 0, 0)


def per_device(matrix_tiles, column_index, precond, right_side, lost_group):
    blocks, cols, tb = right_side.shape
    assert -(-BAND // blocks) == REACH <= lax.axis_size("row")
    total = lax.axis_size("row") * lax.axis_size("grp")

    vec = jax.ShapeDtypeStruct(right_side.shape, jnp.float32)
    vec3 = jax.ShapeDtypeStruct((3,) + right_side.shape, jnp.float32)
    gram = jax.ShapeDtypeStruct((total, cols // 2, 8 * cols), jnp.float32)
    assert tb == 8 * cols
    held = VMEM(right_side.shape, jnp.float32)

    split, halves = split_call(matrix_tiles, precond)
    parts_b, image = tile_call(
        first_kernel, 3, [vec3, vec], [], split, window(right_side, total), column_index, lost_group
    )
    parts_y, gram_outer = tile_call(
        second_kernel, 3, [vec3, gram], [held], split,
        (right_side,) + window(image, total), column_index, lost_group,
    )
    solution, target, head, kept = small_call(
        outer_kernel, [vec] * 4, lost_group, exchange(gram_outer), right_side, image, parts_b, parts_y, halves
    )
    applied, smooth, lost0 = tile_call(
        third_kernel, 2, [vec] * 3, [], split, (halves,) + window(head, total), column_index, lost_group
    )
    lost1, gram_inner = tile_call(
        fourth_kernel, 2, [vec, gram], [held], split,
        (target, head, applied) + window(smooth, total), column_index, lost_group,
    )
    recovered, residual = small_call(
        inner_kernel, [vec] * 2, lost_group, exchange(gram_inner), right_side, solution, kept, head, smooth,
        lost0, lost1,
    )
    return (recovered, residual)


def solution(mesh):
    in_specs = (
        P(("grp", "row"), None, None, None),
        P(("grp", "row"), None),
        P(("grp", "row"), None, None),
        P(("grp", "row"), None, None),
        P(),
    )
    out_specs = (P(("grp", "row"), None, None), P(("grp", "row"), None, None))

    return jax.shard_map(
        per_device, mesh=mesh, in_specs=in_specs, out_specs=out_specs, check_vma=False
    )
```

time: 128 us -> 122 us (0.953)
  Pallas kernels: 33.2 us -> 26.2 us
  starting transfers between devices: 37.5 us -> 39.2 us
  other arithmetic: 2.24 us -> 0.78 us
    pallas_call x2, Pallas kernels: 11.3 us -> 5.01 us  [small_call(): pl.pallas_call(kernel, out_shape=outs, in_specs=[spec(SMEM)] + [spec(VMEM...]
    ppermute x16, starting transfers between devices: 37.5 us -> 39.2 us  [move(): return lax.ppermute(value, AXES, pairs)]
  transfers between devices with their start and end apart: 16 -> 16, of which waited for: 10 -> 11; matrix products, arithmetic and copies ran while one was open for 2% -> 0% of each run, Pallas kernels for 3% -> 3%
where the time goes in v3:
time: 122 us; the launch traced here: 119 us
  starting transfers between devices  39.2 us (32%)
  waiting for transfers between devices  28 us (23%)
  Pallas kernels  26.2 us (21%)
  blocking collectives  22.6 us (19%)
  between operations  1.46 us (1%)
    ppermute x16, starting transfers between devices, move(): return lax.ppermute(value, AXES, pairs)  39.2 us
    ppermute x16, waiting for transfers between devices, move(): return lax.ppermute(value, AXES, pairs)  28 us
    all_to_all x2, blocking collectives, exchange(): return lax.all_to_all(gram, AXES, 0, 0)  22.6 us
    pallas_call x4, Pallas kernels, tile_call(): pl.pallas_call(kernel, out_shape=outs, in_specs=[spec(SMEM), spec(SMEM)]...  17.4 us
    pallas_call x2, Pallas kernels, small_call(): pl.pallas_call(kernel, out_shape=outs, in_specs=[spec(SMEM)] + [spec(VMEM...  5.01 us
    pallas_call x1, Pallas kernels, split_call(): pl.pallas_call(split_kernel, out_shape=[jax.ShapeDtypeStruct((blocks, cou...  3.84 us
  transfers between devices with their start and end apart: 16, of which 11 were waited for; matrix products, arithmetic and copies ran while one was open for 0% of the time, Pallas kernels for 3%

profile of v3, /device:TPU:5, one launch (start us, length us, event | category | flops | bytes accessed | tf_op | source)
XLA Modules:
  0.0 119.2 jit_solution(6573132834267350234)
XLA Ops:
  0.6 0.0 copy-start
  0.6 0.0 copy-start.2
  0.7 0.7 collective-permute-start
  1.4 1.1 collective-permute-done.sw
  2.5 0.8 pad_maximum_fusion
  3.2 3.4 %collective-permute-start.1 = (f32[8,16,128]{2,1,0:T(8,128)S(1)}, f32[8,16,128]{2,1,0:T(8,128)S(1)}, u32[]{:S(2)}, u32[]{:S(2)}) collective-permute-start(f32[8,16,128]{2,1,0:T(8,128)S(1)} %pad_maximum_fusion), channel_id=1, source_target_pairs={{1,2},{2,1},{3,4},{4,3},{5,6},{6,5},{7,8},{8,7},{9,10},{10,9},{11,... | collective-permute-start | bytes 196616 | tf_op jit(solution)/shard_map/ppermute | solution.py:389
  6.7 2.1 %collective-permute-done.1.p1 = f32[8,16,128]{2,1,0:T(8,128)S(1)} collective-permute-done((f32[8,16,128]{2,1,0:T(8,128)S(1)}, f32[8,16,128]{2,1,0:T(8,128)S(1)}, u32[]{:S(2)}, u32[]{:S(2)}) %collective-permute-start.1) | collective-permute-done | bytes 65568 | tf_op jit(solution)/shard_map/ppermute | solution.py:389
  8.8 4.3 %collective-permute-start.2 = (f32[8,16,128]{2,1,0:T(8,128)S(1)}, f32[8,16,128]{2,1,0:T(8,128)S(1)}, u32[]{:S(2)}, u32[]{:S(2)}) collective-permute-start(f32[8,16,128]{2,1,0:T(8,128)S(1)} %collective-permute-done.1.p1), channel_id=1, source_target_pairs={{0,1},{1,0},{2,3},{3,2},{4,5},{5,4},{6,7},{7,6},{8,9},{9,8},{10,11... | collective-permute-start | bytes 196616 | tf_op jit(solution)/shard_map/ppermute | solution.py:389
  13.1 1.9 %collective-permute-start.3 = (f32[4,16,128]{2,1,0:T(8,128)}, f32[4,16,128]{2,1,0:T(8,128)S(1)}, u32[]{:S(2)}, u32[]{:S(2)}) collective-permute-start(f32[4,16,128]{2,1,0:T(8,128)} %right.5), channel_id=1, source_target_pairs={{1,4},{3,6},{4,1},{5,8},{6,3},{7,10},{8,5},{9,12},{10,7},{11,14},{... | collective-permute-start | bytes 98312 | tf_op jit(solution)/shard_map/ppermute | solution.py:389
  15.7 0.0 copy-start.1
  15.7 0.9 copy-done.1
  16.6 3.8 %shard_map.68 = (bf16[4,16,256,256]{3,2,1,0:T(8,128)(2,1)S(1)}, bf16[4,256,128]{2,1,0:T(8,128)(2,1)S(1)}) custom-call(f32[4,32,128,128]{3,2,1,0:T(8,128)} %tiles_hbm.1, f32[4,128,128]{2,1,0:T(8,128)S(1)} %copy-done.1), custom_call_target="tpu_custom_call" | custom-call | bytes 12582912 | tf_op jit(solution)/shard_map/pallas_call | solution.py:139
  20.5 0.0 collective-permute-done.3.p3
  20.5 0.0 collective-permute-done.2.p2
  20.5 0.0 copy-done
  20.5 0.0 copy-done.2
  20.5 3.5 %shard_map.69 = (f32[3,4,16,128]{3,2,1,0:T(8,128)S(1)}, f32[4,16,128]{2,1,0:T(8,128)S(1)}) custom-call(s32[4,32]{1,0:T(4,128)S(1)} %copy-done.2, s32[1]{0:T(128)S(6)} %copy.7.lost_ref, bf16[4,16,256,256]{3,2,1,0:T(8,128)(2,1)S(1)} %get-tuple-element.17.split, f32[4,16,128]{2,1,0:T(8,128)S(1)} %copy-done, f32[4,16,128]{2,1,0:T(8,128)S(1)} %collective-permute-done.sw, ...), custom_call_target="tpu_custom_call" | custom-call | tf_op jit(solution)/shard_map/pallas_call | solution.py:272
  24.0 1.2 collective-permute-start.4
  25.2 0.9 collective-permute-done.4.sw
  26.0 5.2 %collective-permute-start.5 = (f32[8,16,128]{2,1,0:T(8,128)S(1)}, f32[8,16,128]{2,1,0:T(8,128)S(1)}, u32[]{:S(2)}, u32[]{:S(2)}) collective-permute-start(f32[8,16,128]{2,1,0:T(8,128)S(1)} %pad_maximum_fusion.1), channel_id=1, source_target_pairs={{1,2},{2,1},{3,4},{4,3},{5,6},{6,5},{7,8},{8,7},{9,10},{10,9},{11,... | collective-permute-start | bytes 196616 | tf_op jit(solution)/shard_map/ppermute | solution.py:389
  31.3 1.9 %collective-permute-done.5.p1 = f32[8,16,128]{2,1,0:T(8,128)S(1)} collective-permute-done((f32[8,16,128]{2,1,0:T(8,128)S(1)}, f32[8,16,128]{2,1,0:T(8,128)S(1)}, u32[]{:S(2)}, u32[]{:S(2)}) %collective-permute-start.5) | collective-permute-done | bytes 65568 | tf_op jit(solution)/shard_map/ppermute | solution.py:389
  33.2 2.9 %collective-permute-start.6 = (f32[8,16,128]{2,1,0:T(8,128)S(1)}, f32[8,16,128]{2,1,0:T(8,128)S(1)}, u32[]{:S(2)}, u32[]{:S(2)}) collective-permute-start(f32[8,16,128]{2,1,0:T(8,128)S(1)} %collective-permute-done.5.p1), channel_id=1, source_target_pairs={{0,1},{1,0},{2,3},{3,2},{4,5},{5,4},{6,7},{7,6},{8,9},{9,8},{10,11... | collective-permute-start | bytes 196616 | tf_op jit(solution)/shard_map/ppermute | solution.py:389
  36.1 1.9 %collective-permute-start.7 = (f32[4,16,128]{2,1,0:T(8,128)S(1)}, f32[4,16,128]{2,1,0:T(8,128)S(1)}, u32[]{:S(2)}, u32[]{:S(2)}) collective-permute-start(f32[4,16,128]{2,1,0:T(8,128)S(1)} %get-tuple-element.18.v.image), channel_id=1, source_target_pairs={{1,4},{3,6},{4,1},{5,8},{6,3},{7,10},{8,5},{9,12},{10,7},{11,14},{... | collective-permute-start | bytes 98312 | tf_op jit(solution)/shard_map/ppermute | solution.py:389
  38.0 4.2 %collective-permute-done.7.p3 = f32[4,16,128]{2,1,0:T(8,128)S(1)} collective-permute-done((f32[4,16,128]{2,1,0:T(8,128)S(1)}, f32[4,16,128]{2,1,0:T(8,128)S(1)}, u32[]{:S(2)}, u32[]{:S(2)}) %collective-permute-start.7) | collective-permute-done | bytes 32800 | tf_op jit(solution)/shard_map/ppermute | solution.py:389
  42.3 0.0 collective-permute-done.6.p2
  42.3 4.2 %shard_map.70 = (f32[3,4,16,128]{3,2,1,0:T(8,128)S(1)}, f32[32,8,128]{2,1,0:T(8,128)S(1)}) custom-call(s32[4,32]{1,0:T(4,128)S(1)} %copy-done.2, s32[1]{0:T(128)S(6)} %copy.7.lost_ref, bf16[4,16,256,256]{3,2,1,0:T(8,128)(2,1)S(1)} %get-tuple-element.17.split, f32[4,16,128]{2,1,0:T(8,128)S(1)} %copy-done, f32[4,16,128]{2,1,0:T(8,128)S(1)} %get-tuple-element.18.v.image, ...), custom_call_target="tpu_custom_call" | custom-call | tf_op jit(solution)/shard_map/pallas_call | solution.py:272
  46.5 12.0 %all_to_all.10.gathered = f32[32,8,128]{2,1,0:T(8,128)S(1)} all-to-all(f32[32,8,128]{2,1,0:T(8,128)S(1)} %get-tuple-element.19), channel_id=1, replica_groups=mesh['grp'=4,'row'=8] {'grp','row'}, dimensions={0} | all-to-all | bytes 262144 | tf_op jit(solution)/shard_map/all_to_all | solution.py:402
  58.4 2.3 %shard_map.71 = (f32[4,16,128]{2,1,0:T(8,128)S(1)}, f32[4,16,128]{2,1,0:T(8,128)S(1)}, f32[4,16,128]{2,1,0:T(8,128)S(1)}, f32[4,16,128]{2,1,0:T(8,128)S(1)}) custom-call(s32[1]{0:T(128)S(6)} %copy.7.lost_ref, f32[32,8,128]{2,1,0:T(8,128)S(1)} %all_to_all.10.gathered, f32[4,16,128]{2,1,0:T(8,128)S(1)} %copy-done, ...), custom_call_target="tpu_custom_call" | custom-call | tf_op jit(solution)/shard_map/pallas_call | solution.py:378
  60.7 0.6 collective-permute-start.8
  61.3 0.9 collective-permute-done.8.sw
  62.2 2.1 %collective-permute-start.9 = (f32[8,16,128]{2,1,0:T(8,128)S(1)}, f32[8,16,128]{2,1,0:T(8,128)S(1)}, u32[]{:S(2)}, u32[]{:S(2)}) collective-permute-start(f32[8,16,128]{2,1,0:T(8,128)S(1)} %pad_maximum_fusion.2), channel_id=1, source_target_pairs={{1,2},{2,1},{3,4},{4,3},{5,6},{6,5},{7,8},{8,7},{9,10},{10,9},{11,... | collective-permute-start | bytes 196616 | tf_op jit(solution)/shard_map/ppermute | solution.py:389
  64.3 3.5 %collective-permute-done.9.p1 = f32[8,16,128]{2,1,0:T(8,128)S(1)} collective-permute-done((f32[8,16,128]{2,1,0:T(8,128)S(1)}, f32[8,16,128]{2,1,0:T(8,128)S(1)}, u32[]{:S(2)}, u32[]{:S(2)}) %collective-permute-start.9) | collective-permute-done | bytes 65568 | tf_op jit(solution)/shard_map/ppermute | solution.py:389
  67.7 3.9 %collective-permute-start.10 = (f32[8,16,128]{2,1,0:T(8,128)S(1)}, f32[8,16,128]{2,1,0:T(8,128)S(1)}, u32[]{:S(2)}, u32[]{:S(2)}) collective-permute-start(f32[8,16,128]{2,1,0:T(8,128)S(1)} %collective-permute-done.9.p1), channel_id=1, source_target_pairs={{0,1},{1,0},{2,3},{3,2},{4,5},{5,4},{6,7},{7,6},{8,9},{9,8},{10,11... | collective-permute-start | bytes 196616 | tf_op jit(solution)/shard_map/ppermute | solution.py:389
  71.7 1.9 %collective-permute-start.11 = (f32[4,16,128]{2,1,0:T(8,128)S(1)}, f32[4,16,128]{2,1,0:T(8,128)S(1)}, u32[]{:S(2)}, u32[]{:S(2)}) collective-permute-start(f32[4,16,128]{2,1,0:T(8,128)S(1)} %get-tuple-element.24.v.head), channel_id=1, source_target_pairs={{1,4},{3,6},{4,1},{5,8},{6,3},{7,10},{8,5},{9,12},{10,7},{11,14},{... | collective-permute-start | bytes 98312 | tf_op jit(solution)/shard_map/ppermute | solution.py:389
  73.6 4.2 %collective-permute-done.11.p3 = f32[4,16,128]{2,1,0:T(8,128)S(1)} collective-permute-done((f32[4,16,128]{2,1,0:T(8,128)S(1)}, f32[4,16,128]{2,1,0:T(8,128)S(1)}, u32[]{:S(2)}, u32[]{:S(2)}) %collective-permute-start.11) | collective-permute-done | bytes 32800 | tf_op jit(solution)/shard_map/ppermute | solution.py:389
  77.8 0.0 collective-permute-done.10.p2
  77.8 5.7 %shard_map.72 = (f32[4,16,128]{2,1,0:T(8,128)S(1)}, f32[4,16,128]{2,1,0:T(8,128)S(1)}, f32[4,16,128]{2,1,0:T(8,128)S(1)}) custom-call(s32[4,32]{1,0:T(4,128)S(1)} %copy-done.2, s32[1]{0:T(128)S(6)} %copy.7.lost_ref, bf16[4,16,256,256]{3,2,1,0:T(8,128)(2,1)S(1)} %get-tuple-element.17.split, bf16[4,256,128]{2,1,0:T(8,128)(2,1)S(1)} %get-tuple-element.22.precond, ...), custom_call_target="tpu_custom_call" | custom-call | tf_op jit(solution)/shard_map/pallas_call | solution.py:272
  83.5 1.9 %collective-permute-start.12 = (f32[4,16,128]{2,1,0:T(8,128)S(1)}, f32[4,16,128]{2,1,0:T(8,128)S(1)}, u32[]{:S(2)}, u32[]{:S(2)}) collective-permute-start(f32[4,16,128]{2,1,0:T(8,128)S(1)} %get-tuple-element.26.v.smooth), channel_id=1, source_target_pairs={{0,1},{1,0},{2,3},{3,2},{4,5},{5,4},{6,7},{7,6},{8,9},{9,8},{10,11... | collective-permute-start | bytes 98312 | tf_op jit(solution)/shard_map/ppermute | solution.py:389
  85.4 0.9 collective-permute-done.12.sw
  86.3 1.9 %collective-permute-start.13 = (f32[8,16,128]{2,1,0:T(8,128)S(1)}, f32[8,16,128]{2,1,0:T(8,128)S(1)}, u32[]{:S(2)}, u32[]{:S(2)}) collective-permute-start(f32[8,16,128]{2,1,0:T(8,128)S(1)} %pad_maximum_fusion.3), channel_id=1, source_target_pairs={{1,2},{2,1},{3,4},{4,3},{5,6},{6,5},{7,8},{8,7},{9,10},{10,9},{11,... | collective-permute-start | bytes 196616 | tf_op jit(solution)/shard_map/ppermute | solution.py:389
  88.2 4.1 %collective-permute-done.13.p1 = f32[8,16,128]{2,1,0:T(8,128)S(1)} collective-permute-done((f32[8,16,128]{2,1,0:T(8,128)S(1)}, f32[8,16,128]{2,1,0:T(8,128)S(1)}, u32[]{:S(2)}, u32[]{:S(2)}) %collective-permute-start.13) | collective-permute-done | bytes 65568 | tf_op jit(solution)/shard_map/ppermute | solution.py:389
  92.3 3.5 %collective-permute-start.14 = (f32[8,16,128]{2,1,0:T(8,128)S(1)}, f32[8,16,128]{2,1,0:T(8,128)S(1)}, u32[]{:S(2)}, u32[]{:S(2)}) collective-permute-start(f32[8,16,128]{2,1,0:T(8,128)S(1)} %collective-permute-done.13.p1), channel_id=1, source_target_pairs={{0,1},{1,0},{2,3},{3,2},{4,5},{5,4},{6,7},{7,6},{8,9},{9,8},{10,11... | collective-permute-start | bytes 196616 | tf_op jit(solution)/shard_map/ppermute | solution.py:389
  95.8 1.9 %collective-permute-start.15 = (f32[4,16,128]{2,1,0:T(8,128)S(1)}, f32[4,16,128]{2,1,0:T(8,128)S(1)}, u32[]{:S(2)}, u32[]{:S(2)}) collective-permute-start(f32[4,16,128]{2,1,0:T(8,128)S(1)} %get-tuple-element.26.v.smooth), channel_id=1, source_target_pairs={{1,4},{3,6},{4,1},{5,8},{6,3},{7,10},{8,5},{9,12},{10,7},{11,14},{... | collective-permute-start | bytes 98312 | tf_op jit(solution)/shard_map/ppermute | solution.py:389
  97.7 4.2 %collective-permute-done.15.p3 = f32[4,16,128]{2,1,0:T(8,128)S(1)} collective-permute-done((f32[4,16,128]{2,1,0:T(8,128)S(1)}, f32[4,16,128]{2,1,0:T(8,128)S(1)}, u32[]{:S(2)}, u32[]{:S(2)}) %collective-permute-start.15) | collective-permute-done | bytes 32800 | tf_op jit(solution)/shard_map/ppermute | solution.py:389
  101.9 0.0 collective-permute-done.14.p2
  101.9 3.9 %shard_map.73 = (f32[4,16,128]{2,1,0:T(8,128)S(1)}, f32[32,8,128]{2,1,0:T(8,128)S(1)}) custom-call(s32[4,32]{1,0:T(4,128)S(1)} %copy-done.2, s32[1]{0:T(128)S(6)} %copy.7.lost_ref, bf16[4,16,256,256]{3,2,1,0:T(8,128)(2,1)S(1)} %get-tuple-element.17.split, f32[4,16,128]{2,1,0:T(8,128)S(1)} %get-tuple-element.23.target, ...), custom_call_target="tpu_custom_call" | custom-call | tf_op jit(solution)/shard_map/pallas_call | solution.py:272
  105.8 10.6 %all_to_all.11.gathered = f32[32,8,128]{2,1,0:T(8,128)S(1)} all-to-all(f32[32,8,128]{2,1,0:T(8,128)S(1)} %get-tuple-element.27), channel_id=1, replica_groups=mesh['grp'=4,'row'=8] {'grp','row'}, dimensions={0} | all-to-all | bytes 262144 | tf_op jit(solution)/shard_map/all_to_all | solution.py:402
  116.5 2.7 %shard_map.74 = (f32[4,16,128]{2,1,0:T(8,128)}, f32[4,16,128]{2,1,0:T(8,128)}) custom-call(s32[1]{0:T(128)S(6)} %copy.7.lost_ref, f32[32,8,128]{2,1,0:T(8,128)S(1)} %all_to_all.11.gathered, f32[4,16,128]{2,1,0:T(8,128)S(1)} %copy-done, f32[4,16,128]{2,1,0:T(8,128)S(1)} %get-tuple-element.28.solution, f32[4,16,128]{2,1,0:T(8,128)S(1)} %get-tuple-element.29.kept, ...), custom_call_target="tpu_custom_call" | custom-call | tf_op jit(solution)/shard_map/pallas_call | solution.py:378
  (3 shorter events, 0.0 us)
Async XLA Ops:
  0.6 19.8 %copy-start = (f32[4,16,128]{2,1,0:T(8,128)S(1)}, f32[4,16,128]{2,1,0:T(8,128)}, u32[]{:S(2)}) copy-start(f32[4,16,128]{2,1,0:T(8,128)} %right.5) | copy-start | bytes 98308
  0.6 19.8 %copy-start.2 = (s32[4,32]{1,0:T(4,128)S(1)}, s32[4,32]{1,0:T(4,128)}, u32[]{:S(2)}) copy-start(s32[4,32]{1,0:T(4,128)} %columns_ref.7) | copy-start | bytes 1540
  0.7 1.8 %collective-permute-start = (f32[4,16,128]{2,1,0:T(8,128)}, f32[4,16,128]{2,1,0:T(8,128)S(1)}, u32[]{:S(2)}, u32[]{:S(2)}) collective-permute-start(f32[4,16,128]{2,1,0:T(8,128)} %right.5), channel_id=1, source_target_pairs={{0,1},{1,0},{2,3},{3,2},{4,5},{5,4},{6,7},{7,6},{8,9},{9,8},{10,11... | collective-permute-start | bytes 98312 | tf_op jit(solution)/shard_map/ppermute | solution.py:389
  3.2 5.6 %collective-permute-start.1 = (f32[8,16,128]{2,1,0:T(8,128)S(1)}, f32[8,16,128]{2,1,0:T(8,128)S(1)}, u32[]{:S(2)}, u32[]{:S(2)}) collective-permute-start(f32[8,16,128]{2,1,0:T(8,128)S(1)} %pad_maximum_fusion), channel_id=1, source_target_pairs={{1,2},{2,1},{3,4},{4,3},{5,6},{6,5},{7,8},{8,7},{9,10},{10,9},{11,... | collective-permute-start | bytes 196616 | tf_op jit(solution)/shard_map/ppermute | solution.py:389
  8.8 11.7 %collective-permute-start.2 = (f32[8,16,128]{2,1,0:T(8,128)S(1)}, f32[8,16,128]{2,1,0:T(8,128)S(1)}, u32[]{:S(2)}, u32[]{:S(2)}) collective-permute-start(f32[8,16,128]{2,1,0:T(8,128)S(1)} %collective-permute-done.1.p1), channel_id=1, source_target_pairs={{0,1},{1,0},{2,3},{3,2},{4,5},{5,4},{6,7},{7,6},{8,9},{9,8},{10,11... | collective-permute-start | bytes 196616 | tf_op jit(solution)/shard_map/ppermute | solution.py:389
  13.1 7.4 %collective-permute-start.3 = (f32[4,16,128]{2,1,0:T(8,128)}, f32[4,16,128]{2,1,0:T(8,128)S(1)}, u32[]{:S(2)}, u32[]{:S(2)}) collective-permute-start(f32[4,16,128]{2,1,0:T(8,128)} %right.5), channel_id=1, source_target_pairs={{1,4},{3,6},{4,1},{5,8},{6,3},{7,10},{8,5},{9,12},{10,7},{11,14},{... | collective-permute-start | bytes 98312 | tf_op jit(solution)/shard_map/ppermute | solution.py:389
  15.7 1.0 copy-start.1
  24.0 2.0 %collective-permute-start.4 = (f32[4,16,128]{2,1,0:T(8,128)S(1)}, f32[4,16,128]{2,1,0:T(8,128)S(1)}, u32[]{:S(2)}, u32[]{:S(2)}) collective-permute-start(f32[4,16,128]{2,1,0:T(8,128)S(1)} %get-tuple-element.18.v.image), channel_id=1, source_target_pairs={{0,1},{1,0},{2,3},{3,2},{4,5},{5,4},{6,7},{7,6},{8,9},{9,8},{10,11... | collective-permute-start | bytes 98312 | tf_op jit(solution)/shard_map/ppermute | solution.py:389
  26.0 7.2 %collective-permute-start.5 = (f32[8,16,128]{2,1,0:T(8,128)S(1)}, f32[8,16,128]{2,1,0:T(8,128)S(1)}, u32[]{:S(2)}, u32[]{:S(2)}) collective-permute-start(f32[8,16,128]{2,1,0:T(8,128)S(1)} %pad_maximum_fusion.1), channel_id=1, source_target_pairs={{1,2},{2,1},{3,4},{4,3},{5,6},{6,5},{7,8},{8,7},{9,10},{10,9},{11,... | collective-permute-start | bytes 196616 | tf_op jit(solution)/shard_map/ppermute | solution.py:389
  33.2 9.0 %collective-permute-start.6 = (f32[8,16,128]{2,1,0:T(8,128)S(1)}, f32[8,16,128]{2,1,0:T(8,128)S(1)}, u32[]{:S(2)}, u32[]{:S(2)}) collective-permute-start(f32[8,16,128]{2,1,0:T(8,128)S(1)} %collective-permute-done.5.p1), channel_id=1, source_target_pairs={{0,1},{1,0},{2,3},{3,2},{4,5},{5,4},{6,7},{7,6},{8,9},{9,8},{10,11... | collective-permute-start | bytes 196616 | tf_op jit(solution)/shard_map/ppermute | solution.py:389
  36.1 6.1 %collective-permute-start.7 = (f32[4,16,128]{2,1,0:T(8,128)S(1)}, f32[4,16,128]{2,1,0:T(8,128)S(1)}, u32[]{:S(2)}, u32[]{:S(2)}) collective-permute-start(f32[4,16,128]{2,1,0:T(8,128)S(1)} %get-tuple-element.18.v.image), channel_id=1, source_target_pairs={{1,4},{3,6},{4,1},{5,8},{6,3},{7,10},{8,5},{9,12},{10,7},{11,14},{... | collective-permute-start | bytes 98312 | tf_op jit(solution)/shard_map/ppermute | solution.py:389
  60.7 1.4 %collective-permute-start.8 = (f32[4,16,128]{2,1,0:T(8,128)S(1)}, f32[4,16,128]{2,1,0:T(8,128)S(1)}, u32[]{:S(2)}, u32[]{:S(2)}) collective-permute-start(f32[4,16,128]{2,1,0:T(8,128)S(1)} %get-tuple-element.24.v.head), channel_id=1, source_target_pairs={{0,1},{1,0},{2,3},{3,2},{4,5},{5,4},{6,7},{7,6},{8,9},{9,8},{10,11... | collective-permute-start | bytes 98312 | tf_op jit(solution)/shard_map/ppermute | solution.py:389
  62.2 5.6 %collective-permute-start.9 = (f32[8,16,128]{2,1,0:T(8,128)S(1)}, f32[8,16,128]{2,1,0:T(8,128)S(1)}, u32[]{:S(2)}, u32[]{:S(2)}) collective-permute-start(f32[8,16,128]{2,1,0:T(8,128)S(1)} %pad_maximum_fusion.2), channel_id=1, source_target_pairs={{1,2},{2,1},{3,4},{4,3},{5,6},{6,5},{7,8},{8,7},{9,10},{10,9},{11,... | collective-permute-start | bytes 196616 | tf_op jit(solution)/shard_map/ppermute | solution.py:389
  67.7 10.1 %collective-permute-start.10 = (f32[8,16,128]{2,1,0:T(8,128)S(1)}, f32[8,16,128]{2,1,0:T(8,128)S(1)}, u32[]{:S(2)}, u32[]{:S(2)}) collective-permute-start(f32[8,16,128]{2,1,0:T(8,128)S(1)} %collective-permute-done.9.p1), channel_id=1, source_target_pairs={{0,1},{1,0},{2,3},{3,2},{4,5},{5,4},{6,7},{7,6},{8,9},{9,8},{10,11... | collective-permute-start | bytes 196616 | tf_op jit(solution)/shard_map/ppermute | solution.py:389
  71.7 6.1 %collective-permute-start.11 = (f32[4,16,128]{2,1,0:T(8,128)S(1)}, f32[4,16,128]{2,1,0:T(8,128)S(1)}, u32[]{:S(2)}, u32[]{:S(2)}) collective-permute-start(f32[4,16,128]{2,1,0:T(8,128)S(1)} %get-tuple-element.24.v.head), channel_id=1, source_target_pairs={{1,4},{3,6},{4,1},{5,8},{6,3},{7,10},{8,5},{9,12},{10,7},{11,14},{... | collective-permute-start | bytes 98312 | tf_op jit(solution)/shard_map/ppermute | solution.py:389
  83.5 2.7 %collective-permute-start.12 = (f32[4,16,128]{2,1,0:T(8,128)S(1)}, f32[4,16,128]{2,1,0:T(8,128)S(1)}, u32[]{:S(2)}, u32[]{:S(2)}) collective-permute-start(f32[4,16,128]{2,1,0:T(8,128)S(1)} %get-tuple-element.26.v.smooth), channel_id=1, source_target_pairs={{0,1},{1,0},{2,3},{3,2},{4,5},{5,4},{6,7},{7,6},{8,9},{9,8},{10,11... | collective-permute-start | bytes 98312 | tf_op jit(solution)/shard_map/ppermute | solution.py:389
  86.3 6.1 %collective-permute-start.13 = (f32[8,16,128]{2,1,0:T(8,128)S(1)}, f32[8,16,128]{2,1,0:T(8,128)S(1)}, u32[]{:S(2)}, u32[]{:S(2)}) collective-permute-start(f32[8,16,128]{2,1,0:T(8,128)S(1)} %pad_maximum_fusion.3), channel_id=1, source_target_pairs={{1,2},{2,1},{3,4},{4,3},{5,6},{6,5},{7,8},{8,7},{9,10},{10,9},{11,... | collective-permute-start | bytes 196616 | tf_op jit(solution)/shard_map/ppermute | solution.py:389
  92.3 9.6 %collective-permute-start.14 = (f32[8,16,128]{2,1,0:T(8,128)S(1)}, f32[8,16,128]{2,1,0:T(8,128)S(1)}, u32[]{:S(2)}, u32[]{:S(2)}) collective-permute-start(f32[8,16,128]{2,1,0:T(8,128)S(1)} %collective-permute-done.13.p1), channel_id=1, source_target_pairs={{0,1},{1,0},{2,3},{3,2},{4,5},{5,4},{6,7},{7,6},{8,9},{9,8},{10,11... | collective-permute-start | bytes 196616 | tf_op jit(solution)/shard_map/ppermute | solution.py:389
  95.8 6.1 %collective-permute-start.15 = (f32[4,16,128]{2,1,0:T(8,128)S(1)}, f32[4,16,128]{2,1,0:T(8,128)S(1)}, u32[]{:S(2)}, u32[]{:S(2)}) collective-permute-start(f32[4,16,128]{2,1,0:T(8,128)S(1)} %get-tuple-element.26.v.smooth), channel_id=1, source_target_pairs={{1,4},{3,6},{4,1},{5,8},{6,3},{7,10},{8,5},{9,12},{10,7},{11,14},{... | collective-permute-start | bytes 98312 | tf_op jit(solution)/shard_map/ppermute | solution.py:389

commit v4 on v3

--- a/solution.py
+++ b/solution.py
@@ -9,6 +9,7 @@
 BAND = 12
 OFFSETS = (0, 1, -1, -2, 2, 3, -3)
 REACH = 3
+OWN, LOST, ELSE = range(3)
 SLOTS = len(OFFSETS)
 HIGHEST = lax.Precision.HIGHEST
 AXES = ("grp", "row")
@@ -50,19 +51,30 @@
     return high, middle, low
 
 
-def build_table(pieces, place, table_ref, classes, blocks, cols):
-    slot = 0
-    for piece in pieces:
-        for first in range(0, piece.shape[0], blocks):
-            position, flags = place.slot(slot)
-            for block in range(blocks):
-                value = piece[first + block]
-                for k in range(classes):
-                    terms = split3(value * flags[k])
-                    for s, term in enumerate(terms):
-                        rows = pl.ds((3 * k + s) * cols, cols)
-                        table_ref[position * blocks + block, rows, :] = term
-            slot += 1
+def build_table(pieces, place, table_ref, classes, blocks, cols, start=0):
+    for slot, (piece, first) in enumerate(pieces):
+        position, flags = place.slot(slot)
+        for block in range(blocks):
+            entry = position * blocks + block
+            value = None if piece is None else piece[first + block]
+            for k, name in enumerate(classes):
+                base = 3 * (start + k) * cols
+                if piece is None:
+                    table_ref[entry, base : base + 3 * cols, :] = jnp.zeros(
+                        (3 * cols, table_ref.shape[2]), jnp.bfloat16
+                    )
+                    continue
+                for s, term in enumerate(split3(value * flags[name])):
+                    table_ref[entry, base + s * cols : base + (s + 1) * cols, :] = term
+
+
+def slots(v, sw, near, other, far, blocks, skip=0):
+    first = 2 * skip * blocks
+    here = (v, sw) if skip == 0 else (None, None)
+    return (
+        (here[0], 0), (here[1], 0), (near, first), (near, first + blocks),
+        (other, first), (other, first + blocks), (far, skip * blocks),
+    )
 
 
 class Place:
@@ -95,7 +107,7 @@
             [table_ref[columns_ref[row, 2 * pair + j] - base] for j in (0, 1)], axis=1
         )
         part = lax.dot_general(
-            left, split_ref[row, pair], (((1,), (1,)), ((), ())),
+            left, split_ref[row, pair], (((1,), (0,)), ((), ())),
             preferred_element_type=jnp.float32,
         )
         total = part if total is None else total + part
@@ -111,27 +123,39 @@
     return out
 
 
-def split_kernel(tiles_hbm, precond, split, halves, tiles, sems):
+def split_kernel(tiles_hbm, precond_hbm, split, halves, tiles, precond, sems):
     blocks, count, tb, _ = tiles.shape
+    rows, columns = grid16(2 * tb)
+    unit = (rows == columns).astype(jnp.bfloat16)
     copies = [
         pltpu.make_async_copy(tiles_hbm.at[row], tiles.at[row], sems.at[row])
         for row in range(blocks)
     ]
     for copy in copies:
         copy.start()
+    last = pltpu.make_async_copy(precond_hbm, precond, sems.at[blocks])
+    last.start()
+    for row in range(blocks):
+        copies[row].wait()
+        for pair in range(count // 2):
+            highs, rests = [], []
+            for k in (2 * pair, 2 * pair + 1):
+                tile = tiles[row, k]
+                high = tile.astype(jnp.bfloat16)
+                highs.append(high)
+                rests.append((tile - high.astype(jnp.float32)).astype(jnp.bfloat16))
+            both = jnp.concatenate(
+                [jnp.concatenate(highs, axis=1), jnp.concatenate(rests, axis=1)], axis=0
+            )
+            turned = lax.dot_general(
+                unit, both, (((1,), (1,)), ((), ())), preferred_element_type=jnp.float32
+            )
+            split[row, pair] = turned.astype(jnp.bfloat16)
+    last.wait()
     for row in range(blocks):
         high = precond[row].astype(jnp.bfloat16)
         halves[row, 0:tb] = high
         halves[row, tb : 2 * tb] = (precond[row] - high.astype(jnp.float32)).astype(jnp.bfloat16)
-    for row in range(blocks):
-        copies[row].wait()
-        for k in range(count):
-            tile = tiles[row, k]
-            high = tile.astype(jnp.bfloat16)
-            rest = (tile - high.astype(jnp.float32)).astype(jnp.bfloat16)
-            side = (k % 2) * tb
-            split[row, k // 2, 0:tb, side : side + tb] = high
-            split[row, k // 2, tb : 2 * tb, side : side + tb] = rest
 
 
 def split_call(tiles, precond):
@@ -142,12 +166,16 @@
             jax.ShapeDtypeStruct((blocks, count // 2, 2 * tb, 2 * tb), jnp.bfloat16),
             jax.ShapeDtypeStruct((blocks, 2 * tb, tb), jnp.bfloat16),
         ],
-        in_specs=[spec(pltpu.HBM), spec(VMEM)],
+        in_specs=[spec(pltpu.HBM)] * 2,
         out_specs=[spec(VMEM)] * 2,
-        scratch_shapes=[VMEM(tiles.shape, jnp.float32), pltpu.SemaphoreType.DMA((blocks,))],
+        scratch_shapes=[
+            VMEM(tiles.shape, jnp.float32),
+            VMEM(precond.shape, jnp.float32),
+            pltpu.SemaphoreType.DMA((blocks + 1,)),
+        ],
         compiler_params=params(24),
         cost_estimate=pl.CostEstimate(flops=0, bytes_accessed=12 * tiles.size // 2, transcendentals=0),
-    )(pltpu.with_memory_space_constraint(tiles, pltpu.HBM), precond)
+    )(*(pltpu.with_memory_space_constraint(array, pltpu.HBM) for array in (tiles, precond)))
 
 
 def smoothed(value, halves, cols, tb):
@@ -208,7 +236,7 @@
     blocks, cols, _ = v.shape
     place = Place(lost_ref)
     base = place.base(blocks)
-    build_table((v, sw, p1, p2, p3), place, table, 3, blocks, cols)
+    build_table(slots(v, sw, p1, p2, p3, blocks), place, table, (OWN, LOST, ELSE), blocks, cols)
     for row in range(blocks):
         out = row_product(columns_ref, base, table, split, row, 3, cols)
         for k in range(3):
@@ -222,7 +250,7 @@
     blocks, cols, _ = v.shape
     place = Place(lost_ref)
     base = place.base(blocks)
-    build_table((v, sw, p1, p2, p3), place, table, 3, blocks, cols)
+    build_table(slots(v, sw, p1, p2, p3, blocks), place, table, (OWN, LOST, ELSE), blocks, cols)
     for row in range(blocks):
         out = row_product(columns_ref, base, table, split, row, 3, cols)
         for k in range(3):
@@ -234,40 +262,40 @@
 
 
 def third_kernel(
-    columns_ref, lost_ref, split, precond, v, sw, p1, p2, p3, applied, smooth, lost, table
+    columns_ref, lost_ref, split, halves, v, sw, p1, p2, p3, applied, smooth, table
 ):
-    blocks, cols, _ = v.shape
+    blocks, cols, tb = v.shape
     place = Place(lost_ref)
     base = place.base(blocks)
-    build_table((v, sw, p1, p2, p3), place, table, 2, blocks, cols)
-    mine = place.mine
-    for row in range(blocks):
-        out = row_product(columns_ref, base, table, split, row, 2, cols)
-        applied[row] = out[0]
-        lost[row] = out[0] * mine + out[1]
-        smooth[row] = smoothed(out[0], precond[row], cols, v.shape[2])
+    build_table(slots(v, sw, p1, p2, p3, blocks), place, table, (OWN,), blocks, cols)
+    for row in range(blocks):
+        (applied[row],) = row_product(columns_ref, base, table, split, row, 1, cols)
+    for row in range(blocks):
+        smooth[row] = smoothed(applied[row], halves[row], cols, tb)
 
 
 def fourth_kernel(
-    columns_ref, lost_ref, split, target, head, applied, v, sw, p1, p2, p3, lost, gram,
+    columns_ref, lost_ref, split, target, head, applied, v, sw, p1, p2, p3, lost0, lost1, gram,
     table, second,
 ):
     blocks, cols, _ = v.shape
     place = Place(lost_ref)
     base = place.base(blocks)
-    build_table((v, sw, p1, p2, p3), place, table, 2, blocks, cols)
     mine = place.mine
-    for row in range(blocks):
-        out = row_product(columns_ref, base, table, split, row, 2, cols)
+    build_table(slots(v, sw, p1, p2, p3, blocks), place, table, (OWN, LOST), blocks, cols)
+    build_table(slots(v, sw, p1, p2, p3, blocks, 1), place, table, (LOST,), blocks, cols, 2)
+    for row in range(blocks):
+        out = row_product(columns_ref, base, table, split, row, 3, cols)
         second[row] = out[0]
-        lost[row] = out[0] * mine + out[1]
+        lost1[row] = out[0] * mine + out[1]
+        lost0[row] = applied[row] * mine + out[2]
     former = jnp.concatenate([lanes(head), lanes(v)], axis=0)
     latter = jnp.concatenate([lanes(target), lanes(applied), lanes(second)], axis=0)
     pack_gram(gram, former, latter, mine, cols)
 
 
 def tile_call(kernel, classes, outs, extra, split, operands_vmem, columns, lost):
-    blocks, cols, tb = operands_vmem[-1].shape
+    blocks, cols, tb = operands_vmem[-5].shape
     scratch = [VMEM((SLOTS * blocks, 3 * classes * cols, tb), jnp.bfloat16)] + extra
     return pl.pallas_call(
         kernel,
@@ -384,17 +412,22 @@
     )(lost, gathered, *arrays)
 
 
-def move(value, total, where):
+def move(value, where, inside=False):
+    rows = lax.axis_size("row")
+    total = rows * lax.axis_size("grp")
     pairs = [(i, where(i)) for i in range(total) if 0 <= where(i) < total]
+    if inside:
+        pairs = [(i, j) for i, j in pairs if i // rows == j // rows]
     return lax.ppermute(value, AXES, pairs)
 
 
-def window(value, total):
-    swapped = move(value, total, lambda i: i ^ 1)
-    pair = jnp.concatenate([value, swapped], axis=0)
-    near = move(pair, total, lambda i: i - 1 if i % 2 == 0 else i + 1)
-    far = move(value, total, lambda i: i - 3 if i % 2 == 0 else i + 3)
-    other = move(near, total, lambda i: i ^ 1)
+def window(value, inside=False, along=()):
+    swapped = move(value, lambda i: i ^ 1)
+    pair = jnp.concatenate([value, swapped, *along], axis=0)
+    alone = jnp.concatenate([value, along[0]], axis=0) if along else value
+    near = move(pair, lambda i: i - 1 if i % 2 == 0 else i + 1, inside)
+    far = move(alone, lambda i: i - 3 if i % 2 == 0 else i + 3, inside)
+    other = move(near, lambda i: i ^ 1)
     return value, swapped, near, other, far
 
 
@@ -415,21 +448,22 @@
 
     split, halves = split_call(matrix_tiles, precond)
     parts_b, image = tile_call(
-        first_kernel, 3, [vec3, vec], [], split, window(right_side, total), column_index, lost_group
+        first_kernel, 3, [vec3, vec], [], split, window(right_side), column_index, lost_group
     )
     parts_y, gram_outer = tile_call(
         second_kernel, 3, [vec3, gram], [held], split,
-        (right_side,) + window(image, total), column_index, lost_group,
+        (right_side,) + window(image), column_index, lost_group,
     )
     solution, target, head, kept = small_call(
         outer_kernel, [vec] * 4, lost_group, exchange(gram_outer), right_side, image, parts_b, parts_y, halves
     )
-    applied, smooth, lost0 = tile_call(
-        third_kernel, 2, [vec] * 3, [], split, (halves,) + window(head, total), column_index, lost_group
-    )
-    lost1, gram_inner = tile_call(
-        fourth_kernel, 2, [vec, gram], [held], split,
-        (target, head, applied) + window(smooth, total), column_index, lost_group,
+    ahead = window(head, inside=True)
+    applied, smooth = tile_call(
+        third_kernel, 1, [vec] * 2, [], split, (halves,) + ahead, column_index, lost_group
+    )
+    lost0, lost1, gram_inner = tile_call(
+        fourth_kernel, 3, [vec, vec, gram], [held], split,
+        (target, head, applied) + window(smooth, along=ahead[:2]), column_index, lost_group,
     )
     recovered, residual = small_call(
         inner_kernel, [vec] * 2, lost_group, exchange(gram_inner), right_side, solution, kept, head, smooth,

time: 122 us -> 111 us (0.910)
  the two profiles are of different devices: /device:TPU:5 before, /device:TPU:0 now
where the time goes in v4:
time: 111 us; the launch traced here: 110 us
  blocking collectives  42.7 us (38%)
  starting transfers between devices  41 us (37%)
  Pallas kernels  20 us (18%)
  waiting for transfers between devices  4.49 us (4%)
  between operations  1.5 us (1%)
    all_to_all x2, blocking collectives, exchange(): return lax.all_to_all(gram, AXES, 0, 0)  42.7 us
    ppermute x16, starting transfers between devices, move(): return lax.ppermute(value, AXES, pairs)  41 us
    pallas_call x4, Pallas kernels, tile_call(): pl.pallas_call(kernel, out_shape=outs, in_specs=[spec(SMEM), spec(SMEM)]...  10.3 us
    pallas_call x2, Pallas kernels, small_call(): pl.pallas_call(kernel, out_shape=outs, in_specs=[spec(SMEM)] + [spec(VMEM...  5.01 us
    pallas_call x1, Pallas kernels, split_call(): pl.pallas_call(split_kernel, out_shape=[jax.ShapeDtypeStruct((blocks, cou...  4.67 us
    ppermute x16, waiting for transfers between devices, move(): return lax.ppermute(value, AXES, pairs)  4.49 us
  transfers between devices with their start and end apart: 16, of which 7 were waited for; matrix products, arithmetic and copies ran while one was open for 0% of the time, Pallas kernels for 4%

profile of v4, /device:TPU:0, one launch (start us, length us, event | category | flops | bytes accessed | tf_op | source)
XLA Modules:
  0.0 110.4 jit_solution(12938866648813867050)
XLA Ops:
  0.6 0.0 copy-start
  0.6 0.0 copy-start.1
  0.7 0.6 collective-permute-start
  1.2 1.1 collective-permute-done.sw
  2.3 0.8 pad_maximum_fusion.1
  3.0 0.7 collective-permute-start.1
  3.7 0.0 collective-permute-done.1.p1
  3.7 6.2 %collective-permute-start.2 = (f32[8,16,128]{2,1,0:T(8,128)S(1)}, f32[8,16,128]{2,1,0:T(8,128)S(1)}, u32[]{:S(2)}, u32[]{:S(2)}) collective-permute-start(f32[8,16,128]{2,1,0:T(8,128)S(1)} %collective-permute-done.1.p1), channel_id=1, source_target_pairs={{0,1},{1,0},{2,3},{3,2},{4,5},{5,4},{6,7},{7,6},{8,9},{9,8},{10,11... | collective-permute-start | bytes 196616 | tf_op jit(solution)/shard_map/ppermute | solution.py:421
  9.9 0.7 collective-permute-start.3
  11.2 4.7 %shard_map.68 = (bf16[4,16,256,256]{3,2,1,0:T(8,128)(2,1)S(1)}, bf16[4,256,128]{2,1,0:T(8,128)(2,1)S(1)}) custom-call(f32[4,32,128,128]{3,2,1,0:T(8,128)} %tiles_hbm.1, f32[4,128,128]{2,1,0:T(8,128)} %precond_hbm.1), custom_call_target="tpu_custom_call" | custom-call | bytes 12582912 | tf_op jit(solution)/shard_map/pallas_call | solution.py:163
  15.9 0.0 collective-permute-done.3.p3
  15.9 0.0 collective-permute-done.2.p2
  15.9 0.0 copy-done
  15.9 0.0 copy-done.1
  15.9 2.2 %shard_map.69 = (f32[3,4,16,128]{3,2,1,0:T(8,128)S(1)}, f32[4,16,128]{2,1,0:T(8,128)S(1)}) custom-call(s32[4,32]{1,0:T(4,128)S(1)} %copy-done.1, s32[1]{0:T(128)S(6)} %copy.7.lost_ref, bf16[4,16,256,256]{3,2,1,0:T(8,128)(2,1)S(1)} %get-tuple-element.17.split, f32[4,16,128]{2,1,0:T(8,128)S(1)} %copy-done, f32[4,16,128]{2,1,0:T(8,128)S(1)} %collective-permute-done.sw, ...), custom_call_target="tpu_custom_call" | custom-call | tf_op jit(solution)/shard_map/pallas_call | solution.py:300
  18.2 4.6 %collective-permute-start.4 = (f32[4,16,128]{2,1,0:T(8,128)S(1)}, f32[4,16,128]{2,1,0:T(8,128)S(1)}, u32[]{:S(2)}, u32[]{:S(2)}) collective-permute-start(f32[4,16,128]{2,1,0:T(8,128)S(1)} %get-tuple-element.18.v.image), channel_id=1, source_target_pairs={{0,1},{1,0},{2,3},{3,2},{4,5},{5,4},{6,7},{7,6},{8,9},{9,8},{10,11... | collective-permute-start | bytes 98312 | tf_op jit(solution)/shard_map/ppermute | solution.py:421
  22.7 0.9 collective-permute-done.4.sw
  23.6 0.7 collective-permute-start.5
  24.3 0.0 collective-permute-done.5.p1
  24.3 7.2 %collective-permute-start.6 = (f32[8,16,128]{2,1,0:T(8,128)S(1)}, f32[8,16,128]{2,1,0:T(8,128)S(1)}, u32[]{:S(2)}, u32[]{:S(2)}) collective-permute-start(f32[8,16,128]{2,1,0:T(8,128)S(1)} %collective-permute-done.5.p1), channel_id=1, source_target_pairs={{0,1},{1,0},{2,3},{3,2},{4,5},{5,4},{6,7},{7,6},{8,9},{9,8},{10,11... | collective-permute-start | bytes 196616 | tf_op jit(solution)/shard_map/ppermute | solution.py:421
  31.5 0.7 collective-permute-start.7
  32.1 0.0 collective-permute-done.7.p3
  32.1 0.2 collective-permute-done.6.p2
  32.4 2.9 %shard_map.70 = (f32[3,4,16,128]{3,2,1,0:T(8,128)S(1)}, f32[32,8,128]{2,1,0:T(8,128)S(1)}) custom-call(s32[4,32]{1,0:T(4,128)S(1)} %copy-done.1, s32[1]{0:T(128)S(6)} %copy.7.lost_ref, bf16[4,16,256,256]{3,2,1,0:T(8,128)(2,1)S(1)} %get-tuple-element.17.split, f32[4,16,128]{2,1,0:T(8,128)S(1)} %copy-done, f32[4,16,128]{2,1,0:T(8,128)S(1)} %get-tuple-element.18.v.image, ...), custom_call_target="tpu_custom_call" | custom-call | tf_op jit(solution)/shard_map/pallas_call | solution.py:300
  35.3 22.5 %all_to_all.10.gathered = f32[32,8,128]{2,1,0:T(8,128)S(1)} all-to-all(f32[32,8,128]{2,1,0:T(8,128)S(1)} %get-tuple-element.19), channel_id=1, replica_groups=mesh['grp'=4,'row'=8] {'grp','row'}, dimensions={0} | all-to-all | bytes 262144 | tf_op jit(solution)/shard_map/all_to_all | solution.py:435
  57.8 2.3 %shard_map.71 = (f32[4,16,128]{2,1,0:T(8,128)S(1)}, f32[4,16,128]{2,1,0:T(8,128)S(1)}, f32[4,16,128]{2,1,0:T(8,128)S(1)}, f32[4,16,128]{2,1,0:T(8,128)S(1)}) custom-call(s32[1]{0:T(128)S(6)} %copy.7.lost_ref, f32[32,8,128]{2,1,0:T(8,128)S(1)} %all_to_all.10.gathered, f32[4,16,128]{2,1,0:T(8,128)S(1)} %copy-done, ...), custom_call_target="tpu_custom_call" | custom-call | tf_op jit(solution)/shard_map/pallas_call | solution.py:406
  60.1 0.4 collective-permute-start.8
  60.4 0.9 collective-permute-done.8.sw
  61.3 0.7 collective-permute-start.9
  62.0 0.0 collective-permute-done.9.p1
  62.0 5.2 %collective-permute-start.10 = (f32[8,16,128]{2,1,0:T(8,128)S(1)}, f32[8,16,128]{2,1,0:T(8,128)S(1)}, u32[]{:S(2)}, u32[]{:S(2)}) collective-permute-start(f32[8,16,128]{2,1,0:T(8,128)S(1)} %collective-permute-done.9.p1), channel_id=1, source_target_pairs={{0,1},{1,0},{2,3},{3,2},{4,5},{5,4},{6,7},{7,6},{8,9},{9,8},{10,11... | collective-permute-start | bytes 196616 | tf_op jit(solution)/shard_map/ppermute | solution.py:421
  67.2 0.7 collective-permute-start.11
  67.9 0.0 collective-permute-done.11.p3
  67.9 0.2 collective-permute-done.10.p2
  68.1 2.3 %shard_map.72 = (f32[4,16,128]{2,1,0:T(8,128)S(1)}, f32[4,16,128]{2,1,0:T(8,128)S(1)}) custom-call(s32[4,32]{1,0:T(4,128)S(1)} %copy-done.1, s32[1]{0:T(128)S(6)} %copy.7.lost_ref, bf16[4,16,256,256]{3,2,1,0:T(8,128)(2,1)S(1)} %get-tuple-element.17.split, bf16[4,256,128]{2,1,0:T(8,128)(2,1)S(1)} %get-tuple-element.22.precond.halves, ...), custom_call_target="tpu_custom_call" | custom-call | tf_op jit(solution)/shard_map/pallas_call | solution.py:300
  70.5 5.7 %collective-permute-start.12 = (f32[4,16,128]{2,1,0:T(8,128)S(1)}, f32[4,16,128]{2,1,0:T(8,128)S(1)}, u32[]{:S(2)}, u32[]{:S(2)}) collective-permute-start(f32[4,16,128]{2,1,0:T(8,128)S(1)} %get-tuple-element.26.v.smooth), channel_id=1, source_target_pairs={{0,1},{1,0},{2,3},{3,2},{4,5},{5,4},{6,7},{7,6},{8,9},{9,8},{10,11... | collective-permute-start | bytes 98312 | tf_op jit(solution)/shard_map/ppermute | solution.py:421
  76.1 0.9 collective-permute-done.12.sw
  77.0 0.7 collective-permute-start.13
  77.7 0.0 collective-permute-done.13.p1
  77.7 6.0 %collective-permute-start.14 = (f32[16,16,128]{2,1,0:T(8,128)S(1)}, f32[16,16,128]{2,1,0:T(8,128)S(1)}, u32[]{:S(2)}, u32[]{:S(2)}) collective-permute-start(f32[16,16,128]{2,1,0:T(8,128)S(1)} %collective-permute-done.13.p1), channel_id=1, source_target_pairs={{0,1},{1,0},{2,3},{3,2},{4,5},{5,4},{6,7},{7,6},{8,9},{9,8},{10,11... | collective-permute-start | bytes 393224 | tf_op jit(solution)/shard_map/ppermute | solution.py:421
  83.6 0.7 collective-permute-start.15
  84.3 0.0 collective-permute-done.15.p3
  84.3 0.3 collective-permute-done.14.p2
  84.6 2.9 %shard_map.73 = (f32[4,16,128]{2,1,0:T(8,128)S(1)}, f32[4,16,128]{2,1,0:T(8,128)S(1)}, f32[32,8,128]{2,1,0:T(8,128)S(1)}) custom-call(s32[4,32]{1,0:T(4,128)S(1)} %copy-done.1, s32[1]{0:T(128)S(6)} %copy.7.lost_ref, bf16[4,16,256,256]{3,2,1,0:T(8,128)(2,1)S(1)} %get-tuple-element.17.split, f32[4,16,128]{2,1,0:T(8,128)S(1)} %get-tuple-element.23.target, ...), custom_call_target="tpu_custom_call" | custom-call | tf_op jit(solution)/shard_map/pallas_call | solution.py:300
  87.5 20.2 %all_to_all.11.gathered = f32[32,8,128]{2,1,0:T(8,128)S(1)} all-to-all(f32[32,8,128]{2,1,0:T(8,128)S(1)} %get-tuple-element.27), channel_id=1, replica_groups=mesh['grp'=4,'row'=8] {'grp','row'}, dimensions={0} | all-to-all | bytes 262144 | tf_op jit(solution)/shard_map/all_to_all | solution.py:435
  107.7 2.7 %shard_map.74 = (f32[4,16,128]{2,1,0:T(8,128)}, f32[4,16,128]{2,1,0:T(8,128)}) custom-call(s32[1]{0:T(128)S(6)} %copy.7.lost_ref, f32[32,8,128]{2,1,0:T(8,128)S(1)} %all_to_all.11.gathered, f32[4,16,128]{2,1,0:T(8,128)S(1)} %copy-done, f32[4,16,128]{2,1,0:T(8,128)S(1)} %get-tuple-element.28.solution, f32[4,16,128]{2,1,0:T(8,128)S(1)} %get-tuple-element.29.kept, ...), custom_call_target="tpu_custom_call" | custom-call | tf_op jit(solution)/shard_map/pallas_call | solution.py:406
  (4 shorter events, 0.0 us)
Async XLA Ops:
  0.6 15.3 %copy-start = (f32[4,16,128]{2,1,0:T(8,128)S(1)}, f32[4,16,128]{2,1,0:T(8,128)}, u32[]{:S(2)}) copy-start(f32[4,16,128]{2,1,0:T(8,128)} %right.5) | copy-start | bytes 98308
  0.6 15.3 %copy-start.1 = (s32[4,32]{1,0:T(4,128)S(1)}, s32[4,32]{1,0:T(4,128)}, u32[]{:S(2)}) copy-start(s32[4,32]{1,0:T(4,128)} %columns_ref.7) | copy-start | bytes 1540
  0.7 1.6 %collective-permute-start = (f32[4,16,128]{2,1,0:T(8,128)}, f32[4,16,128]{2,1,0:T(8,128)S(1)}, u32[]{:S(2)}, u32[]{:S(2)}) collective-permute-start(f32[4,16,128]{2,1,0:T(8,128)} %right.5), channel_id=1, source_target_pairs={{0,1},{1,0},{2,3},{3,2},{4,5},{5,4},{6,7},{7,6},{8,9},{9,8},{10,11... | collective-permute-start | bytes 98312 | tf_op jit(solution)/shard_map/ppermute | solution.py:421
  3.0 0.7 collective-permute-start.1
  3.7 12.2 %collective-permute-start.2 = (f32[8,16,128]{2,1,0:T(8,128)S(1)}, f32[8,16,128]{2,1,0:T(8,128)S(1)}, u32[]{:S(2)}, u32[]{:S(2)}) collective-permute-start(f32[8,16,128]{2,1,0:T(8,128)S(1)} %collective-permute-done.1.p1), channel_id=1, source_target_pairs={{0,1},{1,0},{2,3},{3,2},{4,5},{5,4},{6,7},{7,6},{8,9},{9,8},{10,11... | collective-permute-start | bytes 196616 | tf_op jit(solution)/shard_map/ppermute | solution.py:421
  9.9 6.0 %collective-permute-start.3 = (f32[4,16,128]{2,1,0:T(8,128)}, f32[4,16,128]{2,1,0:T(8,128)S(1)}, u32[]{:S(2)}, u32[]{:S(2)}) collective-permute-start(f32[4,16,128]{2,1,0:T(8,128)} %right.5), channel_id=1, source_target_pairs={{1,4},{3,6},{4,1},{5,8},{6,3},{7,10},{8,5},{9,12},{10,7},{11,14},{... | collective-permute-start | bytes 98312 | tf_op jit(solution)/shard_map/ppermute | solution.py:421
  18.2 5.4 %collective-permute-start.4 = (f32[4,16,128]{2,1,0:T(8,128)S(1)}, f32[4,16,128]{2,1,0:T(8,128)S(1)}, u32[]{:S(2)}, u32[]{:S(2)}) collective-permute-start(f32[4,16,128]{2,1,0:T(8,128)S(1)} %get-tuple-element.18.v.image), channel_id=1, source_target_pairs={{0,1},{1,0},{2,3},{3,2},{4,5},{5,4},{6,7},{7,6},{8,9},{9,8},{10,11... | collective-permute-start | bytes 98312 | tf_op jit(solution)/shard_map/ppermute | solution.py:421
  23.6 0.7 collective-permute-start.5
  24.3 8.1 %collective-permute-start.6 = (f32[8,16,128]{2,1,0:T(8,128)S(1)}, f32[8,16,128]{2,1,0:T(8,128)S(1)}, u32[]{:S(2)}, u32[]{:S(2)}) collective-permute-start(f32[8,16,128]{2,1,0:T(8,128)S(1)} %collective-permute-done.5.p1), channel_id=1, source_target_pairs={{0,1},{1,0},{2,3},{3,2},{4,5},{5,4},{6,7},{7,6},{8,9},{9,8},{10,11... | collective-permute-start | bytes 196616 | tf_op jit(solution)/shard_map/ppermute | solution.py:421
  31.5 0.7 collective-permute-start.7
  60.1 1.3 %collective-permute-start.8 = (f32[4,16,128]{2,1,0:T(8,128)S(1)}, f32[4,16,128]{2,1,0:T(8,128)S(1)}, u32[]{:S(2)}, u32[]{:S(2)}) collective-permute-start(f32[4,16,128]{2,1,0:T(8,128)S(1)} %get-tuple-element.24.v.head), channel_id=1, source_target_pairs={{0,1},{1,0},{2,3},{3,2},{4,5},{5,4},{6,7},{7,6},{8,9},{9,8},{10,11... | collective-permute-start | bytes 98312 | tf_op jit(solution)/shard_map/ppermute | solution.py:421
  61.3 0.7 collective-permute-start.9
  62.0 6.1 %collective-permute-start.10 = (f32[8,16,128]{2,1,0:T(8,128)S(1)}, f32[8,16,128]{2,1,0:T(8,128)S(1)}, u32[]{:S(2)}, u32[]{:S(2)}) collective-permute-start(f32[8,16,128]{2,1,0:T(8,128)S(1)} %collective-permute-done.9.p1), channel_id=1, source_target_pairs={{0,1},{1,0},{2,3},{3,2},{4,5},{5,4},{6,7},{7,6},{8,9},{9,8},{10,11... | collective-permute-start | bytes 196616 | tf_op jit(solution)/shard_map/ppermute | solution.py:421
  67.2 0.7 collective-permute-start.11
  70.5 6.5 %collective-permute-start.12 = (f32[4,16,128]{2,1,0:T(8,128)S(1)}, f32[4,16,128]{2,1,0:T(8,128)S(1)}, u32[]{:S(2)}, u32[]{:S(2)}) collective-permute-start(f32[4,16,128]{2,1,0:T(8,128)S(1)} %get-tuple-element.26.v.smooth), channel_id=1, source_target_pairs={{0,1},{1,0},{2,3},{3,2},{4,5},{5,4},{6,7},{7,6},{8,9},{9,8},{10,11... | collective-permute-start | bytes 98312 | tf_op jit(solution)/shard_map/ppermute | solution.py:421
  77.0 0.7 collective-permute-start.13
  77.7 6.9 %collective-permute-start.14 = (f32[16,16,128]{2,1,0:T(8,128)S(1)}, f32[16,16,128]{2,1,0:T(8,128)S(1)}, u32[]{:S(2)}, u32[]{:S(2)}) collective-permute-start(f32[16,16,128]{2,1,0:T(8,128)S(1)} %collective-permute-done.13.p1), channel_id=1, source_target_pairs={{0,1},{1,0},{2,3},{3,2},{4,5},{5,4},{6,7},{7,6},{8,9},{9,8},{10,11... | collective-permute-start | bytes 393224 | tf_op jit(solution)/shard_map/ppermute | solution.py:421
  83.6 0.7 collective-permute-start.15

commit v5 on v4

--- a/solution.py
+++ b/solution.py
@@ -11,6 +11,7 @@
 REACH = 3
 OWN, LOST, ELSE = range(3)
 SLOTS = len(OFFSETS)
+STAY = 1
 HIGHEST = lax.Precision.HIGHEST
 AXES = ("grp", "row")
 VMEM = pltpu.VMEM
@@ -51,30 +52,29 @@
     return high, middle, low
 
 
-def build_table(pieces, place, table_ref, classes, blocks, cols, start=0):
-    for slot, (piece, first) in enumerate(pieces):
+def build_table(pieces, vector, place, table_ref, classes, blocks, cols, start=0):
+    v, sw, near, other, far = pieces
+    first = vector * blocks
+    pair = first + v.shape[0]
+    slots = ((v, first), (sw, first), (near, first), (near, pair), (other, first), (other, pair), (far, first))
+    for slot, (piece, base) in enumerate(slots):
         position, flags = place.slot(slot)
         for block in range(blocks):
-            entry = position * blocks + block
-            value = None if piece is None else piece[first + block]
+            value = piece[base + block]
             for k, name in enumerate(classes):
-                base = 3 * (start + k) * cols
-                if piece is None:
-                    table_ref[entry, base : base + 3 * cols, :] = jnp.zeros(
-                        (3 * cols, table_ref.shape[2]), jnp.bfloat16
-                    )
-                    continue
                 for s, term in enumerate(split3(value * flags[name])):
-                    table_ref[entry, base + s * cols : base + (s + 1) * cols, :] = term
-
-
-def slots(v, sw, near, other, far, blocks, skip=0):
-    first = 2 * skip * blocks
-    here = (v, sw) if skip == 0 else (None, None)
-    return (
-        (here[0], 0), (here[1], 0), (near, first), (near, first + blocks),
-        (other, first), (other, first + blocks), (far, skip * blocks),
-    )
+                    rows = pl.ds((3 * (start + k) + s) * cols, cols)
+                    table_ref[position * blocks + block, rows, :] = term
+
+
+class Joined:
+    def __init__(self, first, second):
+        self.parts = (first, second)
+        self.first = first.shape[0]
+        self.shape = (first.shape[0] + second.shape[0], *first.shape[1:])
+
+    def at(self, row):
+        return self.parts[row >= self.first].at[row - self.first * (row >= self.first)]
 
 
 class Place:
@@ -107,7 +107,7 @@
             [table_ref[columns_ref[row, 2 * pair + j] - base] for j in (0, 1)], axis=1
         )
         part = lax.dot_general(
-            left, split_ref[row, pair], (((1,), (0,)), ((), ())),
+            left, split_ref.at(row)[pair], (((1,), (0,)), ((), ())),
             preferred_element_type=jnp.float32,
         )
         total = part if total is None else total + part
@@ -123,7 +123,9 @@
     return out
 
 
-def split_kernel(tiles_hbm, precond_hbm, split, halves, tiles, precond, sems):
+def split_kernel(
+    tiles_hbm, precond_hbm, right_hbm, split_a, split_b, halves, smooth, tiles, precond, right, sems, late_sems
+):
     blocks, count, tb, _ = tiles.shape
     rows, columns = grid16(2 * tb)
     unit = (rows == columns).astype(jnp.bfloat16)
@@ -133,8 +135,12 @@
     ]
     for copy in copies:
         copy.start()
-    last = pltpu.make_async_copy(precond_hbm, precond, sems.at[blocks])
-    last.start()
+    late = [
+        pltpu.make_async_copy(precond_hbm, precond, late_sems.at[0]),
+        pltpu.make_async_copy(right_hbm, right, late_sems.at[1]),
+    ]
+    for copy in late:
+        copy.start()
     for row in range(blocks):
         copies[row].wait()
         for pair in range(count // 2):
@@ -150,32 +156,41 @@
             turned = lax.dot_general(
                 unit, both, (((1,), (1,)), ((), ())), preferred_element_type=jnp.float32
             )
-            split[row, pair] = turned.astype(jnp.bfloat16)
-    last.wait()
+            Joined(split_a, split_b).at(row)[pair] = turned.astype(jnp.bfloat16)
+    for copy in late:
+        copy.wait()
     for row in range(blocks):
         high = precond[row].astype(jnp.bfloat16)
         halves[row, 0:tb] = high
         halves[row, tb : 2 * tb] = (precond[row] - high.astype(jnp.float32)).astype(jnp.bfloat16)
-
-
-def split_call(tiles, precond):
+    for row in range(blocks):
+        smooth[row] = smoothed(right[row], halves[row], right.shape[1], tb)
+
+
+def split_call(tiles, precond, right):
     blocks, count, tb, _ = tiles.shape
     return pl.pallas_call(
         split_kernel,
         out_shape=[
-            jax.ShapeDtypeStruct((blocks, count // 2, 2 * tb, 2 * tb), jnp.bfloat16),
+            jax.ShapeDtypeStruct((rows, count // 2, 2 * tb, 2 * tb), jnp.bfloat16)
+            for rows in (STAY, blocks - STAY)
+        ]
+        + [
             jax.ShapeDtypeStruct((blocks, 2 * tb, tb), jnp.bfloat16),
+            jax.ShapeDtypeStruct(right.shape, jnp.float32),
         ],
-        in_specs=[spec(pltpu.HBM)] * 2,
-        out_specs=[spec(VMEM)] * 2,
+        in_specs=[spec(pltpu.HBM)] * 3,
+        out_specs=[spec(VMEM)] * 4,
         scratch_shapes=[
             VMEM(tiles.shape, jnp.float32),
             VMEM(precond.shape, jnp.float32),
-            pltpu.SemaphoreType.DMA((blocks + 1,)),
+            VMEM(right.shape, jnp.float32),
+            pltpu.SemaphoreType.DMA((blocks,)),
+            pltpu.SemaphoreType.DMA((2,)),
         ],
         compiler_params=params(24),
         cost_estimate=pl.CostEstimate(flops=0, bytes_accessed=12 * tiles.size // 2, transcendentals=0),
-    )(*(pltpu.with_memory_space_constraint(array, pltpu.HBM) for array in (tiles, precond)))
+    )(*(pltpu.with_memory_space_constraint(array, pltpu.HBM) for array in (tiles, precond, right)))
 
 
 def smoothed(value, halves, cols, tb):
@@ -232,79 +247,102 @@
     return g00, g01, g01_t, g02, g02_t, g11, g12
 
 
-def first_kernel(columns_ref, lost_ref, split, v, sw, p1, p2, p3, parts, image, table):
+def first_kernel(
+    columns_ref, lost_ref, split_a, split_b, halves, v, sw, p1, p2, p3, parts, image, smooth, table
+):
     blocks, cols, _ = v.shape
     place = Place(lost_ref)
     base = place.base(blocks)
-    build_table(slots(v, sw, p1, p2, p3, blocks), place, table, (OWN, LOST, ELSE), blocks, cols)
-    for row in range(blocks):
-        out = row_product(columns_ref, base, table, split, row, 3, cols)
+    build_table((v, sw, p1, p2, p3), 0, place, table, (OWN, LOST, ELSE), blocks, cols)
+    for row in range(blocks):
+        out = row_product(columns_ref, base, table, Joined(split_a, split_b), row, 3, cols)
         for k in range(3):
             parts[k, row] = out[k]
         image[row] = out[0] + out[1] + out[2]
+    for row in range(blocks):
+        smooth[row] = smoothed(parts[1, row] + parts[2, row], halves[row], cols, v.shape[2])
 
 
 def second_kernel(
-    columns_ref, lost_ref, split, right, v, sw, p1, p2, p3, parts, gram, table, image
+    columns_ref, lost_ref, split_a, split_b, halves, smooth_b, smooth_o, right, v, sw, p1, p2, p3,
+    parts, gram, smooth, table, image,
 ):
     blocks, cols, _ = v.shape
     place = Place(lost_ref)
     base = place.base(blocks)
-    build_table(slots(v, sw, p1, p2, p3, blocks), place, table, (OWN, LOST, ELSE), blocks, cols)
-    for row in range(blocks):
-        out = row_product(columns_ref, base, table, split, row, 3, cols)
+    build_table((v, sw, p1, p2, p3), 0, place, table, (OWN, LOST, ELSE), blocks, cols)
+    for row in range(blocks):
+        out = row_product(columns_ref, base, table, Joined(split_a, split_b), row, 3, cols)
         for k in range(3):
             parts[k, row] = out[k]
         image[row] = out[0] + out[1] + out[2]
+    for row in range(blocks):
+        smooth[row] = smooth_b[row]
+        smooth[blocks + row] = smooth_o[row]
+        smooth[2 * blocks + row] = smoothed(
+            parts[1, row] + parts[2, row], halves[row], cols, v.shape[2]
+        )
     former = jnp.concatenate([lanes(right), lanes(v)], axis=0)
     latter = jnp.concatenate([former, lanes(image)], axis=0)
     pack_gram(gram, former, latter, None, cols)
 
 
 def third_kernel(
-    columns_ref, lost_ref, split, halves, v, sw, p1, p2, p3, applied, smooth, table
-):
-    blocks, cols, tb = v.shape
+    columns_ref, lost_ref, split_a, split_hbm, v, sw, p1, p2, p3, applied, table, split_b, sems
+):
+    blocks, cols = applied.shape[1], v.shape[1]
+    copies = [
+        pltpu.make_async_copy(split_hbm.at[row], split_b.at[row], sems.at[row])
+        for row in range(blocks - STAY)
+    ]
+    for copy in copies:
+        copy.start()
     place = Place(lost_ref)
     base = place.base(blocks)
-    build_table(slots(v, sw, p1, p2, p3, blocks), place, table, (OWN,), blocks, cols)
-    for row in range(blocks):
-        (applied[row],) = row_product(columns_ref, base, table, split, row, 1, cols)
-    for row in range(blocks):
-        smooth[row] = smoothed(applied[row], halves[row], cols, tb)
+    for vector in range(3):
+        build_table((v, sw, p1, p2, p3), vector, place, table, (OWN,), blocks, cols, vector)
+    for row in range(blocks):
+        if row >= STAY:
+            copies[row - STAY].wait()
+        out = row_product(columns_ref, base, table, Joined(split_a, split_b), row, 3, cols)
+        for vector in range(3):
+            applied[vector, row] = out[vector]
 
 
 def fourth_kernel(
-    columns_ref, lost_ref, split, target, head, applied, v, sw, p1, p2, p3, lost0, lost1, gram,
+    columns_ref, lost_ref, split_a, split_b, target, applied, v, sw, p1, p2, p3, lost0, lost1, gram,
     table, second,
 ):
-    blocks, cols, _ = v.shape
+    blocks, cols, _ = target.shape
     place = Place(lost_ref)
     base = place.base(blocks)
     mine = place.mine
-    build_table(slots(v, sw, p1, p2, p3, blocks), place, table, (OWN, LOST), blocks, cols)
-    build_table(slots(v, sw, p1, p2, p3, blocks, 1), place, table, (LOST,), blocks, cols, 2)
-    for row in range(blocks):
-        out = row_product(columns_ref, base, table, split, row, 3, cols)
+    build_table((v, sw, p1, p2, p3), 0, place, table, (OWN, LOST), blocks, cols)
+    build_table((v, sw, p1, p2, p3), 1, place, table, (LOST,), blocks, cols, 2)
+    for row in range(blocks):
+        out = row_product(columns_ref, base, table, Joined(split_a, split_b), row, 3, cols)
         second[row] = out[0]
         lost1[row] = out[0] * mine + out[1]
         lost0[row] = applied[row] * mine + out[2]
-    former = jnp.concatenate([lanes(head), lanes(v)], axis=0)
+    smooth, head = v.at[0:blocks], v.at[blocks : 2 * blocks]
+    former = jnp.concatenate([lanes(head), lanes(smooth)], axis=0)
     latter = jnp.concatenate([lanes(target), lanes(applied), lanes(second)], axis=0)
     pack_gram(gram, former, latter, mine, cols)
 
 
-def tile_call(kernel, classes, outs, extra, split, operands_vmem, columns, lost):
-    blocks, cols, tb = operands_vmem[-5].shape
+def tile_call(kernel, classes, outs, extra, split, operands_vmem, columns, lost, place=VMEM):
+    blocks = split[0].shape[0] + split[1].shape[0]
+    _, cols, tb = operands_vmem[-1].shape
     scratch = [VMEM((SLOTS * blocks, 3 * classes * cols, tb), jnp.bfloat16)] + extra
     return pl.pallas_call(
         kernel,
         out_shape=outs,
-        in_specs=[spec(SMEM), spec(SMEM)] + [spec(VMEM)] * (1 + len(operands_vmem)),
+        in_specs=[spec(SMEM), spec(SMEM), spec(VMEM), spec(place)]
+        + [spec(VMEM)] * len(operands_vmem),
         out_specs=[spec(VMEM)] * len(outs),
         scratch_shapes=scratch,
         compiler_params=params(16),
-    )(columns, lost, split, *operands_vmem)
+    )(columns, lost, *split, *operands_vmem)
 
 
 def eliminate(matrix, target):
@@ -346,47 +384,57 @@
 
 
 def outer_kernel(
-    lost_ref, gathered, right, image, parts_b, parts_y, precond, solution, target, head, kept
+    lost_ref, gathered, right, image, parts_b, parts_y, smooth, moved, halves,
+    solution, target, applied, kept, pair,
 ):
     blocks, cols, tb = right.shape
     mine = Place(lost_ref).mine
     weights = coefficients(gathered, cols)
-
-    def basis(pick):
-        return jnp.concatenate(
-            [
-                jnp.concatenate([pick(0, i) for i in range(blocks)], axis=1),
-                jnp.concatenate([pick(1, i) for i in range(blocks)], axis=1),
-            ],
-            axis=0,
-        )
-
-    parts = (parts_b, parts_y)
-    own = (right, image)
+    span = blocks * tb
+
+    def wide(pick):
+        return jnp.concatenate([pick(i) for i in range(blocks)], axis=1)
+
+    def others(parts):
+        return wide(lambda i: parts[1, i] + parts[2, i])
+
+    def kept_part(parts):
+        return wide(lambda i: parts[0, i] * (1.0 - mine) + parts[2, i])
+
     stacked = jnp.concatenate(
         [
-            basis(lambda n, i: own[n][i]),
-            basis(lambda n, i: parts[n][1, i] + parts[n][2, i]),
-            basis(lambda n, i: parts[n][0, i] * (1.0 - mine) + parts[n][2, i]),
+            jnp.concatenate([lanes(right), lanes(image)], axis=0),
+            jnp.concatenate([kept_part(parts_b), kept_part(parts_y)], axis=0),
+            jnp.concatenate([others(parts_b), others(parts_y)], axis=0),
+            jnp.concatenate(
+                [wide(lambda i: smooth[blocks + i]), wide(lambda i: smooth[2 * blocks + i])], axis=0
+            ),
+            jnp.concatenate([wide(lambda i: moved[1, i]), wide(lambda i: moved[2, i])], axis=0),
         ],
         axis=1,
     )
     made = dot_tn(weights, stacked)
-    span = blocks * tb
+
+    def block(number, i):
+        return made[:, number * span + i * tb : number * span + (i + 1) * tb]
+
     for i in range(blocks):
-        solution[i] = made[:, i * tb : (i + 1) * tb]
-        aim = right[i] - made[:, span + i * tb : span + (i + 1) * tb]
-        target[i] = aim
-        head[i] = smoothed(aim, precond[i], cols, tb)
-        kept[i] = made[:, 2 * span + i * tb : 2 * span + (i + 1) * tb]
+        solution[i] = block(0, i)
+        kept[i] = block(1, i)
+        target[i] = right[i] - block(2, i)
+        pair[blocks + i] = smooth[i] - block(3, i)
+        image_of_head = moved[0, i] - block(4, i)
+        applied[i] = image_of_head
+        pair[i] = smoothed(image_of_head, halves[i], cols, tb)
 
 
 def inner_kernel(
-    lost_ref, gathered, right, solution, kept, head, smooth, lost0, lost1, recovered, residual
+    lost_ref, gathered, right, solution, kept, pair, lost0, lost1, recovered, residual
 ):
     blocks, cols, tb = right.shape
     mine = Place(lost_ref).mine
     weights = coefficients(gathered, cols)
+    smooth, head = pair.at[0:blocks], pair.at[blocks : 2 * blocks]
     stacked = jnp.concatenate(
         [
             jnp.concatenate([lanes(head), lanes(lost0)], axis=1),
@@ -400,6 +448,36 @@
         estimate = made[:, i * tb : (i + 1) * tb]
         recovered[i] = jnp.where(mine > 0.5, estimate, solution[i])
         residual[i] = right[i] - kept[i] - made[:, span + i * tb : span + (i + 1) * tb]
+
+
+def reload_kernel(split_hbm, split, sems):
+    blocks, pairs = split.shape[0], split.shape[1]
+    chunk = pairs // 4
+    copies = [
+        pltpu.make_async_copy(
+            split_hbm.at[row, k * chunk : (k + 1) * chunk],
+            split.at[row, k * chunk : (k + 1) * chunk],
+            sems.at[row, k],
+        )
+        for row in range(blocks)
+        for k in range(4)
+    ]
+    for copy in copies:
+        copy.start()
+    for copy in copies:
+        copy.wait()
+
+
+def reload_call(split):
+    return pl.pallas_call(
+        reload_kernel,
+        out_shape=jax.ShapeDtypeStruct(split.shape, split.dtype),
+        in_specs=[spec(pltpu.HBM)],
+        out_specs=spec(VMEM),
+        scratch_shapes=[pltpu.SemaphoreType.DMA((split.shape[0], 4))],
+        compiler_params=params(16),
+        cost_estimate=pl.CostEstimate(flops=0, bytes_accessed=4 * split.size, transcendentals=0),
+    )(split)
 
 
 def small_call(kernel, outs, lost, gathered, *arrays):
@@ -421,12 +499,11 @@
     return lax.ppermute(value, AXES, pairs)
 
 
-def window(value, inside=False, along=()):
+def window(value, inside=False):
     swapped = move(value, lambda i: i ^ 1)
-    pair = jnp.concatenate([value, swapped, *along], axis=0)
-    alone = jnp.concatenate([value, along[0]], axis=0) if along else value
+    pair = jnp.concatenate([value, swapped], axis=0)
     near = move(pair, lambda i: i - 1 if i % 2 == 0 else i + 1, inside)
-    far = move(alone, lambda i: i - 3 if i % 2 == 0 else i + 3, inside)
+    far = move(value, lambda i: i - 3 if i % 2 == 0 else i + 3, inside)
     other = move(near, lambda i: i ^ 1)
     return value, swapped, near, other, far
 
@@ -440,33 +517,43 @@
     assert -(-BAND // blocks) == REACH <= lax.axis_size("row")
     total = lax.axis_size("row") * lax.axis_size("grp")
 
-    vec = jax.ShapeDtypeStruct(right_side.shape, jnp.float32)
-    vec3 = jax.ShapeDtypeStruct((3,) + right_side.shape, jnp.float32)
+    def shape(*lead):
+        return jax.ShapeDtypeStruct((*lead, cols, tb), jnp.float32)
+
+    vec, vec3 = shape(blocks), shape(3, blocks)
     gram = jax.ShapeDtypeStruct((total, cols // 2, 8 * cols), jnp.float32)
     assert tb == 8 * cols
     held = VMEM(right_side.shape, jnp.float32)
-
-    split, halves = split_call(matrix_tiles, precond)
-    parts_b, image = tile_call(
-        first_kernel, 3, [vec3, vec], [], split, window(right_side), column_index, lost_group
-    )
-    parts_y, gram_outer = tile_call(
-        second_kernel, 3, [vec3, gram], [held], split,
-        (right_side,) + window(image), column_index, lost_group,
-    )
-    solution, target, head, kept = small_call(
-        outer_kernel, [vec] * 4, lost_group, exchange(gram_outer), right_side, image, parts_b, parts_y, halves
-    )
-    ahead = window(head, inside=True)
-    applied, smooth = tile_call(
-        third_kernel, 1, [vec] * 2, [], split, (halves,) + ahead, column_index, lost_group
-    )
+    placing = (column_index, lost_group)
+
+    *split, halves, smooth_b = split_call(matrix_tiles, precond, right_side)
+    parts_b, image, smooth_o = tile_call(
+        first_kernel, 3, [vec3, vec, vec], [], split,
+        (halves,) + window(right_side), *placing,
+    )
+    parts_y, gram_outer, smooth = tile_call(
+        second_kernel, 3, [vec3, gram, shape(3 * blocks)], [held], split,
+        (halves, smooth_b, smooth_o, right_side) + window(image), *placing,
+    )
+    around = window(smooth, inside=True)
+    gathered = exchange(gram_outer)
+    held_split = pltpu.with_memory_space_constraint(split[1], pltpu.HBM)
+    (moved,) = tile_call(
+        third_kernel, 3, [vec3],
+        [VMEM(split[1].shape, split[1].dtype), pltpu.SemaphoreType.DMA((blocks - STAY,))],
+        (split[0], held_split), around, *placing, place=pltpu.HBM,
+    )
+    solution, target, applied, kept, pair = small_call(
+        outer_kernel, [vec] * 4 + [shape(2 * blocks)], lost_group, gathered, right_side, image,
+        parts_b, parts_y, smooth, moved, halves,
+    )
+    split = (split[0], reload_call(held_split))
     lost0, lost1, gram_inner = tile_call(
         fourth_kernel, 3, [vec, vec, gram], [held], split,
-        (target, head, applied) + window(smooth, along=ahead[:2]), column_index, lost_group,
+        (target, applied) + window(pair), *placing,
     )
     recovered, residual = small_call(
-        inner_kernel, [vec] * 2, lost_group, exchange(gram_inner), right_side, solution, kept, head, smooth,
+        inner_kernel, [vec] * 2, lost_group, exchange(gram_inner), right_side, solution, kept, pair,
         lost0, lost1,
     )
     return (recovered, residual)

time: 111 us -> 108 us (0.973)
  blocking collectives: 42.7 us -> 20.8 us
  starting transfers between devices: 41 us -> 51.5 us
  Pallas kernels: 20 us -> 26.8 us
  waiting for transfers between devices: 4.49 us -> 6.03 us
    all_to_all x2 -> x1, blocking collectives: 42.7 us -> 20.8 us  [exchange(): return lax.all_to_all(gram, AXES, 0, 0)]
    all_to_all x0 -> x1, starting transfers between devices: none -> 10.4 us  [exchange(): return lax.all_to_all(gram, AXES, 0, 0)]
    pallas_call x5 -> x6, Pallas kernels: 15 us -> 21.7 us  [the longest x4 13.9 us: tile_call(): pl.pallas_call(kernel, out_shape=outs, in_specs=[spec(SMEM), spec(SMEM),...]
    all_to_all x0 -> x1, waiting for transfers between devices: none -> 1.48 us  [exchange(): return lax.all_to_all(gram, AXES, 0, 0)]
  transfers between devices with their start and end apart: 16 -> 17, of which waited for: 7 -> 7; matrix products, arithmetic and copies ran while one was open for 0% -> 0% of each run, Pallas kernels for 4% -> 12%
where the time goes in v5:
time: 108 us
  starting transfers between devices  51.5 us (48%)
  Pallas kernels  26.8 us (25%)
  blocking collectives  20.8 us (19%)
  waiting for transfers between devices  6.03 us (6%)
  between operations  1.53 us (1%)
    ppermute x16, starting transfers between devices, move(): return lax.ppermute(value, AXES, pairs)  41.1 us
    all_to_all x1, blocking collectives, exchange(): return lax.all_to_all(gram, AXES, 0, 0)  20.8 us
    pallas_call x4, Pallas kernels, tile_call(): pl.pallas_call(kernel, out_shape=outs, in_specs=[spec(SMEM), spec(SMEM),...  13.9 us
    all_to_all x1, starting transfers between devices, exchange(): return lax.all_to_all(gram, AXES, 0, 0)  10.4 us
    pallas_call x2, Pallas kernels, small_call(): pl.pallas_call(kernel, out_shape=outs, in_specs=[spec(SMEM)] + [spec(VMEM...  5.14 us
    pallas_call x1, Pallas kernels, split_call(): pl.pallas_call(split_kernel, out_shape=[jax.ShapeDtypeStruct((rows, count...  4.87 us
    ppermute x16, waiting for transfers between devices, move(): return lax.ppermute(value, AXES, pairs)  4.55 us
    pallas_call x1, Pallas kernels, reload_call(): pl.pallas_call(reload_kernel, out_shape=jax.ShapeDtypeStruct(split.shape,...  2.88 us
  transfers between devices with their start and end apart: 17, of which 7 were waited for; matrix products, arithmetic and copies ran while one was open for 0% of the time, Pallas kernels for 12%

profile of v5, /device:TPU:0, one launch (start us, length us, event | category | flops | bytes accessed | tf_op | source)
XLA Modules:
  0.0 107.6 jit_solution(12825787088834096111)
XLA Ops:
  0.6 0.0 copy-start.1
  0.6 0.0 copy-start.2
  0.7 0.6 collective-permute-start
  1.2 1.1 collective-permute-done.sw
  2.3 0.8 pad_maximum_fusion.2
  3.0 0.7 collective-permute-start.1
  3.7 0.0 collective-permute-done.1.p1
  3.7 6.2 %collective-permute-start.2 = (f32[8,16,128]{2,1,0:T(8,128)S(1)}, f32[8,16,128]{2,1,0:T(8,128)S(1)}, u32[]{:S(2)}, u32[]{:S(2)}) collective-permute-start(f32[8,16,128]{2,1,0:T(8,128)S(1)} %collective-permute-done.1.p1), channel_id=1, source_target_pairs={{0,1},{1,0},{2,3},{3,2},{4,5},{5,4},{6,7},{7,6},{8,9},{9,8},{10,11... | collective-permute-start | bytes 196616 | tf_op jit(solution)/shard_map/ppermute | solution.py:499
  9.9 0.7 collective-permute-start.3
  11.2 4.9 %shard_map.68 = (bf16[1,16,256,256]{3,2,1,0:T(8,128)(2,1)S(1)}, bf16[3,16,256,256]{3,2,1,0:T(8,128)(2,1)S(1)}, bf16[4,256,128]{2,1,0:T(8,128)(2,1)S(1)}, f32[4,16,128]{2,1,0:T(8,128)S(1)}) custom-call(f32[4,32,128,128]{3,2,1,0:T(8,128)} %tiles_hbm.1, f32[4,128,128]{2,1,0:T(8,128)} %precond_hbm.1, f32[4,16,128]{2,1,0:T(8,128)} %right.5), custom_call_target="tpu_custom_call" | custom-call | bytes 12582912 | tf_op jit(solution)/shard_map/pallas_call | solution.py:172
  16.1 0.0 copy-start
  16.1 0.0 collective-permute-done.3.p3
  16.1 0.0 collective-permute-done.2.p2
  16.1 0.0 copy-done.1
  16.1 0.0 copy-done.2
  16.1 2.3 %shard_map.70 = (f32[3,4,16,128]{3,2,1,0:T(8,128)S(1)}, f32[4,16,128]{2,1,0:T(8,128)S(1)}, f32[4,16,128]{2,1,0:T(8,128)S(1)}) custom-call(s32[4,32]{1,0:T(4,128)S(1)} %copy-done.2, s32[1]{0:T(128)S(6)} %copy.7.lost_ref, bf16[1,16,256,256]{3,2,1,0:T(8,128)(2,1)S(1)} %get-tuple-element.20.split_a, ...), custom_call_target="tpu_custom_call" | custom-call | tf_op jit(solution)/shard_map/pallas_call | solution.py:337
  18.5 4.6 %collective-permute-start.4 = (f32[4,16,128]{2,1,0:T(8,128)S(1)}, f32[4,16,128]{2,1,0:T(8,128)S(1)}, u32[]{:S(2)}, u32[]{:S(2)}) collective-permute-start(f32[4,16,128]{2,1,0:T(8,128)S(1)} %get-tuple-element.25.v.image), channel_id=1, source_target_pairs={{0,1},{1,0},{2,3},{3,2},{4,5},{5,4},{6,7},{7,6},{8,9},{9,8},{10,11... | collective-permute-start | bytes 98312 | tf_op jit(solution)/shard_map/ppermute | solution.py:499
  23.1 0.9 collective-permute-done.4.sw
  23.9 0.7 collective-permute-start.5
  24.6 0.0 collective-permute-done.5.p1
  24.6 7.9 %collective-permute-start.6 = (f32[8,16,128]{2,1,0:T(8,128)S(1)}, f32[8,16,128]{2,1,0:T(8,128)S(1)}, u32[]{:S(2)}, u32[]{:S(2)}) collective-permute-start(f32[8,16,128]{2,1,0:T(8,128)S(1)} %collective-permute-done.5.p1), channel_id=1, source_target_pairs={{0,1},{1,0},{2,3},{3,2},{4,5},{5,4},{6,7},{7,6},{8,9},{9,8},{10,11... | collective-permute-start | bytes 196616 | tf_op jit(solution)/shard_map/ppermute | solution.py:499
  32.5 0.7 collective-permute-start.7
  33.2 0.0 collective-permute-done.7.p3
  33.2 0.2 collective-permute-done.6.p2
  33.4 3.6 %shard_map.71 = (f32[3,4,16,128]{3,2,1,0:T(8,128)S(1)}, f32[32,8,128]{2,1,0:T(8,128)}, f32[12,16,128]{2,1,0:T(8,128)S(1)}) custom-call(s32[4,32]{1,0:T(4,128)S(1)} %copy-done.2, s32[1]{0:T(128)S(6)} %copy.7.lost_ref, bf16[1,16,256,256]{3,2,1,0:T(8,128)(2,1)S(1)} %get-tuple-element.20.split_a, ...), custom_call_target="tpu_custom_call" | custom-call | tf_op jit(solution)/shard_map/pallas_call | solution.py:337
  37.0 0.0 copy-done
  37.0 5.2 %collective-permute-start.8 = (f32[12,16,128]{2,1,0:T(8,128)S(1)}, f32[12,16,128]{2,1,0:T(8,128)S(1)}, u32[]{:S(2)}, u32[]{:S(2)}) collective-permute-start(f32[12,16,128]{2,1,0:T(8,128)S(1)} %get-tuple-element.29.v.smooth), channel_id=1, source_target_pairs={{0,1},{1,0},{2,3},{3,2},{4,5},{5,4},{6,7},{7,6},{8,9},{9,8},{10,11... | collective-permute-start | bytes 294920 | tf_op jit(solution)/shard_map/ppermute | solution.py:499
  42.2 0.9 collective-permute-done.8.sw
  43.2 0.7 collective-permute-start.9
  43.8 10.4 %all-to-all-start = ((f32[32,8,128]{2,1,0:T(8,128)}), f32[32,8,128]{2,1,0:T(8,128)S(1)}, u32[]{:S(2)}, u32[]{:S(2)}) async-start(f32[32,8,128]{2,1,0:T(8,128)} %get-tuple-element.26), calls=%async_computation | async-start | bytes 262144 | tf_op jit(solution)/shard_map/all_to_all | solution.py:512
  54.2 0.0 collective-permute-done.9.p1
  54.3 0.3 collective-permute-start.10
  54.6 0.7 collective-permute-start.11
  55.2 0.0 collective-permute-done.11.p3
  55.2 0.5 collective-permute-done.10.p2
  55.8 5.2 %shard_map.72.moved = f32[3,4,16,128]{3,2,1,0:T(8,128)S(1)} custom-call(s32[4,32]{1,0:T(4,128)S(1)} %copy-done.2, s32[1]{0:T(128)S(6)} %copy.7.lost_ref, bf16[1,16,256,256]{3,2,1,0:T(8,128)(2,1)S(1)} %get-tuple-element.20.split_a, bf16[3,16,256,256]{3,2,1,0:T(8,128)(2,1)} %copy-done, f32[12,16,128]{2,1,0:T(8,128)S(1)} %get-tuple-element.29.v.smooth, ...), custom_call_target="tpu_custom_call" | custom-call | tf_op jit(solution)/shard_map/pallas_call | solution.py:337
  60.9 1.5 %all-to-all-done.gathered = f32[32,8,128]{2,1,0:T(8,128)S(1)} async-done(((f32[32,8,128]{2,1,0:T(8,128)}), f32[32,8,128]{2,1,0:T(8,128)S(1)}, u32[]{:S(2)}, u32[]{:S(2)}) %all-to-all-start) | async-done | bytes 131104 | tf_op jit(solution)/shard_map/all_to_all | solution.py:512
  62.4 2.4 %shard_map.73 = (f32[4,16,128]{2,1,0:T(8,128)S(1)}, f32[4,16,128]{2,1,0:T(8,128)S(1)}, f32[4,16,128]{2,1,0:T(8,128)S(1)}, f32[4,16,128]{2,1,0:T(8,128)S(1)}, f32[8,16,128]{2,1,0:T(8,128)S(1)}) custom-call(s32[1]{0:T(128)S(6)} %copy.7.lost_ref, f32[32,8,128]{2,1,0:T(8,128)S(1)} %all-to-all-done.gathered, f32[4,16,128]{2,1,0:T(8,128)S(1)} %copy-done.1, ...), custom_call_target="tpu_custom_call" | custom-call | tf_op jit(solution)/shard_map/pallas_call | solution.py:484
  64.8 5.0 %collective-permute-start.12 = (f32[8,16,128]{2,1,0:T(8,128)S(1)}, f32[8,16,128]{2,1,0:T(8,128)S(1)}, u32[]{:S(2)}, u32[]{:S(2)}) collective-permute-start(f32[8,16,128]{2,1,0:T(8,128)S(1)} %get-tuple-element.32.v.pair), channel_id=1, source_target_pairs={{0,1},{1,0},{2,3},{3,2},{4,5},{5,4},{6,7},{7,6},{8,9},{9,8},{10,11... | collective-permute-start | bytes 196616 | tf_op jit(solution)/shard_map/ppermute | solution.py:499
  69.8 0.9 collective-permute-done.12.sw
  70.7 0.7 collective-permute-start.13
  71.4 0.0 collective-permute-done.13.p1
  71.4 6.0 %collective-permute-start.14 = (f32[16,16,128]{2,1,0:T(8,128)S(1)}, f32[16,16,128]{2,1,0:T(8,128)S(1)}, u32[]{:S(2)}, u32[]{:S(2)}) collective-permute-start(f32[16,16,128]{2,1,0:T(8,128)S(1)} %collective-permute-done.13.p1), channel_id=1, source_target_pairs={{0,1},{1,0},{2,3},{3,2},{4,5},{5,4},{6,7},{7,6},{8,9},{9,8},{10,11... | collective-permute-start | bytes 393224 | tf_op jit(solution)/shard_map/ppermute | solution.py:499
  77.4 0.8 collective-permute-start.15
  78.2 2.9 %shard_map.69.split_b = bf16[3,16,256,256]{3,2,1,0:T(8,128)(2,1)S(1)} custom-call(bf16[3,16,256,256]{3,2,1,0:T(8,128)(2,1)} %copy-done), custom_call_target="tpu_custom_call" | custom-call | bytes 12582912 | tf_op jit(solution)/shard_map/pallas_call | solution.py:472
  81.1 0.0 collective-permute-done.15.p3
  81.1 0.0 collective-permute-done.14.p2
  81.1 2.9 %shard_map.74 = (f32[4,16,128]{2,1,0:T(8,128)S(1)}, f32[4,16,128]{2,1,0:T(8,128)S(1)}, f32[32,8,128]{2,1,0:T(8,128)S(1)}) custom-call(s32[4,32]{1,0:T(4,128)S(1)} %copy-done.2, s32[1]{0:T(128)S(6)} %copy.7.lost_ref, bf16[1,16,256,256]{3,2,1,0:T(8,128)(2,1)S(1)} %get-tuple-element.20.split_a, bf16[3,16,256,256]{3,2,1,0:T(8,128)(2,1)S(1)} %shard_map.69.split_b, ...), custom_call_target="tpu_custom_call" | custom-call | tf_op jit(solution)/shard_map/pallas_call | solution.py:337
  84.0 20.8 %all_to_all.10.gathered = f32[32,8,128]{2,1,0:T(8,128)S(1)} all-to-all(f32[32,8,128]{2,1,0:T(8,128)S(1)} %get-tuple-element.33), channel_id=1, replica_groups=mesh['grp'=4,'row'=8] {'grp','row'}, dimensions={0} | all-to-all | bytes 262144 | tf_op jit(solution)/shard_map/all_to_all | solution.py:512
  104.8 2.7 %shard_map.75 = (f32[4,16,128]{2,1,0:T(8,128)}, f32[4,16,128]{2,1,0:T(8,128)}) custom-call(s32[1]{0:T(128)S(6)} %copy.7.lost_ref, f32[32,8,128]{2,1,0:T(8,128)S(1)} %all_to_all.10.gathered, f32[4,16,128]{2,1,0:T(8,128)S(1)} %copy-done.1, f32[4,16,128]{2,1,0:T(8,128)S(1)} %get-tuple-element.34.solution, f32[4,16,128]{2,1,0:T(8,128)S(1)} %get-tuple-element.35.kept, ...), custom_call_target="tpu_custom_call" | custom-call | tf_op jit(solution)/shard_map/pallas_call | solution.py:484
  (3 shorter events, 0.0 us)
Async XLA Ops:
  0.6 15.5 %copy-start.1 = (f32[4,16,128]{2,1,0:T(8,128)S(1)}, f32[4,16,128]{2,1,0:T(8,128)}, u32[]{:S(2)}) copy-start(f32[4,16,128]{2,1,0:T(8,128)} %right.5) | copy-start | bytes 98308
  0.6 15.5 %copy-start.2 = (s32[4,32]{1,0:T(4,128)S(1)}, s32[4,32]{1,0:T(4,128)}, u32[]{:S(2)}) copy-start(s32[4,32]{1,0:T(4,128)} %columns_ref.7) | copy-start | bytes 1540
  0.7 1.6 %collective-permute-start = (f32[4,16,128]{2,1,0:T(8,128)}, f32[4,16,128]{2,1,0:T(8,128)S(1)}, u32[]{:S(2)}, u32[]{:S(2)}) collective-permute-start(f32[4,16,128]{2,1,0:T(8,128)} %right.5), channel_id=1, source_target_pairs={{0,1},{1,0},{2,3},{3,2},{4,5},{5,4},{6,7},{7,6},{8,9},{9,8},{10,11... | collective-permute-start | bytes 98312 | tf_op jit(solution)/shard_map/ppermute | solution.py:499
  3.0 0.7 collective-permute-start.1
  3.7 12.4 %collective-permute-start.2 = (f32[8,16,128]{2,1,0:T(8,128)S(1)}, f32[8,16,128]{2,1,0:T(8,128)S(1)}, u32[]{:S(2)}, u32[]{:S(2)}) collective-permute-start(f32[8,16,128]{2,1,0:T(8,128)S(1)} %collective-permute-done.1.p1), channel_id=1, source_target_pairs={{0,1},{1,0},{2,3},{3,2},{4,5},{5,4},{6,7},{7,6},{8,9},{9,8},{10,11... | collective-permute-start | bytes 196616 | tf_op jit(solution)/shard_map/ppermute | solution.py:499
  9.9 6.2 %collective-permute-start.3 = (f32[4,16,128]{2,1,0:T(8,128)}, f32[4,16,128]{2,1,0:T(8,128)S(1)}, u32[]{:S(2)}, u32[]{:S(2)}) collective-permute-start(f32[4,16,128]{2,1,0:T(8,128)} %right.5), channel_id=1, source_target_pairs={{1,4},{3,6},{4,1},{5,8},{6,3},{7,10},{8,5},{9,12},{10,7},{11,14},{... | collective-permute-start | bytes 98312 | tf_op jit(solution)/shard_map/ppermute | solution.py:499
  16.1 20.9 %copy-start = (bf16[3,16,256,256]{3,2,1,0:T(8,128)(2,1)}, bf16[3,16,256,256]{3,2,1,0:T(8,128)(2,1)S(1)}, u32[]{:S(2)}) copy-start(bf16[3,16,256,256]{3,2,1,0:T(8,128)(2,1)S(1)} %get-tuple-element.21.split_hbm.split_b) | copy-start | bytes 18874372
  18.5 5.4 %collective-permute-start.4 = (f32[4,16,128]{2,1,0:T(8,128)S(1)}, f32[4,16,128]{2,1,0:T(8,128)S(1)}, u32[]{:S(2)}, u32[]{:S(2)}) collective-permute-start(f32[4,16,128]{2,1,0:T(8,128)S(1)} %get-tuple-element.25.v.image), channel_id=1, source_target_pairs={{0,1},{1,0},{2,3},{3,2},{4,5},{5,4},{6,7},{7,6},{8,9},{9,8},{10,11... | collective-permute-start | bytes 98312 | tf_op jit(solution)/shard_map/ppermute | solution.py:499
  23.9 0.7 collective-permute-start.5
  24.6 8.8 %collective-permute-start.6 = (f32[8,16,128]{2,1,0:T(8,128)S(1)}, f32[8,16,128]{2,1,0:T(8,128)S(1)}, u32[]{:S(2)}, u32[]{:S(2)}) collective-permute-start(f32[8,16,128]{2,1,0:T(8,128)S(1)} %collective-permute-done.5.p1), channel_id=1, source_target_pairs={{0,1},{1,0},{2,3},{3,2},{4,5},{5,4},{6,7},{7,6},{8,9},{9,8},{10,11... | collective-permute-start | bytes 196616 | tf_op jit(solution)/shard_map/ppermute | solution.py:499
  32.5 0.7 collective-permute-start.7
  37.0 6.2 %collective-permute-start.8 = (f32[12,16,128]{2,1,0:T(8,128)S(1)}, f32[12,16,128]{2,1,0:T(8,128)S(1)}, u32[]{:S(2)}, u32[]{:S(2)}) collective-permute-start(f32[12,16,128]{2,1,0:T(8,128)S(1)} %get-tuple-element.29.v.smooth), channel_id=1, source_target_pairs={{0,1},{1,0},{2,3},{3,2},{4,5},{5,4},{6,7},{7,6},{8,9},{9,8},{10,11... | collective-permute-start | bytes 294920 | tf_op jit(solution)/shard_map/ppermute | solution.py:499
  43.2 11.1 %collective-permute-start.9 = (f32[24,16,128]{2,1,0:T(8,128)S(1)}, f32[24,16,128]{2,1,0:T(8,128)S(1)}, u32[]{:S(2)}, u32[]{:S(2)}) collective-permute-start(f32[24,16,128]{2,1,0:T(8,128)S(1)} %pad_maximum_fusion), channel_id=1, source_target_pairs={{1,2},{2,1},{3,4},{4,3},{5,6},{6,5},{9,10},{10,9},{11,12},{12,11},... | collective-permute-start | bytes 589832 | tf_op jit(solution)/shard_map/ppermute | solution.py:499
  43.8 18.6 %all-to-all-start = ((f32[32,8,128]{2,1,0:T(8,128)}), f32[32,8,128]{2,1,0:T(8,128)S(1)}, u32[]{:S(2)}, u32[]{:S(2)}) async-start(f32[32,8,128]{2,1,0:T(8,128)} %get-tuple-element.26), calls=%async_computation | async-start | bytes 262144 | tf_op jit(solution)/shard_map/all_to_all | solution.py:512
  54.3 1.5 %collective-permute-start.10 = (f32[24,16,128]{2,1,0:T(8,128)S(1)}, f32[24,16,128]{2,1,0:T(8,128)S(1)}, u32[]{:S(2)}, u32[]{:S(2)}) collective-permute-start(f32[24,16,128]{2,1,0:T(8,128)S(1)} %collective-permute-done.9.p1), channel_id=1, source_target_pairs={{0,1},{1,0},{2,3},{3,2},{4,5},{5,4},{6,7},{7,6},{8,9},{9,8},{10,11... | collective-permute-start | bytes 589832 | tf_op jit(solution)/shard_map/ppermute | solution.py:499
  54.6 0.7 collective-permute-start.11
  64.8 5.9 %collective-permute-start.12 = (f32[8,16,128]{2,1,0:T(8,128)S(1)}, f32[8,16,128]{2,1,0:T(8,128)S(1)}, u32[]{:S(2)}, u32[]{:S(2)}) collective-permute-start(f32[8,16,128]{2,1,0:T(8,128)S(1)} %get-tuple-element.32.v.pair), channel_id=1, source_target_pairs={{0,1},{1,0},{2,3},{3,2},{4,5},{5,4},{6,7},{7,6},{8,9},{9,8},{10,11... | collective-permute-start | bytes 196616 | tf_op jit(solution)/shard_map/ppermute | solution.py:499
  70.7 0.7 collective-permute-start.13
  71.4 9.7 %collective-permute-start.14 = (f32[16,16,128]{2,1,0:T(8,128)S(1)}, f32[16,16,128]{2,1,0:T(8,128)S(1)}, u32[]{:S(2)}, u32[]{:S(2)}) collective-permute-start(f32[16,16,128]{2,1,0:T(8,128)S(1)} %collective-permute-done.13.p1), channel_id=1, source_target_pairs={{0,1},{1,0},{2,3},{3,2},{4,5},{5,4},{6,7},{7,6},{8,9},{9,8},{10,11... | collective-permute-start | bytes 393224 | tf_op jit(solution)/shard_map/ppermute | solution.py:499
  77.4 3.7 %collective-permute-start.15 = (f32[8,16,128]{2,1,0:T(8,128)S(1)}, f32[8,16,128]{2,1,0:T(8,128)S(1)}, u32[]{:S(2)}, u32[]{:S(2)}) collective-permute-start(f32[8,16,128]{2,1,0:T(8,128)S(1)} %get-tuple-element.32.v.pair), channel_id=1, source_target_pairs={{1,4},{3,6},{4,1},{5,8},{6,3},{7,10},{8,5},{9,12},{10,7},{11,14},{... | collective-permute-start | bytes 196616 | tf_op jit(solution)/shard_map/ppermute | solution.py:499

commit v6 on v5

--- a/solution.py
+++ b/solution.py
@@ -11,6 +11,7 @@
 REACH = 3
 OWN, LOST, ELSE = range(3)
 SLOTS = len(OFFSETS)
+TERMS = 2
 STAY = 1
 HIGHEST = lax.Precision.HIGHEST
 AXES = ("grp", "row")
@@ -44,12 +45,9 @@
     return jnp.dot(former, latter, precision=HIGHEST, preferred_element_type=jnp.float32)
 
 
-def split3(value):
+def terms_of(value):
     high = value.astype(jnp.bfloat16)
-    rest = value - high.astype(jnp.float32)
-    middle = rest.astype(jnp.bfloat16)
-    low = (rest - middle.astype(jnp.float32)).astype(jnp.bfloat16)
-    return high, middle, low
+    return high, (value - high.astype(jnp.float32)).astype(jnp.bfloat16)
 
 
 def build_table(pieces, vector, place, table_ref, classes, blocks, cols, start=0):
@@ -62,8 +60,8 @@
         for block in range(blocks):
             value = piece[base + block]
             for k, name in enumerate(classes):
-                for s, term in enumerate(split3(value * flags[name])):
-                    rows = pl.ds((3 * (start + k) + s) * cols, cols)
+                for s, term in enumerate(terms_of(value * flags[name])):
+                    rows = pl.ds((TERMS * (start + k) + s) * cols, cols)
                     table_ref[position * blocks + block, rows, :] = term
 
 
@@ -114,12 +112,8 @@
     total = total[:, :tb] + total[:, tb:]
     out = []
     for k in range(classes):
-        base = 3 * k * cols
-        out.append(
-            total[base : base + cols]
-            + total[base + cols : base + 2 * cols]
-            + total[base + 2 * cols : base + 3 * cols]
-        )
+        base = TERMS * k * cols
+        out.append(total[base : base + cols] + total[base + cols : base + 2 * cols])
     return out
 
 
@@ -144,6 +138,16 @@
     for row in range(blocks):
         copies[row].wait()
         for pair in range(count // 2):
+            place = Joined(split_a, split_b).at(row)
+            if pair % 2 == 1:
+                for k in (0, 1):
+                    tile = tiles[row, 2 * pair + k].T
+                    high = tile.astype(jnp.bfloat16)
+                    place[pair, k * tb : (k + 1) * tb, 0:tb] = high
+                    place[pair, k * tb : (k + 1) * tb, tb : 2 * tb] = (
+                        tile - high.astype(jnp.float32)
+                    ).astype(jnp.bfloat16)
+                continue
             highs, rests = [], []
             for k in (2 * pair, 2 * pair + 1):
                 tile = tiles[row, k]
@@ -156,7 +160,7 @@
             turned = lax.dot_general(
                 unit, both, (((1,), (1,)), ((), ())), preferred_element_type=jnp.float32
             )
-            Joined(split_a, split_b).at(row)[pair] = turned.astype(jnp.bfloat16)
+            place[pair] = turned.astype(jnp.bfloat16)
     for copy in late:
         copy.wait()
     for row in range(blocks):
@@ -194,12 +198,12 @@
 
 
 def smoothed(value, halves, cols, tb):
-    left = jnp.concatenate(split3(value), axis=0)
+    left = jnp.concatenate(terms_of(value), axis=0)
     both = lax.dot_general(
         left, halves, (((1,), (1,)), ((), ())), preferred_element_type=jnp.float32
     )
     both = both[:, :tb] + both[:, tb:]
-    return both[:cols] + both[cols : 2 * cols] + both[2 * cols :]
+    return both[:cols] + both[cols:]
 
 
 def lanes(ref):
@@ -212,19 +216,18 @@
     return rows, columns
 
 
-def pack_gram(gram_ref, former, latter, scale, cols):
-    gram = dot_nt(former, latter)
+def pack_gram(gram_ref, early, late, turned, scale, cols):
     if scale is not None:
-        gram = gram * scale
-    g00, g01, g02 = (gram[:cols, k * cols : (k + 1) * cols] for k in range(3))
-    g11, g12 = (gram[cols:, k * cols : (k + 1) * cols] for k in (1, 2))
+        early, late, turned = early * scale, late * scale, turned * scale
+    g00, g01, g11 = early[:cols, :cols], early[:cols, cols:], early[cols:, cols:]
+    g02, g12 = late[:cols], late[cols:]
     rows, columns = grid16(cols)
     upper = rows <= columns
     first = jnp.where(upper, g00, g11)
     middle = jnp.sum(jnp.where(rows == columns, g11, 0.0), axis=1, keepdims=True)
     last = jnp.where(rows == columns + 1, middle, 0.0)
     last = jnp.where((rows == cols - 1) & (columns == 0), g11[0:1, 0:1], last)
-    last = jnp.where(upper, 0.5 * (g12 + g12.T), last)
+    last = jnp.where(upper, 0.5 * (g12 + turned), last)
     flat = jnp.concatenate([first, g01, g02, last], axis=1)
     half = cols // 2
     packed = jnp.concatenate([flat[:half], flat[half:]], axis=1)
@@ -271,6 +274,8 @@
     place = Place(lost_ref)
     base = place.base(blocks)
     build_table((v, sw, p1, p2, p3), 0, place, table, (OWN, LOST, ELSE), blocks, cols)
+    former = jnp.concatenate([lanes(right), lanes(v)], axis=0)
+    early = dot_nt(former, former)
     for row in range(blocks):
         out = row_product(columns_ref, base, table, Joined(split_a, split_b), row, 3, cols)
         for k in range(3):
@@ -282,9 +287,9 @@
         smooth[2 * blocks + row] = smoothed(
             parts[1, row] + parts[2, row], halves[row], cols, v.shape[2]
         )
-    former = jnp.concatenate([lanes(right), lanes(v)], axis=0)
-    latter = jnp.concatenate([former, lanes(image)], axis=0)
-    pack_gram(gram, former, latter, None, cols)
+    late = dot_nt(former, lanes(image))
+    turned = dot_nt(lanes(image), lanes(v))
+    pack_gram(gram, early, late, turned, None, cols)
 
 
 def third_kernel(
@@ -319,21 +324,23 @@
     mine = place.mine
     build_table((v, sw, p1, p2, p3), 0, place, table, (OWN, LOST), blocks, cols)
     build_table((v, sw, p1, p2, p3), 1, place, table, (LOST,), blocks, cols, 2)
+    smooth, head = v.at[0:blocks], v.at[blocks : 2 * blocks]
+    former = jnp.concatenate([lanes(head), lanes(smooth)], axis=0)
+    early = dot_nt(former, jnp.concatenate([lanes(target), lanes(applied)], axis=0))
     for row in range(blocks):
         out = row_product(columns_ref, base, table, Joined(split_a, split_b), row, 3, cols)
         second[row] = out[0]
         lost1[row] = out[0] * mine + out[1]
         lost0[row] = applied[row] * mine + out[2]
-    smooth, head = v.at[0:blocks], v.at[blocks : 2 * blocks]
-    former = jnp.concatenate([lanes(head), lanes(smooth)], axis=0)
-    latter = jnp.concatenate([lanes(target), lanes(applied), lanes(second)], axis=0)
-    pack_gram(gram, former, latter, mine, cols)
+    late = dot_nt(former, lanes(second))
+    turned = dot_nt(lanes(second), lanes(smooth))
+    pack_gram(gram, early, late, turned, mine, cols)
 
 
 def tile_call(kernel, classes, outs, extra, split, operands_vmem, columns, lost, place=VMEM):
     blocks = split[0].shape[0] + split[1].shape[0]
     _, cols, tb = operands_vmem[-1].shape
-    scratch = [VMEM((SLOTS * blocks, 3 * classes * cols, tb), jnp.bfloat16)] + extra
+    scratch = [VMEM((SLOTS * blocks, TERMS * classes * cols, tb), jnp.bfloat16)] + extra
     return pl.pallas_call(
         kernel,
         out_shape=outs,
@@ -375,9 +382,11 @@
     inverse = eliminate(g00, unit)
     moved = dot_nn(jnp.concatenate([g01, g11], axis=0), advance)
     squares = g00 - moved[:cols] - dot_tn(advance, g01_t - moved[cols:])
+    start = jnp.concatenate([unit, -advance], axis=0)
     mixing = dot_nn(inverse, squares)
     heading = jnp.concatenate([unit + mixing, -advance], axis=0)
-    curvature = dot_tn(heading, dot_nn(big, heading))
+    turned = dot_nn(big, start) + dot_nn(dot_nn(big[:, :cols], inverse), squares)
+    curvature = dot_tn(heading, turned)
     second = eliminate(curvature, squares)
     combo = dot_nn(heading, second)
     return jnp.concatenate([combo[:cols] + advance, combo[cols:]], axis=0)

time: 108 us -> 107 us (level)
  Pallas kernels: 26.8 us -> 25.1 us
    all_to_all x1, starting transfers between devices: 10.4 us -> 11.6 us  [exchange(): return lax.all_to_all(gram, AXES, 0, 0)]
    ppermute x16, starting transfers between devices: 41.1 us -> 39.9 us  [move(): return lax.ppermute(value, AXES, pairs)]
  transfers between devices with their start and end apart: 17 -> 17, of which waited for: 7 -> 7; matrix products, arithmetic and copies ran while one was open for 0% -> 0% of each run, Pallas kernels for 12% -> 11%
where the time goes in v6:
time: 107 us; the launch traced here: 106 us
  starting transfers between devices  51.6 us (48%)
  Pallas kernels  25.1 us (23%)
  blocking collectives  21 us (20%)
  waiting for transfers between devices  6.38 us (6%)
  between operations  1.52 us (1%)
    ppermute x16, starting transfers between devices, move(): return lax.ppermute(value, AXES, pairs)  39.9 us
    all_to_all x1, blocking collectives, exchange(): return lax.all_to_all(gram, AXES, 0, 0)  21 us
    pallas_call x4, Pallas kernels, tile_call(): pl.pallas_call(kernel, out_shape=outs, in_specs=[spec(SMEM), spec(SMEM),...  12.8 us
    all_to_all x1, starting transfers between devices, exchange(): return lax.all_to_all(gram, AXES, 0, 0)  11.6 us
    pallas_call x2, Pallas kernels, small_call(): pl.pallas_call(kernel, out_shape=outs, in_specs=[spec(SMEM)] + [spec(VMEM...  5.02 us
    ppermute x16, waiting for transfers between devices, move(): return lax.ppermute(value, AXES, pairs)  4.55 us
    pallas_call x1, Pallas kernels, split_call(): pl.pallas_call(split_kernel, out_shape=[jax.ShapeDtypeStruct((rows, count...  4.31 us
    pallas_call x1, Pallas kernels, reload_call(): pl.pallas_call(reload_kernel, out_shape=jax.ShapeDtypeStruct(split.shape,...  2.88 us
  transfers between devices with their start and end apart: 17, of which 7 were waited for; matrix products, arithmetic and copies ran while one was open for 0% of the time, Pallas kernels for 11%

profile of v6, /device:TPU:0, one launch (start us, length us, event | category | flops | bytes accessed | tf_op | source)
XLA Modules:
  0.0 106.3 jit_solution(12079677233990190873)
XLA Ops:
  0.6 0.0 copy-start.1
  0.6 0.0 copy-start.2
  0.7 0.6 collective-permute-start
  1.2 1.1 %collective-permute-done.sw = f32[4,16,128]{2,1,0:T(8,128)S(1)} collective-permute-done((f32[4,16,128]{2,1,0:T(8,128)}, f32[4,16,128]{2,1,0:T(8,128)S(1)}, u32[]{:S(2)}, u32[]{:S(2)}) %collective-permute-start) | collective-permute-done | bytes 32800 | tf_op jit(solution)/shard_map/ppermute | solution.py:508
  2.3 0.8 pad_maximum_fusion.2
  3.0 0.7 collective-permute-start.1
  3.7 0.0 collective-permute-done.1.p1
  3.7 6.2 %collective-permute-start.2 = (f32[8,16,128]{2,1,0:T(8,128)S(1)}, f32[8,16,128]{2,1,0:T(8,128)S(1)}, u32[]{:S(2)}, u32[]{:S(2)}) collective-permute-start(f32[8,16,128]{2,1,0:T(8,128)S(1)} %collective-permute-done.1.p1), channel_id=1, source_target_pairs={{0,1},{1,0},{2,3},{3,2},{4,5},{5,4},{6,7},{7,6},{8,9},{9,8},{10,11... | collective-permute-start | bytes 196616 | tf_op jit(solution)/shard_map/ppermute | solution.py:508
  9.9 0.7 collective-permute-start.3
  11.2 4.3 %shard_map.68 = (bf16[1,16,256,256]{3,2,1,0:T(8,128)(2,1)S(1)}, bf16[3,16,256,256]{3,2,1,0:T(8,128)(2,1)S(1)}, bf16[4,256,128]{2,1,0:T(8,128)(2,1)S(1)}, f32[4,16,128]{2,1,0:T(8,128)S(1)}) custom-call(f32[4,32,128,128]{3,2,1,0:T(8,128)} %tiles_hbm.1, f32[4,128,128]{2,1,0:T(8,128)} %precond_hbm.1, f32[4,16,128]{2,1,0:T(8,128)} %right.5), custom_call_target="tpu_custom_call" | custom-call | bytes 12582912 | tf_op jit(solution)/shard_map/pallas_call | solution.py:176
  15.5 0.0 copy-start
  15.5 0.0 collective-permute-done.3.p3
  15.5 0.0 collective-permute-done.2.p2
  15.6 0.0 copy-done.1
  15.6 0.0 copy-done.2
  15.6 2.3 %shard_map.70 = (f32[3,4,16,128]{3,2,1,0:T(8,128)S(1)}, f32[4,16,128]{2,1,0:T(8,128)S(1)}, f32[4,16,128]{2,1,0:T(8,128)S(1)}) custom-call(s32[4,32]{1,0:T(4,128)S(1)} %copy-done.2, s32[1]{0:T(128)S(6)} %copy.7.lost_ref, bf16[1,16,256,256]{3,2,1,0:T(8,128)(2,1)S(1)} %get-tuple-element.20.split_a, ...), custom_call_target="tpu_custom_call" | custom-call | tf_op jit(solution)/shard_map/pallas_call | solution.py:344
  17.9 4.5 %collective-permute-start.4 = (f32[4,16,128]{2,1,0:T(8,128)S(1)}, f32[4,16,128]{2,1,0:T(8,128)S(1)}, u32[]{:S(2)}, u32[]{:S(2)}) collective-permute-start(f32[4,16,128]{2,1,0:T(8,128)S(1)} %get-tuple-element.25.v.image), channel_id=1, source_target_pairs={{0,1},{1,0},{2,3},{3,2},{4,5},{5,4},{6,7},{7,6},{8,9},{9,8},{10,11... | collective-permute-start | bytes 98312 | tf_op jit(solution)/shard_map/ppermute | solution.py:508
  22.4 0.9 collective-permute-done.4.sw
  23.3 0.7 collective-permute-start.5
  23.9 0.0 collective-permute-done.5.p1
  23.9 7.2 %collective-permute-start.6 = (f32[8,16,128]{2,1,0:T(8,128)S(1)}, f32[8,16,128]{2,1,0:T(8,128)S(1)}, u32[]{:S(2)}, u32[]{:S(2)}) collective-permute-start(f32[8,16,128]{2,1,0:T(8,128)S(1)} %collective-permute-done.5.p1), channel_id=1, source_target_pairs={{0,1},{1,0},{2,3},{3,2},{4,5},{5,4},{6,7},{7,6},{8,9},{9,8},{10,11... | collective-permute-start | bytes 196616 | tf_op jit(solution)/shard_map/ppermute | solution.py:508
  31.2 0.7 collective-permute-start.7
  31.8 0.0 collective-permute-done.7.p3
  31.8 0.2 collective-permute-done.6.p2
  32.1 3.3 %shard_map.71 = (f32[3,4,16,128]{3,2,1,0:T(8,128)S(1)}, f32[32,8,128]{2,1,0:T(8,128)}, f32[12,16,128]{2,1,0:T(8,128)S(1)}) custom-call(s32[4,32]{1,0:T(4,128)S(1)} %copy-done.2, s32[1]{0:T(128)S(6)} %copy.7.lost_ref, bf16[1,16,256,256]{3,2,1,0:T(8,128)(2,1)S(1)} %get-tuple-element.20.split_a, ...), custom_call_target="tpu_custom_call" | custom-call | tf_op jit(solution)/shard_map/pallas_call | solution.py:344
  35.4 0.0 copy-done
  35.4 5.2 %collective-permute-start.8 = (f32[12,16,128]{2,1,0:T(8,128)S(1)}, f32[12,16,128]{2,1,0:T(8,128)S(1)}, u32[]{:S(2)}, u32[]{:S(2)}) collective-permute-start(f32[12,16,128]{2,1,0:T(8,128)S(1)} %get-tuple-element.29.v.smooth), channel_id=1, source_target_pairs={{0,1},{1,0},{2,3},{3,2},{4,5},{5,4},{6,7},{7,6},{8,9},{9,8},{10,11... | collective-permute-start | bytes 294920 | tf_op jit(solution)/shard_map/ppermute | solution.py:508
  40.6 0.9 collective-permute-done.8.sw
  41.5 0.7 collective-permute-start.9
  42.2 11.6 %all-to-all-start = ((f32[32,8,128]{2,1,0:T(8,128)}), f32[32,8,128]{2,1,0:T(8,128)S(1)}, u32[]{:S(2)}, u32[]{:S(2)}) async-start(f32[32,8,128]{2,1,0:T(8,128)} %get-tuple-element.26), calls=%async_computation | async-start | bytes 262144 | tf_op jit(solution)/shard_map/all_to_all | solution.py:521
  53.9 0.0 collective-permute-done.9.p1
  53.9 0.3 collective-permute-start.10
  54.2 0.7 collective-permute-start.11
  54.8 0.0 collective-permute-done.11.p3
  54.9 0.5 collective-permute-done.10.p2
  55.4 4.8 %shard_map.72.moved = f32[3,4,16,128]{3,2,1,0:T(8,128)S(1)} custom-call(s32[4,32]{1,0:T(4,128)S(1)} %copy-done.2, s32[1]{0:T(128)S(6)} %copy.7.lost_ref, bf16[1,16,256,256]{3,2,1,0:T(8,128)(2,1)S(1)} %get-tuple-element.20.split_a, bf16[3,16,256,256]{3,2,1,0:T(8,128)(2,1)} %copy-done, f32[12,16,128]{2,1,0:T(8,128)S(1)} %get-tuple-element.29.v.smooth, ...), custom_call_target="tpu_custom_call" | custom-call | tf_op jit(solution)/shard_map/pallas_call | solution.py:344
  60.2 1.8 %all-to-all-done.gathered = f32[32,8,128]{2,1,0:T(8,128)S(1)} async-done(((f32[32,8,128]{2,1,0:T(8,128)}), f32[32,8,128]{2,1,0:T(8,128)S(1)}, u32[]{:S(2)}, u32[]{:S(2)}) %all-to-all-start) | async-done | bytes 131104 | tf_op jit(solution)/shard_map/all_to_all | solution.py:521
  62.0 2.3 %shard_map.73 = (f32[4,16,128]{2,1,0:T(8,128)S(1)}, f32[4,16,128]{2,1,0:T(8,128)S(1)}, f32[4,16,128]{2,1,0:T(8,128)S(1)}, f32[4,16,128]{2,1,0:T(8,128)S(1)}, f32[8,16,128]{2,1,0:T(8,128)S(1)}) custom-call(s32[1]{0:T(128)S(6)} %copy.7.lost_ref, f32[32,8,128]{2,1,0:T(8,128)S(1)} %all-to-all-done.gathered, f32[4,16,128]{2,1,0:T(8,128)S(1)} %copy-done.1, ...), custom_call_target="tpu_custom_call" | custom-call | tf_op jit(solution)/shard_map/pallas_call | solution.py:493
  64.3 4.7 %collective-permute-start.12 = (f32[8,16,128]{2,1,0:T(8,128)S(1)}, f32[8,16,128]{2,1,0:T(8,128)S(1)}, u32[]{:S(2)}, u32[]{:S(2)}) collective-permute-start(f32[8,16,128]{2,1,0:T(8,128)S(1)} %get-tuple-element.32.v.pair), channel_id=1, source_target_pairs={{0,1},{1,0},{2,3},{3,2},{4,5},{5,4},{6,7},{7,6},{8,9},{9,8},{10,11... | collective-permute-start | bytes 196616 | tf_op jit(solution)/shard_map/ppermute | solution.py:508
  69.0 0.9 collective-permute-done.12.sw
  69.9 0.7 collective-permute-start.13
  70.6 0.0 collective-permute-done.13.p1
  70.6 6.0 %collective-permute-start.14 = (f32[16,16,128]{2,1,0:T(8,128)S(1)}, f32[16,16,128]{2,1,0:T(8,128)S(1)}, u32[]{:S(2)}, u32[]{:S(2)}) collective-permute-start(f32[16,16,128]{2,1,0:T(8,128)S(1)} %collective-permute-done.13.p1), channel_id=1, source_target_pairs={{0,1},{1,0},{2,3},{3,2},{4,5},{5,4},{6,7},{7,6},{8,9},{9,8},{10,11... | collective-permute-start | bytes 393224 | tf_op jit(solution)/shard_map/ppermute | solution.py:508
  76.6 0.7 collective-permute-start.15
  77.2 2.9 %shard_map.69.split_b = bf16[3,16,256,256]{3,2,1,0:T(8,128)(2,1)S(1)} custom-call(bf16[3,16,256,256]{3,2,1,0:T(8,128)(2,1)} %copy-done), custom_call_target="tpu_custom_call" | custom-call | bytes 12582912 | tf_op jit(solution)/shard_map/pallas_call | solution.py:481
  80.1 0.0 collective-permute-done.15.p3
  80.1 0.0 collective-permute-done.14.p2
  80.1 2.5 %shard_map.74 = (f32[4,16,128]{2,1,0:T(8,128)S(1)}, f32[4,16,128]{2,1,0:T(8,128)S(1)}, f32[32,8,128]{2,1,0:T(8,128)S(1)}) custom-call(s32[4,32]{1,0:T(4,128)S(1)} %copy-done.2, s32[1]{0:T(128)S(6)} %copy.7.lost_ref, bf16[1,16,256,256]{3,2,1,0:T(8,128)(2,1)S(1)} %get-tuple-element.20.split_a, bf16[3,16,256,256]{3,2,1,0:T(8,128)(2,1)S(1)} %shard_map.69.split_b, ...), custom_call_target="tpu_custom_call" | custom-call | tf_op jit(solution)/shard_map/pallas_call | solution.py:344
  82.6 21.0 %all_to_all.10.gathered = f32[32,8,128]{2,1,0:T(8,128)S(1)} all-to-all(f32[32,8,128]{2,1,0:T(8,128)S(1)} %get-tuple-element.33), channel_id=1, replica_groups=mesh['grp'=4,'row'=8] {'grp','row'}, dimensions={0} | all-to-all | bytes 262144 | tf_op jit(solution)/shard_map/all_to_all | solution.py:521
  103.6 2.7 %shard_map.75 = (f32[4,16,128]{2,1,0:T(8,128)}, f32[4,16,128]{2,1,0:T(8,128)}) custom-call(s32[1]{0:T(128)S(6)} %copy.7.lost_ref, f32[32,8,128]{2,1,0:T(8,128)S(1)} %all_to_all.10.gathered, f32[4,16,128]{2,1,0:T(8,128)S(1)} %copy-done.1, f32[4,16,128]{2,1,0:T(8,128)S(1)} %get-tuple-element.34.solution, f32[4,16,128]{2,1,0:T(8,128)S(1)} %get-tuple-element.35.kept, ...), custom_call_target="tpu_custom_call" | custom-call | tf_op jit(solution)/shard_map/pallas_call | solution.py:493
  (3 shorter events, 0.0 us)
Async XLA Ops:
  0.6 14.9 %copy-start.1 = (f32[4,16,128]{2,1,0:T(8,128)S(1)}, f32[4,16,128]{2,1,0:T(8,128)}, u32[]{:S(2)}) copy-start(f32[4,16,128]{2,1,0:T(8,128)} %right.5) | copy-start | bytes 98308
  0.6 14.9 %copy-start.2 = (s32[4,32]{1,0:T(4,128)S(1)}, s32[4,32]{1,0:T(4,128)}, u32[]{:S(2)}) copy-start(s32[4,32]{1,0:T(4,128)} %columns_ref.7) | copy-start | bytes 1540
  0.7 1.6 %collective-permute-start = (f32[4,16,128]{2,1,0:T(8,128)}, f32[4,16,128]{2,1,0:T(8,128)S(1)}, u32[]{:S(2)}, u32[]{:S(2)}) collective-permute-start(f32[4,16,128]{2,1,0:T(8,128)} %right.5), channel_id=1, source_target_pairs={{0,1},{1,0},{2,3},{3,2},{4,5},{5,4},{6,7},{7,6},{8,9},{9,8},{10,11... | collective-permute-start | bytes 98312 | tf_op jit(solution)/shard_map/ppermute | solution.py:508
  3.0 0.7 collective-permute-start.1
  3.7 11.8 %collective-permute-start.2 = (f32[8,16,128]{2,1,0:T(8,128)S(1)}, f32[8,16,128]{2,1,0:T(8,128)S(1)}, u32[]{:S(2)}, u32[]{:S(2)}) collective-permute-start(f32[8,16,128]{2,1,0:T(8,128)S(1)} %collective-permute-done.1.p1), channel_id=1, source_target_pairs={{0,1},{1,0},{2,3},{3,2},{4,5},{5,4},{6,7},{7,6},{8,9},{9,8},{10,11... | collective-permute-start | bytes 196616 | tf_op jit(solution)/shard_map/ppermute | solution.py:508
  9.9 5.6 %collective-permute-start.3 = (f32[4,16,128]{2,1,0:T(8,128)}, f32[4,16,128]{2,1,0:T(8,128)S(1)}, u32[]{:S(2)}, u32[]{:S(2)}) collective-permute-start(f32[4,16,128]{2,1,0:T(8,128)} %right.5), channel_id=1, source_target_pairs={{1,4},{3,6},{4,1},{5,8},{6,3},{7,10},{8,5},{9,12},{10,7},{11,14},{... | collective-permute-start | bytes 98312 | tf_op jit(solution)/shard_map/ppermute | solution.py:508
  15.5 19.8 %copy-start = (bf16[3,16,256,256]{3,2,1,0:T(8,128)(2,1)}, bf16[3,16,256,256]{3,2,1,0:T(8,128)(2,1)S(1)}, u32[]{:S(2)}) copy-start(bf16[3,16,256,256]{3,2,1,0:T(8,128)(2,1)S(1)} %get-tuple-element.21.split_hbm.split_b) | copy-start | bytes 18874372
  17.9 5.4 %collective-permute-start.4 = (f32[4,16,128]{2,1,0:T(8,128)S(1)}, f32[4,16,128]{2,1,0:T(8,128)S(1)}, u32[]{:S(2)}, u32[]{:S(2)}) collective-permute-start(f32[4,16,128]{2,1,0:T(8,128)S(1)} %get-tuple-element.25.v.image), channel_id=1, source_target_pairs={{0,1},{1,0},{2,3},{3,2},{4,5},{5,4},{6,7},{7,6},{8,9},{9,8},{10,11... | collective-permute-start | bytes 98312 | tf_op jit(solution)/shard_map/ppermute | solution.py:508
  23.3 0.7 collective-permute-start.5
  23.9 8.1 %collective-permute-start.6 = (f32[8,16,128]{2,1,0:T(8,128)S(1)}, f32[8,16,128]{2,1,0:T(8,128)S(1)}, u32[]{:S(2)}, u32[]{:S(2)}) collective-permute-start(f32[8,16,128]{2,1,0:T(8,128)S(1)} %collective-permute-done.5.p1), channel_id=1, source_target_pairs={{0,1},{1,0},{2,3},{3,2},{4,5},{5,4},{6,7},{7,6},{8,9},{9,8},{10,11... | collective-permute-start | bytes 196616 | tf_op jit(solution)/shard_map/ppermute | solution.py:508
  31.2 0.7 collective-permute-start.7
  35.4 6.2 %collective-permute-start.8 = (f32[12,16,128]{2,1,0:T(8,128)S(1)}, f32[12,16,128]{2,1,0:T(8,128)S(1)}, u32[]{:S(2)}, u32[]{:S(2)}) collective-permute-start(f32[12,16,128]{2,1,0:T(8,128)S(1)} %get-tuple-element.29.v.smooth), channel_id=1, source_target_pairs={{0,1},{1,0},{2,3},{3,2},{4,5},{5,4},{6,7},{7,6},{8,9},{9,8},{10,11... | collective-permute-start | bytes 294920 | tf_op jit(solution)/shard_map/ppermute | solution.py:508
  41.5 12.3 %collective-permute-start.9 = (f32[24,16,128]{2,1,0:T(8,128)S(1)}, f32[24,16,128]{2,1,0:T(8,128)S(1)}, u32[]{:S(2)}, u32[]{:S(2)}) collective-permute-start(f32[24,16,128]{2,1,0:T(8,128)S(1)} %pad_maximum_fusion), channel_id=1, source_target_pairs={{1,2},{2,1},{3,4},{4,3},{5,6},{6,5},{9,10},{10,9},{11,12},{12,11},... | collective-permute-start | bytes 589832 | tf_op jit(solution)/shard_map/ppermute | solution.py:508
  42.2 19.8 %all-to-all-start = ((f32[32,8,128]{2,1,0:T(8,128)}), f32[32,8,128]{2,1,0:T(8,128)S(1)}, u32[]{:S(2)}, u32[]{:S(2)}) async-start(f32[32,8,128]{2,1,0:T(8,128)} %get-tuple-element.26), calls=%async_computation | async-start | bytes 262144 | tf_op jit(solution)/shard_map/all_to_all | solution.py:521
  53.9 1.5 %collective-permute-start.10 = (f32[24,16,128]{2,1,0:T(8,128)S(1)}, f32[24,16,128]{2,1,0:T(8,128)S(1)}, u32[]{:S(2)}, u32[]{:S(2)}) collective-permute-start(f32[24,16,128]{2,1,0:T(8,128)S(1)} %collective-permute-done.9.p1), channel_id=1, source_target_pairs={{0,1},{1,0},{2,3},{3,2},{4,5},{5,4},{6,7},{7,6},{8,9},{9,8},{10,11... | collective-permute-start | bytes 589832 | tf_op jit(solution)/shard_map/ppermute | solution.py:508
  54.2 0.7 collective-permute-start.11
  64.3 5.6 %collective-permute-start.12 = (f32[8,16,128]{2,1,0:T(8,128)S(1)}, f32[8,16,128]{2,1,0:T(8,128)S(1)}, u32[]{:S(2)}, u32[]{:S(2)}) collective-permute-start(f32[8,16,128]{2,1,0:T(8,128)S(1)} %get-tuple-element.32.v.pair), channel_id=1, source_target_pairs={{0,1},{1,0},{2,3},{3,2},{4,5},{5,4},{6,7},{7,6},{8,9},{9,8},{10,11... | collective-permute-start | bytes 196616 | tf_op jit(solution)/shard_map/ppermute | solution.py:508
  69.9 0.7 collective-permute-start.13
  70.6 9.5 %collective-permute-start.14 = (f32[16,16,128]{2,1,0:T(8,128)S(1)}, f32[16,16,128]{2,1,0:T(8,128)S(1)}, u32[]{:S(2)}, u32[]{:S(2)}) collective-permute-start(f32[16,16,128]{2,1,0:T(8,128)S(1)} %collective-permute-done.13.p1), channel_id=1, source_target_pairs={{0,1},{1,0},{2,3},{3,2},{4,5},{5,4},{6,7},{7,6},{8,9},{9,8},{10,11... | collective-permute-start | bytes 393224 | tf_op jit(solution)/shard_map/ppermute | solution.py:508
  76.6 3.6 %collective-permute-start.15 = (f32[8,16,128]{2,1,0:T(8,128)S(1)}, f32[8,16,128]{2,1,0:T(8,128)S(1)}, u32[]{:S(2)}, u32[]{:S(2)}) collective-permute-start(f32[8,16,128]{2,1,0:T(8,128)S(1)} %get-tuple-element.32.v.pair), channel_id=1, source_target_pairs={{1,4},{3,6},{4,1},{5,8},{6,3},{7,10},{8,5},{9,12},{10,7},{11,14},{... | collective-permute-start | bytes 196616 | tf_op jit(solution)/shard_map/ppermute | solution.py:508
